TPU v7x, 32 devices: a whole 2x2x4 slice. The times are simulated.
32 devices in a mesh: rep: 4 (over y, x), shard: 8 (over z, core).
Axes of the slice: x: 2, y: 2, z: 4, core: 2. Of those that a mesh axis runs over, the one named last changes fastest.
Arguments:
- tokens: bfloat16 [8192, 2048], P(('rep', 'shard')), may hold values from -6 to 6
- lengths: int32 [32], P(('rep', 'shard')), may hold values from 128 to 256, as said below
- routes: int32 [8192, 8], P(('rep', 'shard')), may hold values from 0 to 15, all different within a row; in each aligned block of 256 rows (0 to 255, 256 to 511, ...) at most 144 rows name the same one
- gain_attn: float32 [2048], replicated, may hold values from 0.1 to 1.9
- gain_query: float32 [128], replicated, may hold values from 0.1 to 1.9
- gain_key: float32 [128], replicated, may hold values from 0.1 to 1.9
- w_query: bfloat16 [2048, 2048], P(None, 'shard'), may hold values from -0.125 to 0.125
- w_key: bfloat16 [2048, 2048], P(None, 'shard'), may hold values from -0.125 to 0.125
- w_value: bfloat16 [2048, 2048], P(None, 'shard'), may hold values from -0.125 to 0.125
- w_out: bfloat16 [2048, 2048], P('shard'), may hold values from -0.75 to 0.75
- gain_moe: float32 [2048], replicated, may hold values from 0.1 to 1.9
- w_router: bfloat16 [2048, 16], replicated, may hold values from -0.0625 to 0.0625
- w_gate: bfloat16 [16, 2048, 1024], P('shard'), may hold values from -0.125 to 0.125
- w_up: bfloat16 [16, 2048, 1024], P('shard'), may hold values from -0.125 to 0.125
- w_down: bfloat16 [16, 1024, 2048], P('shard'), may hold values from -1.5 to 1.5
- out_grad: bfloat16 [8192, 2048], P(('rep', 'shard')), may hold values from -6 to 6
Outputs:
- output: bfloat16 [8192, 2048], P(('rep', 'shard'))
- input_grad: float32 [8192, 2048], P(('rep', 'shard'))
- grad_gain_attn: float32 [2048], replicated
- grad_gain_query: float32 [128], replicated
- grad_gain_key: float32 [128], replicated
- grad_w_query: float32 [2048, 2048], P(None, 'shard')
- grad_w_key: float32 [2048, 2048], P(None, 'shard')
- grad_w_value: float32 [2048, 2048], P(None, 'shard')
- grad_w_out: float32 [2048, 2048], P('shard')
- grad_gain_moe: float32 [2048], replicated
- grad_w_router: float32 [2048, 16], replicated
- grad_w_gate: float32 [16, 2048, 1024], P('shard')
- grad_w_up: float32 [16, 2048, 1024], P('shard')
- grad_w_down: float32 [16, 1024, 2048], P('shard')
Inputs may be any that keep to these rules, and one draw needn't show every extreme that they name: `lengths`: valid tokens of each sequence; some sequence is full. `routes`: each row names 8 different experts; among the 256 rows of one sequence no expert is named by more than 144 rows, a bound that some block reaches.
All inputs are finite; a program needn't handle non-finite values.
Results may differ from a plain program's by a relative error of at most 0.024.
Values may be sent and summed in bfloat16 or wider, within the bound.
A program may use at most 320 MiB of HBM per device.

v0:
```python
import jax
import jax.numpy as jnp
from jax import lax
from jax.sharding import PartitionSpec as P

CAP = 144


EPS_NORM = 1e-06
ROPE_BASE = 50000.0
MASKED = -1e30


def rms_scale(values, gain_vec):
    return (
        values * lax.rsqrt(jnp.mean(values * values, axis=-1, keepdims=True) + EPS_NORM) * gain_vec
    )


def rope_tables(seq_len, head_dim):
    half_dim = head_dim // 2
    places = jnp.arange(seq_len, dtype=jnp.float32)
    freqs = ROPE_BASE ** (-jnp.arange(half_dim, dtype=jnp.float32) * (2.0 / head_dim))
    angles = places[:, None] * freqs[None, :]
    cos_tab = jnp.concatenate([jnp.cos(angles), jnp.cos(angles)], axis=-1)
    sine_tab = jnp.concatenate([jnp.sin(angles), jnp.sin(angles)], axis=-1)
    return (cos_tab, sine_tab)


def rotate_half(values, cos_tab, sine_tab):
    half_dim = values.shape[-1] // 2
    turned = jnp.concatenate([-values[..., half_dim:], values[..., :half_dim]], axis=-1)
    return values * cos_tab[:, None, :] + turned * sine_tab[:, None, :]


def head_prepare(raw_proj, gain_vec, cos_tab, sine_tab):
    return rotate_half(rms_scale(raw_proj, gain_vec), cos_tab, sine_tab)


def soft_max(logit_vals):
    upper = jnp.max(logit_vals, axis=-1, keepdims=True)
    expo = jnp.exp(logit_vals - upper)
    return expo / jnp.sum(expo, axis=-1, keepdims=True)


def slot_table(route_rows, expert_count):
    flat_ids = route_rows.reshape(-1)
    one_hot = (flat_ids[:, None] == jnp.arange(expert_count, dtype=jnp.int32)[None, :]).astype(
        jnp.int32
    )
    before = jnp.cumsum(one_hot, axis=0) - one_hot
    ranks = jnp.sum(before * one_hot, axis=1)
    return flat_ids * CAP + ranks


def attend(query_rot, key_rot, value_low, key_valid, score_scale):
    scores = (
        jnp.einsum("sqhd,skhd->shqk", query_rot, key_rot, preferred_element_type=jnp.float32)
        * score_scale
    )
    scores = jnp.where(key_valid[:, None, None, :], scores, MASKED)
    upper = jnp.max(scores, axis=-1, keepdims=True)
    expo = jnp.exp(scores - upper)
    total = jnp.sum(expo, axis=-1, keepdims=True)
    weights = (expo / total).astype(jnp.bfloat16)
    result = jnp.einsum("shqk,skhd->sqhd", weights, value_low, preferred_element_type=jnp.float32)
    return (result.astype(jnp.bfloat16), upper + jnp.log(total))


def attend_back(query_rot, key_rot, value_low, key_valid, score_scale, log_total, grad_result):
    scores = (
        jnp.einsum("sqhd,skhd->shqk", query_rot, key_rot, preferred_element_type=jnp.float32)
        * score_scale
    )
    scores = jnp.where(key_valid[:, None, None, :], scores, MASKED)
    probs_full = jnp.exp(scores - log_total)
    weights = probs_full.astype(jnp.bfloat16)
    grad_value = jnp.einsum(
        "shqk,sqhd->skhd", weights, grad_result, preferred_element_type=jnp.float32
    ).astype(jnp.bfloat16)
    grad_prob = jnp.einsum(
        "sqhd,skhd->shqk", grad_result, value_low, preferred_element_type=jnp.float32
    )
    mean_term = jnp.sum(probs_full * grad_prob, axis=-1, keepdims=True)
    grad_score = (probs_full * (grad_prob - mean_term)).astype(jnp.bfloat16)
    grad_query = (
        jnp.einsum("shqk,skhd->sqhd", grad_score, key_rot, preferred_element_type=jnp.float32)
        * score_scale
    )
    grad_key = (
        jnp.einsum("shqk,sqhd->skhd", grad_score, query_rot, preferred_element_type=jnp.float32)
        * score_scale
    )
    return (grad_query, grad_key, grad_value)


def local(
    tokens,
    lengths,
    routes,
    gain_attn,
    gain_query,
    gain_key,
    w_query,
    w_key,
    w_value,
    w_out,
    gain_moe,
    w_router,
    w_gate,
    w_up,
    w_down,
    out_grad,
):
    row_count, model_width = tokens.shape
    head_dim = gain_query.shape[0]
    group_count = lax.axis_size("shard")
    expert_count = w_router.shape[1]
    inputs = tokens.astype(jnp.float32)
    row_valid = jnp.arange(row_count, dtype=jnp.int32) < lengths[0]
    row_mask = row_valid.astype(jnp.float32)
    cos_tab, sine_tab = rope_tables(row_count, head_dim)
    score_scale = head_dim ** (-0.5)
    normed_low = rms_scale(inputs, gain_attn).astype(jnp.bfloat16)
    source, key_marks = (
        lax.all_gather(normed_low, "shard", axis=0, tiled=True),
        lax.all_gather(row_mask.astype(jnp.bfloat16), "shard", axis=0, tiled=True),
    )
    key_valid = key_marks.reshape(group_count, row_count) > 0.5
    proj_query, proj_key, proj_value, proj_out = (w_query, w_key, w_value, w_out)
    head_local = proj_query.shape[1] // head_dim
    four_shape = (group_count, row_count, head_local, head_dim)
    flat_shape = (group_count * row_count, head_local * head_dim)
    query_raw = jnp.dot(source, proj_query, preferred_element_type=jnp.float32).reshape(four_shape)
    key_raw = jnp.dot(source, proj_key, preferred_element_type=jnp.float32).reshape(four_shape)
    value_low = jnp.dot(source, proj_value, preferred_element_type=jnp.float32).astype(jnp.bfloat16)
    value_low = value_low.reshape(four_shape)
    query_rot = head_prepare(query_raw, gain_query, cos_tab, sine_tab).astype(jnp.bfloat16)
    key_rot = head_prepare(key_raw, gain_key, cos_tab, sine_tab).astype(jnp.bfloat16)
    attended, log_total = attend(query_rot, key_rot, value_low, key_valid, score_scale)
    flat_attended = attended.reshape(flat_shape)
    branch = lax.psum_scatter(
        jnp.dot(flat_attended, proj_out, preferred_element_type=jnp.float32),
        "shard",
        scatter_dimension=0,
        tiled=True,
    )
    hidden = inputs + branch
    moe_low = rms_scale(hidden, gain_moe).astype(jnp.bfloat16)
    router_probs = soft_max(jnp.dot(moe_low, w_router, preferred_element_type=jnp.float32))
    route_hot = (
        routes[:, :, None] == jnp.arange(expert_count, dtype=jnp.int32)[None, None, :]
    ).astype(jnp.float32)
    gate_vals = jnp.sum(router_probs[:, None, :] * route_hot, axis=-1)
    slot_ids = slot_table(routes, expert_count)
    copies = jnp.repeat(moe_low, routes.shape[1], axis=0)
    send_rows = jnp.zeros((expert_count * CAP, model_width), jnp.bfloat16).at[slot_ids].set(copies)
    arrived = lax.all_to_all(
        send_rows.reshape(expert_count, CAP, model_width),
        "shard",
        split_axis=0,
        concat_axis=1,
        tiled=True,
    )
    gate_act = jnp.einsum("erd,edf->erf", arrived, w_gate, preferred_element_type=jnp.float32)
    up_act = jnp.einsum("erd,edf->erf", arrived, w_up, preferred_element_type=jnp.float32)
    sig_gate = jax.nn.sigmoid(gate_act)
    silu_gate = gate_act * sig_gate
    joined = (silu_gate * up_act).astype(jnp.bfloat16)
    expert_out = jnp.einsum(
        "erf,efd->erd", joined, w_down, preferred_element_type=jnp.float32
    ).astype(jnp.bfloat16)
    returned = lax.all_to_all(expert_out, "shard", split_axis=1, concat_axis=0, tiled=True).reshape(
        expert_count * CAP, model_width
    )
    picked = returned[slot_ids].astype(jnp.float32).reshape(row_count, -1, model_width)
    mixture = jnp.sum(picked * gate_vals[:, :, None], axis=1)
    output = (hidden + mixture).astype(jnp.bfloat16)
    grad_out = out_grad.astype(jnp.float32) * row_mask[:, None]
    grad_gates = jnp.sum(picked * grad_out[:, None, :], axis=-1)
    grad_rows = (
        (gate_vals[:, :, None] * grad_out[:, None, :]).astype(jnp.bfloat16).reshape(-1, model_width)
    )
    grad_send = (
        jnp.zeros((expert_count * CAP, model_width), jnp.bfloat16).at[slot_ids].set(grad_rows)
    )
    grad_arrived = lax.all_to_all(
        grad_send.reshape(expert_count, CAP, model_width),
        "shard",
        split_axis=0,
        concat_axis=1,
        tiled=True,
    )
    grad_joined = jnp.einsum(
        "erd,efd->erf", grad_arrived, w_down, preferred_element_type=jnp.float32
    )
    grad_down = jnp.einsum("erf,erd->efd", joined, grad_arrived, preferred_element_type=jnp.float32)
    grad_gate_act = (grad_joined * up_act * sig_gate * (1.0 + gate_act * (1.0 - sig_gate))).astype(
        jnp.bfloat16
    )
    grad_up_act = (grad_joined * silu_gate).astype(jnp.bfloat16)
    grad_expert_in = jnp.einsum(
        "erf,edf->erd", grad_gate_act, w_gate, preferred_element_type=jnp.float32
    ) + jnp.einsum("erf,edf->erd", grad_up_act, w_up, preferred_element_type=jnp.float32)
    grad_expert_in = grad_expert_in.astype(jnp.bfloat16)
    grad_gate_w = jnp.einsum(
        "erd,erf->edf", arrived, grad_gate_act, preferred_element_type=jnp.float32
    )
    grad_up_w = jnp.einsum("erd,erf->edf", arrived, grad_up_act, preferred_element_type=jnp.float32)
    grad_back = lax.all_to_all(
        grad_expert_in, "shard", split_axis=1, concat_axis=0, tiled=True
    ).reshape(expert_count * CAP, model_width)
    grad_moe_in = jnp.sum(
        grad_back[slot_ids].astype(jnp.float32).reshape(row_count, -1, model_width), axis=1
    )
    grad_probs = jnp.sum(grad_gates[:, :, None] * route_hot, axis=1)
    grad_logits = router_probs * (
        grad_probs - jnp.sum(router_probs * grad_probs, axis=-1, keepdims=True)
    )
    router_full = w_router.astype(jnp.float32)
    grad_moe_in = grad_moe_in + jnp.dot(grad_logits, router_full.T, precision=lax.Precision.HIGHEST)
    grad_router = jnp.dot(
        moe_low.astype(jnp.float32).T, grad_logits, precision=lax.Precision.HIGHEST
    )
    moe_unused, pull_moe = jax.vjp(rms_scale, hidden, gain_moe)
    grad_hidden_part, grad_gain_moe = pull_moe(grad_moe_in)
    grad_hidden = grad_out + grad_hidden_part
    grad_branch = grad_hidden.astype(jnp.bfloat16)
    branch_rows = lax.all_gather(grad_branch, "shard", axis=0, tiled=True)
    grad_attended = jnp.dot(branch_rows, proj_out.T, preferred_element_type=jnp.float32).astype(
        jnp.bfloat16
    )
    grad_out_w = jnp.dot(flat_attended.T, branch_rows, preferred_element_type=jnp.float32)
    grad_query_rot, grad_key_rot, grad_value = attend_back(
        query_rot,
        key_rot,
        value_low,
        key_valid,
        score_scale,
        log_total,
        grad_attended.reshape(four_shape),
    )

    def prepare(raw_proj, gain_vec):
        return head_prepare(raw_proj, gain_vec, cos_tab, sine_tab)

    query_unused, pull_query = jax.vjp(prepare, query_raw, gain_query)
    grad_query_raw, grad_gain_query = pull_query(grad_query_rot)
    key_unused, pull_key = jax.vjp(prepare, key_raw, gain_key)
    grad_key_raw, grad_gain_key = pull_key(grad_key_rot)
    grad_q_low = grad_query_raw.astype(jnp.bfloat16).reshape(flat_shape)
    grad_k_low = grad_key_raw.astype(jnp.bfloat16).reshape(flat_shape)
    grad_v_low = grad_value.reshape(flat_shape)
    grad_query_w = jnp.dot(source.T, grad_q_low, preferred_element_type=jnp.float32)
    grad_key_w = jnp.dot(source.T, grad_k_low, preferred_element_type=jnp.float32)
    grad_value_w = jnp.dot(source.T, grad_v_low, preferred_element_type=jnp.float32)
    grad_normed = lax.psum_scatter(
        (
            jnp.dot(grad_q_low, proj_query.T, preferred_element_type=jnp.float32)
            + jnp.dot(grad_k_low, proj_key.T, preferred_element_type=jnp.float32)
            + jnp.dot(grad_v_low, proj_value.T, preferred_element_type=jnp.float32)
        ).astype(jnp.bfloat16),
        "shard",
        scatter_dimension=0,
        tiled=True,
    ).astype(jnp.float32)
    attn_unused, pull_attn = jax.vjp(rms_scale, inputs, gain_attn)
    grad_input_part, grad_gain_attn = pull_attn(grad_normed)
    grad_input = grad_hidden + grad_input_part
    summed = (
        lax.psum(grad_query_w.astype(jnp.bfloat16), "rep").astype(jnp.float32),
        lax.psum(grad_key_w.astype(jnp.bfloat16), "rep").astype(jnp.float32),
        lax.psum(grad_value_w.astype(jnp.bfloat16), "rep").astype(jnp.float32),
        lax.psum(grad_out_w.astype(jnp.bfloat16), "rep").astype(jnp.float32),
        lax.psum(grad_gate_w.astype(jnp.bfloat16), "rep").astype(jnp.float32),
        lax.psum(grad_up_w.astype(jnp.bfloat16), "rep").astype(jnp.float32),
        lax.psum(grad_down.astype(jnp.bfloat16), "rep").astype(jnp.float32),
    )
    shared = lax.psum(
        (grad_gain_attn, grad_gain_query, grad_gain_key, grad_gain_moe, grad_router),
        ("rep", "shard"),
    )
    return (
        output,
        grad_input,
        shared[0],
        shared[1],
        shared[2],
        summed[0],
        summed[1],
        summed[2],
        summed[3],
        shared[3],
        shared[4],
        summed[4],
        summed[5],
        summed[6],
    )


def solution(mesh):
    return jax.shard_map(
        local,
        mesh=mesh,
        in_specs=(
            P(("rep", "shard"), None),
            P(("rep", "shard")),
            P(("rep", "shard"), None),
            P(),
            P(),
            P(),
            P(None, "shard"),
            P(None, "shard"),
            P(None, "shard"),
            P("shard", None),
            P(),
            P(),
            P("shard", None, None),
            P("shard", None, None),
            P("shard", None, None),
            P(("rep", "shard"), None),
        ),
        out_specs=(
            P(("rep", "shard"), None),
            P(("rep", "shard"), None),
            P(),
            P(),
            P(),
            P(None, "shard"),
            P(None, "shard"),
            P(None, "shard"),
            P("shard", None),
            P(),
            P(),
            P("shard", None, None),
            P("shard", None, None),
            P("shard", None, None),
        ),
        check_vma=False,
    )
```

profile of v0, /device:TPU:0, one launch (start us, length us, event | category | flops | bytes accessed | tf_op | source)
XLA Modules:
  0.0 2252.8 jit_solution(6892973722710807610)
XLA Ops:
  13.3 13.4 all-gather
  28.4 69.1 %all-gather.4.cloned.1.call-done = bf16[2048,2048]{1,0:T(8,128)(2,1)} async-done(((bf16[256,2048]{1,0:T(8,128)(2,1)}), bf16[2048,2048]{1,0:T(8,128)(2,1)}) %all-gather.4.cloned.1.call-update) | async-done | bytes 8388624 | tf_op jit(solution)/shard_map/all_gather | solution.py:126
  97.5 7.1 fusion.73
  104.6 2.8 reshape.259
  108.7 3.2 multiply_reduce_fusion.8
  114.7 8.0 fusion.72
  122.8 3.2 reshape.258
  126.0 4.9 multiply_reduce_fusion.9
  130.9 4.1 copy.289
  135.0 6.9 convolution_convert_fusion.9
  157.3 8.5 fusion.74
  167.1 4.5 reduce-window.6
  174.1 158.8 %reduce-scatter.3.cloned.1.call-done = f32[256,2048]{1,0:T(8,128)} async-done(((f32[2048,2048]{1,0:T(8,128)}), f32[256,2048]{1,0:T(8,128)}) %reduce-scatter.3.cloned.1.call-update) | async-done | bytes 2097168 | tf_op jit(solution)/shard_map/reduce_scatter | solution.py:142
  339.3 18.6 scatter_custom_fusion.1
  357.9 5.4 all-to-all-start.2
  363.4 17.6 scatter_custom_fusion
  380.9 188.8 %all-to-all-done.2 = bf16[16,144,2048]{2,1,0:T(8,128)(2,1)} async-done(((bf16[16,144,2048]{2,1,0:T(8,128)(2,1)}), bf16[16,144,2048]{2,1,0:T(8,128)(2,1)}, u32[]{:S(2)}, u32[]{:S(2)}) %all-to-all-start.2) | async-done | bytes 9437216 | tf_op jit(solution)/shard_map/all_to_all | solution.py:187
  569.7 5.5 all-to-all-start
  575.2 9.2 copy.306
  584.5 197.1 %all-to-all-done = bf16[16,144,2048]{2,1,0:T(8,128)(2,1)} async-done(((bf16[16,144,2048]{2,1,0:T(8,128)(2,1)}), bf16[16,144,2048]{2,1,0:T(8,128)(2,1)}, u32[]{:S(2)}, u32[]{:S(2)}) %all-to-all-start) | async-done | bytes 9437216 | tf_op jit(solution)/shard_map/all_to_all | solution.py:158
  781.6 9.4 copy.301
  790.9 17.2 fusion.76
  808.2 14.5 fusion.75
  822.7 22.9 %multiply_convert_fusion = (bf16[2,1152,1024]{2,1,0:T(8,128)(2,1)}, bf16[2,1152,1024]{2,1,0:T(8,128)(2,1)}, bf16[2,1152,1024]{2,1,0:T(8,128)(2,1)}) fusion(f32[2,1152,1024]{2,1,0:T(8,128)} %fusion.75, f32[2,1152,1024]{2,1,0:T(8,128)} %fusion.76, bf16[2,1152,2048]{2,1,0:T(8,128)(2,1)} %bitcast.161, bf16[2,1024,2048]{2,1,0:T(8,128)(2,1)} %param.30), kind=kOutput, calls=%fused_computation.14 | convolution fusion | flops 9699065856 | bytes 50855936 | tf_op jit(solution)/shard_map/erd,efd->erf/dot_general | solution.py:194
  845.5 14.2 convolution_convert_fusion
  859.8 27.9 %copy.302 = bf16[2,1152,2048]{2,0,1:T(2,128)(2,1)} copy(bf16[2,1152,2048]{2,1,0:T(8,128)(2,1)S(1)} %convolution_convert_fusion) | data formatting | bytes 18874368 | tf_op jit(solution)/shard_map/convert_element_type | solution.py:172
  887.7 5.3 all-to-all-start.1
  893.0 17.5 fusion.77
  910.5 18.6 add_convert_fusion
  929.1 18.2 copy.307
  947.3 152.0 %all-to-all-done.1 = bf16[2,1152,2048]{2,0,1:T(2,128)(2,1)} async-done(((bf16[2,1152,2048]{2,0,1:T(2,128)(2,1)}), bf16[2,1152,2048]{2,0,1:T(2,128)(2,1)}, u32[]{:S(2)}, u32[]{:S(2)}) %all-to-all-start.1) | async-done | bytes 9437216 | tf_op jit(solution)/shard_map/all_to_all | solution.py:173
  1099.4 5.1 all-to-all-start.3
  1104.8 11.8 copy.303
  1116.6 21.9 gather_fusion
  1138.5 9.5 fusion.1
  1148.2 162.6 %all-to-all-done.3 = bf16[2,1152,2048]{2,0,1:T(2,128)(2,1)} async-done(((bf16[2,1152,2048]{2,0,1:T(2,128)(2,1)}), bf16[2,1152,2048]{2,0,1:T(2,128)(2,1)}, u32[]{:S(2)}, u32[]{:S(2)}) %all-to-all-start.3) | async-done | bytes 9437216 | tf_op jit(solution)/shard_map/all_to_all | solution.py:210
  1310.8 11.8 copy.308
  1322.7 21.4 gather_fusion.1
  1344.1 11.4 convert_reduce_fusion
  1355.6 3.9 multiply_reduce_fusion.1
  1359.6 2.9 fusion.66
  1362.6 80.9 %all-gather.6.cloned.1.call-done = bf16[2048,2048]{1,0:T(8,128)(2,1)} async-done(((bf16[256,2048]{1,0:T(8,128)(2,1)}), bf16[2048,2048]{1,0:T(8,128)(2,1)}) %all-gather.6.cloned.1.call-update) | async-done | bytes 8388624 | tf_op jit(solution)/shard_map/all_gather | solution.py:229
  1443.5 5.8 convolution_convert_fusion.8
  1453.1 3.2 fusion.42
  1464.1 3.0 multiply_reduce_fusion.2
  1470.2 8.6 fusion.79
  1478.8 8.6 fusion.80
  1487.3 15.6 add_convert_fusion.1
  1503.1 18.2 convolution_convert_fusion.1
  1521.3 17.2 convolution_convert_fusion.2
  1538.6 15.7 convolution_convert_fusion.3
  1554.3 6.7 convolution_convert_fusion.4
  1561.0 7.1 convolution_convert_fusion.5
  1568.2 7.1 convolution_convert_fusion.6
  1575.3 3.5 convolution_convert_fusion.7
  1581.3 10.0 reduce-scatter.5.cloned.1.call-done
  1593.6 3.8 fusion.22
  1597.3 38.9 %all-reduce.4 = (f32[2048]{0:T(1024)}, f32[128]{0:T(128)}, f32[128]{0:T(128)}, f32[2048]{0:T(1024)}) all-reduce(f32[2048]{0:T(1024)S(1)} %get-tuple-element.22, f32[128]{0:T(128)S(1)} %get-tuple-element.56, f32[128]{0:T(128)S(1)} %get-tuple-element.18, f32[2048]{0:T(1024)S(1)} %copy-done.65), channel_id=1, replica_groups=mesh['rep'=4,'shard'=8] {'rep','shard'}, use_global_device_ids=true, to_apply=%region_27.28 | all-reduce | flops 4352 | bytes 34816 | tf_op jit(solution)/shard_map/psum | solution.py:279
  1636.2 478.4 %all-reduce.11.cloned.1.call-done = (bf16[2048,256]{1,0:T(8,128)(2,1)}, bf16[2048,256]{1,0:T(8,128)(2,1)}, bf16[2048,256]{1,0:T(8,128)(2,1)}, bf16[256,2048]{1,0...) async-done(((bf16[2048,256]{1,0:T(8,128)(2,1)}, bf16[2048,256]{1,0:T(8,128)(2,1)}, ...) | async-done | bytes 29360144 | tf_op jit(solution)/shard_map/psum | solution.py:271
  2114.6 2.9 convert_element_type.198
  2123.2 11.7 convert_element_type.206
  2134.9 11.7 convert_element_type.208
  2146.6 11.7 convert_element_type.210
  2158.3 85.6 %all-reduce.9.cloned.1.call-done = f32[2048,16]{0,1:T(8,128)} async-done(((f32[2048,16]{0,1:T(8,128)}), f32[2048,16]{0,1:T(8,128)}) %all-reduce.9.cloned.1.call-update) | async-done | bytes 131088 | tf_op jit(solution)/shard_map/psum | solution.py:279
  (283 shorter events, 63.4 us)
Async XLA Ops:
  7.2 150.1 %copy-start = (bf16[256,2048]{1,0:T(8,128)(2,1)S(1)}, bf16[256,2048]{1,0:T(8,128)(2,1)}, u32[]{:S(2)}) copy-start(bf16[256,2048]{1,0:T(8,128)(2,1)} %param.25) | copy-start | bytes 3145732
  7.2 90.3 %copy-start.33 = (bf16[2048,256]{1,0:T(8,128)(2,1)S(1)}, bf16[2048,256]{1,0:T(8,128)(2,1)}, u32[]{:S(2)}) copy-start(bf16[2048,256]{1,0:T(8,128)(2,1)} %param.23) | copy-start | bytes 3145732
  7.2 90.3 %all-gather.4.cloned.1.call-start = ((), (), s32[]{:S(2)}) async-start(), calls=%async_computation.6 | async-start | bytes 9437184 | tf_op jit(solution)/shard_map/all_gather | solution.py:126
  12.6 320.2 %reduce-scatter.3.cloned.1.call-start = ((), (), s32[]{:S(2)}) async-start(), calls=%async_computation.7 | async-start | bytes 18874368 | tf_op jit(solution)/shard_map/reduce_scatter | solution.py:142
  114.7 33.3 %copy-start.3 = (f32[8,256,2,128]{1,3,2,0:T(8,128)}, f32[8,256,2,128]{1,3,2,0:T(8,128)S(1)}, u32[]{:S(2)}) copy-start(f32[8,256,2,128]{1,3,2,0:T(8,128)S(1)} %copy.292) | copy-start | bytes 6291460
  141.9 6.1 copy-start.82
  141.9 6.1 copy-start.84
  146.4 3.9 copy-start.48
  165.8 6.7 copy-start.22
  166.5 166.3 %copy-start.8 = (bf16[256,2048]{1,0:T(8,128)(2,1)S(1)}, bf16[256,2048]{1,0:T(8,128)(2,1)}, u32[]{:S(2)}) copy-start(bf16[256,2048]{1,0:T(8,128)(2,1)} %param.16) | copy-start | bytes 3145732
  172.3 162.5 %copy-start.86 = (f32[256]{0:T(256)}, f32[256]{0:T(256)S(1)}, u32[]{:S(2)}) copy-start(f32[256]{0:T(256)S(1)} %compare_convert_fusion) | copy-start | bytes 3076
  172.5 190.8 %copy-start.66 = (s32[2048,1]{0,1:T(1,128)}, s32[2048,1]{0,1:T(1,128)S(1)}, u32[]{:S(2)}) copy-start(s32[2048,1]{0,1:T(1,128)S(1)} %compare_select_fusion) | copy-start | bytes 24580
  172.5 163.6 %copy-start.61 = (f32[2048]{0:T(1024)S(1)}, f32[2048]{0:T(1024)}, u32[]{:S(2)}) copy-start(f32[2048]{0:T(1024)} %param.26) | copy-start | bytes 24580
  174.1 163.3 %copy-start.39 = (bf16[2048,16]{0,1:T(8,128)(2,1)S(1)}, bf16[2048,16]{0,1:T(8,128)(2,1)}, u32[]{:S(2)}) copy-start(bf16[2048,16]{0,1:T(8,128)(2,1)} %param.27) | copy-start | bytes 196612
  334.8 3.1 copy-start.80
  334.8 4.5 copy-start.10
  334.8 3.1 copy-start.70
  339.2 18.7 copy-start.30
  357.9 5.4 copy-start.14
  357.9 211.8 %all-to-all-start.2 = ((bf16[16,144,2048]{2,1,0:T(8,128)(2,1)}), bf16[16,144,2048]{2,1,0:T(8,128)(2,1)}, u32[]{:S(2)}, u32[]{:S(2)}) async-start(bf16[16,144,2048]{2,1,0:T(8,128)(2,1)} %bitcast.160), calls=%async_computation.3 | async-start | bytes 18874368 | tf_op jit(solution)/shard_map/all_to_all | solution.py:187
  569.7 211.9 %all-to-all-start = ((bf16[16,144,2048]{2,1,0:T(8,128)(2,1)}), bf16[16,144,2048]{2,1,0:T(8,128)(2,1)}, u32[]{:S(2)}, u32[]{:S(2)}) async-start(bf16[16,144,2048]{2,1,0:T(8,128)(2,1)} %bitcast.159), calls=%async_computation.1 | async-start | bytes 18874368 | tf_op jit(solution)/shard_map/all_to_all | solution.py:158
  790.9 17.2 copy-start.16
  887.7 211.7 %all-to-all-start.1 = ((bf16[2,1152,2048]{2,0,1:T(2,128)(2,1)}), bf16[2,1152,2048]{2,0,1:T(2,128)(2,1)}, u32[]{:S(2)}, u32[]{:S(2)}) async-start(bf16[2,1152,2048]{2,0,1:T(2,128)(2,1)} %copy.302), calls=%async_computation.2 | async-start | bytes 18874368 | tf_op jit(solution)/shard_map/all_to_all | solution.py:173
  947.3 157.4 %copy-start.67 = (s32[2048,1]{0,1:T(1,128)S(1)}, s32[2048,1]{0,1:T(1,128)}, u32[]{:S(2)}) copy-start(s32[2048,1]{0,1:T(1,128)} %copy-done.66) | copy-start | bytes 24580
  1099.4 211.4 %all-to-all-start.3 = ((bf16[2,1152,2048]{2,0,1:T(2,128)(2,1)}), bf16[2,1152,2048]{2,0,1:T(2,128)(2,1)}, u32[]{:S(2)}, u32[]{:S(2)}) async-start(bf16[2,1152,2048]{2,0,1:T(2,128)(2,1)} %copy.307), calls=%async_computation.4 | async-start | bytes 18874368 | tf_op jit(solution)/shard_map/all_to_all | solution.py:210
  1104.5 339.0 %all-gather.6.cloned.1.call-start = ((), (), s32[]{:S(2)}) async-start(), calls=%async_computation.8 | async-start | bytes 9437184 | tf_op jit(solution)/shard_map/all_gather | solution.py:229
  1116.6 21.9 copy-start.11
  1116.6 21.9 copy-start.31
  1138.5 9.6 copy-start.59
  1138.5 9.6 copy-start.47
  1138.5 9.6 copy-start.73
  1138.5 9.6 copy-start.77
  1148.1 207.4 %copy-start.44 = (f32[256,16]{0,1:T(8,128)}, f32[256,16]{0,1:T(8,128)S(1)}, u32[]{:S(2)}) copy-start(f32[256,16]{0,1:T(8,128)S(1)} %select_reduce_fusion) | copy-start | bytes 49156
  1148.2 207.3 %copy-start.78 = (f32[256]{0:T(256)}, f32[256]{0:T(256)S(1)}, u32[]{:S(2)}) copy-start(f32[256]{0:T(256)S(1)} %multiply_reduce_fusion.10) | copy-start | bytes 3076
  1344.0 11.5 copy-start.7
  1344.0 11.5 copy-start.40
  1344.0 11.5 copy-start.42
  1344.1 11.5 copy-start.62
  1344.1 11.5 copy-start.71
  1355.5 4.0 copy-start.81
  1355.6 4.0 copy-start.21
  1355.6 4.0 copy-start.23
  1355.6 4.0 copy-start.87
  1362.5 228.8 %reduce-scatter.5.cloned.1.call-start = ((), (), s32[]{:S(2)}) async-start(), calls=%async_computation.9 | async-start | bytes 9437184 | tf_op jit(solution)/shard_map/reduce_scatter | solution.py:257
  1450.6 5.7 copy-start.27
  1453.1 3.5 copy-start.2
  1470.2 8.6 copy-start.28
  1470.2 8.6 copy-start.34
  1503.0 611.6 %all-reduce.11.cloned.1.call-start = ((), (), s32[]{:S(2)}) async-start(), calls=%async_computation.11 | async-start | bytes 58720256 | tf_op jit(solution)/shard_map/psum | solution.py:271
  1503.0 35.5 %slice-start = ((s8[9437184]{0:T(1024)(128)(4,1)}), s8[4194304]{0:T(1024)(128)(4,1)S(1)}, s32[]{:S(2)}) async-start(s8[9437184]{0:T(1024)(128)(4,1)} %bitcast.166), calls=%async_computation.12 | async-start | bytes 8388608
  1503.0 35.5 %slice-start.1 = ((s8[9437184]{0:T(1024)(128)(4,1)}), s8[4194304]{0:T(1024)(128)(4,1)S(1)}, s32[]{:S(2)}) async-start(s8[9437184]{0:T(1024)(128)(4,1)} %bitcast.166), calls=%async_computation.13 | async-start | bytes 8388608
  1521.3 17.2 slice-start.2
  1538.5 15.7 copy-start.25
  1561.0 7.1 copy-start.29
  1561.0 14.2 slice-start.3
  1568.2 7.1 slice-start.4
  1578.8 12.5 copy-start.9
  1578.8 12.4 copy-start.60
  1578.9 12.4 copy-start.69
  1578.9 14.7 copy-start.75
  1578.9 665.0 %all-reduce.9.cloned.1.call-start = ((), (), s32[]{:S(2)}) async-start(), calls=%async_computation.10 | async-start | bytes 262144 | tf_op jit(solution)/shard_map/psum | solution.py:279
  1581.3 16.1 copy-start.65
  2114.6 5.6 copy-start.36
  2114.6 7.0 copy-start.35
  (39 other events, 61.3 us)
Sparse Core Ops, SparseCore 0:
  12.7 84.7 all-gather.3
  165.9 166.8 reduce-scatter.2
  1362.6 80.8 all-gather.5
  1503.1 88.1 reduce-scatter.4
  1597.0 517.5 all-reduce.10
  2121.5 122.3 all-reduce.8
where the time goes:
time: 2260 us; the launch traced here: 2250 us
  waiting for transfers between devices  1580 us (70%)
  matrix products  263 us (12%)
  local copies, waits for them, and re-layouts  191 us (8%)
  other arithmetic  125 us (6%)
  blocking collectives  52.3 us (2%)
    psum x1, waiting for transfers between devices, local(): lax.psum(grad_query_w.astype(jnp.bfloat16), 'rep').astype(jnp.float32)  478 us
    all_to_all x1, waiting for transfers between devices, local(): lax.all_to_all(send_rows.reshape(expert_count, CAP, model_width), 'shard'...  197 us
    all_to_all x1, waiting for transfers between devices, local(): lax.all_to_all(grad_send.reshape(expert_count, CAP, model_width), 'shard'...  189 us
    all_to_all x1, waiting for transfers between devices, local(): lax.all_to_all(grad_expert_in, 'shard', split_axis=1, concat_axis=0, tile...  163 us
    reduce_scatter x1, waiting for transfers between devices, local(): lax.psum_scatter(jnp.dot(flat_attended, proj_out, preferred_element_type=...  159 us
    all_to_all x1, waiting for transfers between devices, local(): lax.all_to_all(expert_out, 'shard', split_axis=1, concat_axis=0, tiled=True)  152 us
    psum x1, waiting for transfers between devices, local(): lax.psum((grad_gain_attn, grad_gain_query, grad_gain_key, grad_gain_moe,...  85.6 us
    all_gather x1, waiting for transfers between devices, local(): branch_rows = lax.all_gather(grad_branch, 'shard', axis=0, tiled=True)  80.9 us
  transfers between devices with their start and end apart: 10, of which 10 were waited for; matrix products, arithmetic and copies ran while one was open for 12% of the time, Pallas kernels for 0%

commit v1 on v0

v1 whole, which is shorter than its diff:
```python
import functools

import jax
import jax.numpy as jnp
from jax import lax
from jax.experimental import pallas as pl
from jax.experimental.pallas import tpu as pltpu
from jax.sharding import PartitionSpec as P

CAP = 144
LINES = 16
EPS_NORM = 1e-06
ROPE_BASE = 50000.0
MASKED = -1e30
VMEM_BYTES = 60 * 1024 * 1024
LOW = jnp.bfloat16
WIDE = jnp.float32
COST = pl.CostEstimate(flops=1 << 20, bytes_accessed=1 << 16, transcendentals=0)


def dot_nn(a, b):
    return lax.dot_general(a, b, (((1,), (0,)), ((), ())), preferred_element_type=WIDE)


def dot_nt(a, b):
    return lax.dot_general(a, b, (((1,), (1,)), ((), ())), preferred_element_type=WIDE)


def dot_tn(a, b):
    return lax.dot_general(a, b, (((0,), (0,)), ((), ())), preferred_element_type=WIDE)


def rope_tables(seq_len, head_dim):
    half_dim = head_dim // 2
    places = jnp.arange(seq_len, dtype=WIDE)
    freqs = ROPE_BASE ** (-jnp.arange(half_dim, dtype=WIDE) * (2.0 / head_dim))
    angles = places[:, None] * freqs[None, :]
    cosine, sine = (jnp.cos(angles), jnp.sin(angles))
    return (
        jnp.concatenate([cosine, cosine], axis=-1),
        jnp.concatenate([-sine, sine], axis=-1),
    )


def head_forward(raw, gain, cos_tab, sin_tab):
    scale = lax.rsqrt(jnp.mean(raw * raw, axis=-1, keepdims=True) + EPS_NORM)
    plain = raw * scale
    scaled = plain * gain
    turned = pltpu.roll(scaled, raw.shape[-1] // 2, axis=1)
    return (scaled * cos_tab + turned * sin_tab, plain, scale)


def head_backward(grad, plain, scale, gain, cos_tab, sin_tab):
    back = grad * cos_tab + pltpu.roll(grad * sin_tab, grad.shape[-1] // 2, axis=1)
    gain_grad = jnp.sum(back * plain, axis=0, keepdims=True)
    back = back * gain
    raw_grad = scale * (back - plain * jnp.mean(back * plain, axis=-1, keepdims=True))
    return (raw_grad, gain_grad)


def soft_weights(query, key, length, score_scale):
    scores = dot_nt(query, key) * score_scale
    places = lax.broadcasted_iota(jnp.int32, scores.shape, 1).astype(WIDE)
    scores = jnp.where(places < length, scores, MASKED)
    expo = jnp.exp(scores - jnp.max(scores, axis=-1, keepdims=True))
    return expo / jnp.sum(expo, axis=-1, keepdims=True)


def attend_block(normed, length, wq, wk, wv, wo, gq, gk, cos_tab, sin_tab, keep):
    head_dim = gq.shape[-1]
    query_raw, key_raw = (dot_nn(normed, wq[...]), dot_nn(normed, wk[...]))
    value = dot_nn(normed, wv[...]).astype(LOW)
    heads = []
    for head in range(query_raw.shape[-1] // head_dim):
        span = slice(head * head_dim, (head + 1) * head_dim)
        query = head_forward(query_raw[:, span], gq, cos_tab, sin_tab)[0].astype(LOW)
        key = head_forward(key_raw[:, span], gk, cos_tab, sin_tab)[0].astype(LOW)
        weights = soft_weights(query, key, length, head_dim**-0.5).astype(LOW)
        heads.append(dot_nn(weights, value[:, span]).astype(LOW))
    joined = heads[0] if len(heads) == 1 else jnp.concatenate(heads, axis=-1)
    keep(query_raw, key_raw, value, joined)
    return dot_nn(joined, wo[...]).astype(LOW)


def attend_kernel(
    pk_ref, wq, wk, wv, wo, gq, gk, cos_ref, sin_ref, part_ref, qr_ref, kr_ref, v_ref, o_ref
):
    rows = pk_ref.shape[1] - LINES
    length = pk_ref[0, rows:, rows : rows + 128].astype(WIDE)[0:1, 0:1]

    def keep(query_raw, key_raw, value, joined):
        qr_ref[0], kr_ref[0], v_ref[0], o_ref[0] = (query_raw, key_raw, value, joined)

    part_ref[0] = attend_block(
        pk_ref[0, :rows], length, wq, wk, wv, wo, gq[...], gk[...], cos_ref[...], sin_ref[...], keep
    )


def whole_spec(array):
    return pl.BlockSpec(array.shape, lambda *_: (0,) * array.ndim, pipeline_mode=pl.Buffered(1))


def first_spec(array):
    return pl.BlockSpec((1,) + array.shape[1:], lambda i: (i,) + (0,) * (array.ndim - 1))


def attend_forward(packets, wq, wk, wv, wo, gq, gk, cos_tab, sin_tab):
    count, lines, width = packets.shape
    rows, wide = (lines - LINES, wq.shape[1])
    fixed = (wq, wk, wv, wo, gq, gk, cos_tab, sin_tab)
    out = (
        jax.ShapeDtypeStruct((count, rows, width), LOW),
        jax.ShapeDtypeStruct((count, rows, wide), WIDE),
        jax.ShapeDtypeStruct((count, rows, wide), WIDE),
        jax.ShapeDtypeStruct((count, rows, wide), LOW),
        jax.ShapeDtypeStruct((count, rows, wide), LOW),
    )
    return pl.pallas_call(
        attend_kernel,
        grid=(count,),
        in_specs=[first_spec(packets)] + [whole_spec(array) for array in fixed],
        out_specs=[first_spec(array) for array in out],
        out_shape=out,
        compiler_params=pltpu.CompilerParams(vmem_limit_bytes=VMEM_BYTES),
        cost_estimate=COST,
        name="attend_forward",
    )(packets, *fixed)


def attend_back_kernel(
    da_ref, pk_ref, qr_ref, kr_ref, v_ref, o_ref,
    wq, wk, wv, wo, gq, gk, cos_ref, sin_ref,
    part_ref, gw_in, gw_out, gain_q, gain_k, gain_n,
):
    rows = pk_ref.shape[1] - LINES
    head_dim = gq.shape[-1]
    length = pk_ref[0, rows:, rows : rows + 128].astype(WIDE)[0:1, 0:1]
    cos_tab, sin_tab = (cos_ref[...], sin_ref[...])
    score_scale = head_dim**-0.5

    @pl.when(pl.program_id(0) == 0)
    def _():
        for ref in (gw_in, gw_out, gain_q, gain_k, gain_n):
            ref[...] = jnp.zeros_like(ref)

    upper = da_ref[0]
    grad_joined = dot_nt(upper, wo[...]).astype(LOW)
    gw_out[...] += dot_tn(o_ref[0], upper)
    grads_q, grads_k, grads_v = ([], [], [])
    for head in range(qr_ref.shape[-1] // head_dim):
        span = slice(head * head_dim, (head + 1) * head_dim)
        query, plain_q, scale_q = head_forward(qr_ref[0, :, span], gq[...], cos_tab, sin_tab)
        key, plain_k, scale_k = head_forward(kr_ref[0, :, span], gk[...], cos_tab, sin_tab)
        query, key, value = (query.astype(LOW), key.astype(LOW), v_ref[0, :, span])
        probs = soft_weights(query, key, length, score_scale)
        grad_out = grad_joined[:, span]
        grads_v.append(dot_tn(probs.astype(LOW), grad_out).astype(LOW))
        grad_probs = dot_nt(grad_out, value)
        inner = jnp.sum(probs * grad_probs, axis=-1, keepdims=True)
        grad_scores = (probs * (grad_probs - inner)).astype(LOW)
        grad_q, head_gain_q = head_backward(
            dot_nn(grad_scores, key) * score_scale, plain_q, scale_q, gq[...], cos_tab, sin_tab
        )
        grad_k, head_gain_k = head_backward(
            dot_tn(grad_scores, query) * score_scale, plain_k, scale_k, gk[...], cos_tab, sin_tab
        )
        gain_q[...] += head_gain_q
        gain_k[...] += head_gain_k
        grads_q.append(grad_q.astype(LOW))
        grads_k.append(grad_k.astype(LOW))
    wide = qr_ref.shape[-1]
    grads = jnp.concatenate(grads_q + grads_k + grads_v, axis=-1)
    part = (
        dot_nt(grads[:, :wide], wq[...])
        + dot_nt(grads[:, wide : 2 * wide], wk[...])
        + dot_nt(grads[:, 2 * wide :], wv[...])
    )
    normed = pk_ref[0, :rows]
    part_ref[0] = part.astype(LOW)
    gain_n[...] += jnp.sum(part * normed.astype(WIDE), axis=0, keepdims=True)
    gw_in[...] += dot_tn(normed, grads)


def attend_backward(upper, packets, kept, wq, wk, wv, wo, gq, gk, cos_tab, sin_tab):
    count, lines, width = packets.shape
    rows, wide = (lines - LINES, wq.shape[1])
    blocks = (upper, packets) + tuple(kept)
    fixed = (wq, wk, wv, wo, gq, gk, cos_tab, sin_tab)
    sums = tuple(
        jax.ShapeDtypeStruct(shape, WIDE)
        for shape in ((width, 3 * wide), wo.shape, gq.shape, gk.shape, (1, width))
    )
    return pl.pallas_call(
        attend_back_kernel,
        grid=(count,),
        in_specs=[first_spec(array) for array in blocks] + [whole_spec(array) for array in fixed],
        out_specs=[first_spec(upper)] + [whole_spec(array) for array in sums],
        out_shape=(jax.ShapeDtypeStruct((count, rows, width), LOW),) + sums,
        compiler_params=pltpu.CompilerParams(vmem_limit_bytes=VMEM_BYTES),
        cost_estimate=COST,
        name="attend_backward",
    )(*blocks, *fixed)


def slot_spots(table, expert):
    row_count = table.shape[1]
    slots = lax.broadcasted_iota(jnp.int32, (CAP, row_count), 0).astype(WIDE) + 1.0
    mine = lax.broadcasted_iota(jnp.int32, table.shape, 0) == expert
    ranks = jnp.sum(jnp.where(mine, table, 0.0), axis=0, keepdims=True)
    return (slots == ranks).astype(LOW)


def expert_kernel(counts, batch, ex_ref, wg, wu, wd, wr, *refs):
    sources = len(counts)
    rows_in, cots_in = (refs[:sources], refs[sources : 2 * sources])
    x_ref, y_ref, m_ref, dg_ref, du_ref, dgate_ref, rows_buf, cots_buf, sems = refs[2 * sources :]
    steps = sum(counts) // batch
    turn = pl.program_id(0) * steps + pl.program_id(1)
    slot = lax.rem(turn, 2)
    row_count = rows_buf.shape[2]

    def copies(source, offset, place):
        span = pl.ds(offset, batch)
        return (
            pltpu.make_async_copy(rows_in[source].at[span], rows_buf.at[place], sems.at[0, place]),
            pltpu.make_async_copy(cots_in[source].at[span], cots_buf.at[place], sems.at[1, place]),
        )

    def fetch(step, place):
        begin = 0
        for source, count in enumerate(counts):
            size = count // batch

            @pl.when((step >= begin) & (step < begin + size))
            def _(source=source, begin=begin):
                for copy in copies(source, (step - begin) * batch, place):
                    copy.start()

            begin += size

    @pl.when(turn == 0)
    def _():
        fetch(turn, slot)

    @pl.when(turn + 1 < pl.num_programs(0) * steps)
    def _():
        fetch(lax.rem(turn + 1, steps), 1 - slot)

    for copy in copies(0, 0, slot):
        copy.wait()
    hidden = wg.shape[-1]
    expert = ex_ref[pl.program_id(0)]
    for seq in range(batch):
        table = cots_buf[slot, seq, row_count:, :row_count].astype(WIDE)
        spots = slot_spots(table, expert)
        span = pl.ds(seq * CAP, CAP)
        x_ref[0, span] = dot_nn(spots, rows_buf[slot, seq]).astype(LOW)
        y_ref[0, span] = dot_nn(spots, cots_buf[slot, seq, :row_count]).astype(LOW)
    x_all, y_all = (x_ref[0], y_ref[0])
    logits = dot_nn(x_all, wr[...])
    expo = jnp.exp(logits - jnp.max(logits, axis=-1, keepdims=True))
    chosen = lax.broadcasted_iota(jnp.int32, expo.shape, 1) == expert
    gates = jnp.sum(jnp.where(chosen, expo, 0.0), axis=-1, keepdims=True) / jnp.sum(
        expo, axis=-1, keepdims=True
    )
    step = min(256, hidden)
    dgate = jnp.zeros((x_all.shape[0], 1), WIDE)
    for start in range(0, hidden, step):
        span = slice(start, start + step)
        gate_act, up_act = (dot_nn(x_all, wg[0, :, span]), dot_nn(x_all, wu[0, :, span]))
        plain_grad = dot_nt(y_all, wd[0, span, :])
        sig = jax.nn.sigmoid(gate_act)
        silu = gate_act * sig
        joined = silu * up_act
        dgate += jnp.sum(joined * plain_grad, axis=-1, keepdims=True)
        grad = plain_grad * gates
        m_ref[0, :, span] = (joined * gates).astype(LOW)
        dg_ref[0, :, span] = (grad * up_act * (sig + silu * (1.0 - sig))).astype(LOW)
        du_ref[0, :, span] = (grad * silu).astype(LOW)
    dgate_ref[0] = jnp.broadcast_to(dgate, dgate_ref.shape[1:])


def expert_acts(ids, rows, cots, wg, wu, wd, wr, batch=4):
    row_count, width = rows[0].shape[1:]
    counts = tuple(array.shape[0] for array in rows)
    count = sum(counts)
    own, _, hidden = wg.shape
    out_rows = batch * CAP

    def acts(cols, kind=LOW):
        return jax.ShapeDtypeStruct((own, count * CAP, cols), kind)

    def act_spec(cols):
        return pl.BlockSpec((1, out_rows, cols), lambda e, i: (e, i, 0))

    def weight_spec(array):
        return pl.BlockSpec(
            (1,) + array.shape[1:], lambda e, i: (e, 0, 0), pipeline_mode=pl.Buffered(1)
        )

    any_spec = pl.BlockSpec(memory_space=pl.ANY)
    columns = (width, width, hidden, hidden, hidden, 128)
    return pl.pallas_call(
        functools.partial(expert_kernel, counts, batch),
        grid=(own, count // batch),
        in_specs=[
            pl.BlockSpec(memory_space=pltpu.SMEM),
            weight_spec(wg),
            weight_spec(wu),
            weight_spec(wd),
            pl.BlockSpec(wr.shape, lambda e, i: (0, 0)),
        ]
        + [any_spec] * (2 * len(counts)),
        out_specs=[act_spec(cols) for cols in columns],
        out_shape=tuple(acts(cols) for cols in columns[:5]) + (acts(128, WIDE),),
        scratch_shapes=[
            pltpu.VMEM((2, batch) + rows[0].shape[1:], LOW),
            pltpu.VMEM((2, batch) + cots[0].shape[1:], LOW),
            pltpu.SemaphoreType.DMA((2, 2)),
        ],
        compiler_params=pltpu.CompilerParams(vmem_limit_bytes=VMEM_BYTES),
        cost_estimate=COST,
        name="expert_acts",
    )(ids, wg, wu, wd, wr, *rows, *cots)


def pull_kernel(ex_ref, rows_ref, cot_ref, dg_ref, du_ref, dgate_ref, wg, wu, wr, part_ref, router):
    batch, row_count, _ = rows_ref.shape
    own = wg.shape[0]

    @pl.when(pl.program_id(0) == 0)
    def _():
        router[...] = jnp.zeros_like(router)

    backs = [
        (dot_nt(dg_ref[e], wg[e]) + dot_nt(du_ref[e], wu[e])).astype(LOW) for e in range(own)
    ]
    for seq in range(batch):
        table = cot_ref[seq, :, :row_count].astype(WIDE)
        logits = dot_nn(rows_ref[seq], wr[...])
        expo = jnp.exp(logits - jnp.max(logits, axis=-1, keepdims=True))
        probs = expo / jnp.sum(expo, axis=-1, keepdims=True)
        columns = lax.broadcasted_iota(jnp.int32, probs.shape, 1)
        grad_logits = jnp.zeros_like(probs)
        span = slice(seq * CAP, (seq + 1) * CAP)
        total = jnp.zeros(part_ref.shape[1:], WIDE)
        for e in range(own):
            spots = slot_spots(table, ex_ref[e])
            total += dot_tn(spots, backs[e][span])
            dgate = dgate_ref[e, span]
            high = dgate.astype(LOW)
            rest = (dgate - high.astype(WIDE)).astype(LOW)
            at_rows = (dot_tn(spots, high) + dot_tn(spots, rest))[:, : probs.shape[1]]
            chosen = (columns == ex_ref[e]).astype(WIDE)
            prob = jnp.sum(probs * chosen, axis=-1, keepdims=True)
            grad_logits += at_rows * prob * (chosen - probs)
        low_logits = grad_logits.astype(LOW)
        part_ref[seq] = (total + dot_nt(low_logits, wr[...])).astype(LOW)
        router[...] += dot_tn(rows_ref[seq], low_logits)


def mix_kernel(ex_ref, cot_ref, m_ref, wd, part_ref):
    batch, row_count, _ = part_ref.shape
    own = wd.shape[0]
    outs = [dot_nn(m_ref[e], wd[e]).astype(LOW) for e in range(own)]
    for seq in range(batch):
        table = cot_ref[seq, :, :row_count].astype(WIDE)
        span = slice(seq * CAP, (seq + 1) * CAP)
        total = sum(dot_tn(slot_spots(table, ex_ref[e]), outs[e][span]) for e in range(own))
        part_ref[seq] = total.astype(LOW)


def spread_call(kernel, name, ids, by_seq, cots, by_slot, fixed, router_shape, batch=2):
    count, lines, width = cots.shape
    row_count = lines - LINES
    part = jax.ShapeDtypeStruct((count, row_count, width), LOW)

    def seq_spec(array):
        return pl.BlockSpec((batch,) + array.shape[1:], lambda i: (i, 0, 0))

    def slot_spec(array):
        return pl.BlockSpec((array.shape[0], batch * CAP, array.shape[2]), lambda i: (0, i, 0))

    return pl.pallas_call(
        kernel,
        grid=(count // batch,),
        in_specs=[pl.BlockSpec(memory_space=pltpu.SMEM)]
        + [seq_spec(array) for array in by_seq]
        + [pl.BlockSpec((batch, LINES, width), lambda i: (i, row_count // LINES, 0))]
        + [slot_spec(array) for array in by_slot]
        + [whole_spec(array) for array in fixed],
        out_specs=[seq_spec(part)] + [whole_spec(shape) for shape in router_shape],
        out_shape=[part] + list(router_shape),
        compiler_params=pltpu.CompilerParams(vmem_limit_bytes=VMEM_BYTES),
        cost_estimate=COST,
        name=name,
    )(ids, *by_seq, cots, *by_slot, *fixed)


def weight_grad(lefts, rights):
    own, _, left_cols = lefts[0].shape
    right_cols = rights[0].shape[-1]
    sets = len(lefts)
    left_tile, right_tile = (min(512, left_cols), min(1024, right_cols))

    def kernel(*refs):
        refs[2 * sets][0] = sum(dot_tn(refs[i][0], refs[sets + i][0]) for i in range(sets))

    return pl.pallas_call(
        kernel,
        grid=(own, right_cols // right_tile, left_cols // left_tile),
        in_specs=[
            pl.BlockSpec((1, array.shape[1], left_tile), lambda e, r, l: (e, 0, l))
            for array in lefts
        ]
        + [
            pl.BlockSpec((1, array.shape[1], right_tile), lambda e, r, l: (e, 0, r))
            for array in rights
        ],
        out_specs=pl.BlockSpec((1, left_tile, right_tile), lambda e, r, l: (e, l, r)),
        out_shape=jax.ShapeDtypeStruct((own, left_cols, right_cols), WIDE),
        compiler_params=pltpu.CompilerParams(vmem_limit_bytes=VMEM_BYTES),
        cost_estimate=COST,
        name="weight_grad",
    )(*lefts, *rights)


def rms_parts(values):
    scale = lax.rsqrt(jnp.mean(values * values, axis=-1, keepdims=True) + EPS_NORM)
    return (values * scale, scale)


def rms_back(plain, scale, gain, grad):
    back = grad * gain
    return scale * (back - plain * jnp.mean(back * plain, axis=-1, keepdims=True))


def local(
    tokens, lengths, routes, gain_attn, gain_query, gain_key,
    w_query, w_key, w_value, w_out, gain_moe, w_router,
    w_gate, w_up, w_down, out_grad,
):
    row_count, width = tokens.shape
    head_dim = gain_query.shape[0]
    groups, replicas = (lax.axis_size("shard"), lax.axis_size("rep"))
    expert_count, own = (w_router.shape[1], w_gate.shape[0])
    wide = w_query.shape[1]
    after = lax.optimization_barrier
    gain_q, gain_k = (gain_query.reshape(1, -1), gain_key.reshape(1, -1))
    cos_tab, sin_tab = rope_tables(row_count, head_dim)
    ids = lax.axis_index("shard") * own + jnp.arange(own, dtype=jnp.int32)

    def flip_replica(values, bits):
        return lax.ppermute(values, "rep", [(i, i ^ bits) for i in range(replicas)])

    def flip_shard(values, bits):
        return lax.ppermute(values, "shard", [(i, i ^ bits) for i in range(groups)])

    def own_rail(blocks):
        pairs = blocks.reshape((groups // 2, 2) + blocks.shape[1:])
        return lax.dynamic_index_in_dim(pairs, lax.axis_index("shard") % 2, axis=1, keepdims=False)

    def foreign(blocks):
        rail = own_rail(blocks)
        mine = [flip_replica(rail, bits) for bits in (1, 2, 3)]
        return mine + [flip_shard(values, 1) for values in mine]

    def scatter_sum(parts):
        return lax.psum_scatter(
            parts.reshape(-1, width), "shard", scatter_dimension=0, tiled=True
        ).astype(WIDE)

    inputs = tokens.astype(WIDE)
    row_mask = (jnp.arange(row_count, dtype=jnp.int32) < lengths[0])[:, None]
    named = jnp.any(
        routes[None, :, :] == jnp.arange(expert_count, dtype=jnp.int32)[:, None, None], axis=-1
    )
    upto = (jnp.arange(row_count)[:, None] <= jnp.arange(row_count)[None, :]).astype(LOW)
    ranks = jnp.where(named, dot_nn(named.astype(LOW), upto), 0.0).astype(LOW)
    lines = jnp.concatenate(
        [ranks, jnp.broadcast_to(lengths[0].astype(LOW), (expert_count, width - row_count))], axis=1
    )
    plain_in, scale_in = rms_parts(inputs)
    packet = jnp.concatenate([(plain_in * gain_attn).astype(LOW), lines], axis=0)
    packets = lax.all_gather(packet, "shard", axis=0)
    cot_low = jnp.where(row_mask, out_grad, 0.0)
    cot_packet = jnp.concatenate([cot_low, lines], axis=0)
    cot_packet, packets = after((cot_packet, packets))
    cots = lax.all_gather(cot_packet, "shard", axis=0)

    heads = (w_query, w_key, w_value, w_out, gain_q, gain_k, cos_tab, sin_tab)
    part, *kept = attend_forward(packets, *heads)
    hidden = inputs + scatter_sum(part)
    plain_mid, scale_mid = rms_parts(hidden)
    moe_low = (plain_mid * gain_moe).astype(LOW)
    rows_all = lax.all_gather(moe_low, "shard", axis=0)

    share = replicas == 4
    acts = [expert_acts(ids, [rows_all], [cots], w_gate, w_up, w_down, w_router)]
    if share:
        far_rows, far_cots = (foreign(rows_all), foreign(cots))
    _, _, gated, grad_gate_act, grad_up_act, dgates = acts[0]
    router_shape = (jax.ShapeDtypeStruct(w_router.shape, WIDE),)
    pull_part, grad_router = spread_call(
        pull_kernel, "expert_pull", ids, (rows_all,), cots,
        (grad_gate_act, grad_up_act, dgates), (w_gate, w_up, w_router), router_shape,
    )
    grad_moe_in = scatter_sum(pull_part)
    gated, pull_part = after((gated, pull_part))
    (mix_part,) = spread_call(mix_kernel, "expert_mix", ids, (), cots, (gated,), (w_down,), ())
    if share:
        near, far_cots[0:2], mix_part = after((far_rows[0:2], far_cots[0:2], mix_part))
        acts.append(expert_acts(ids, near, far_cots[0:2], w_gate, w_up, w_down, w_router))
        grad_moe_in, acts = after((grad_moe_in, acts))

    grad_out = cot_low.astype(WIDE)
    grad_hidden = grad_out + rms_back(plain_mid, scale_mid, gain_moe, grad_moe_in)
    gain_moe_sum = jnp.sum(grad_moe_in * plain_mid, axis=0)
    branch_low = grad_hidden.astype(LOW)
    upper = lax.all_gather(branch_low, "shard", axis=0)
    if share:
        rest, branch_low = after((far_rows[2:], branch_low))
        acts.append(expert_acts(ids, rest, far_cots[2:], w_gate, w_up, w_down, w_router))
        upper, acts = after((upper, acts))
    part, gw_in, gw_out, sum_q, sum_k, sum_n = attend_backward(upper, packets, kept, *heads)
    mix_part, upper = after((mix_part, upper))
    mixture = scatter_sum(mix_part)
    output = (hidden + mixture).astype(LOW)

    acts, part = after((acts, part))
    grad_normed = scatter_sum(part)
    grad_input = grad_hidden + rms_back(plain_in, scale_in, gain_attn, grad_normed)

    def replica_sum(values):
        if replicas != 4:
            return lax.psum(values.astype(LOW), "rep")
        me = lax.axis_index("rep")
        pieces = values.astype(LOW).reshape((replicas, -1) + values.shape[1:])

        def piece(place):
            return lax.dynamic_index_in_dim(pieces, place, axis=0, keepdims=False)

        total = piece(me).astype(WIDE)
        for bits in (1, 2, 3):
            total = total + flip_replica(piece(me ^ bits), bits).astype(WIDE)
        low = total.astype(LOW)
        found = jnp.stack([low] + [flip_replica(low, bits) for bits in (1, 2, 3)])
        order = me ^ jnp.arange(replicas, dtype=jnp.int32)
        return jnp.take(found, order, axis=0).reshape(values.shape)

    sum_in, sum_out = (replica_sum(gw_in).astype(WIDE), replica_sum(gw_out).astype(WIDE))
    small = jnp.concatenate(
        [sum_n[0] / gain_attn, sum_q[0], sum_k[0], gain_moe_sum, grad_router.reshape(-1)]
    )
    for axis, size, flip in (("rep", replicas, flip_replica), ("shard", groups, flip_shard)):
        if size & (size - 1):
            small = lax.psum(small, axis)
        else:
            bits = 1
            while bits < size:
                small = small + flip(small, bits)
                bits *= 2
    edges = [0, width, width + head_dim, width + 2 * head_dim, 2 * width + 2 * head_dim]
    grad_gain_attn, grad_gain_query, grad_gain_key, grad_gain_moe = (
        small[a:b] for a, b in zip(edges[:-1], edges[1:])
    )
    grad_router = small[edges[-1] :].reshape(w_router.shape)

    def sets(place):
        return [act[place] for act in acts]

    grad_gate_w = weight_grad(sets(0), sets(3))
    grad_up_w = weight_grad(sets(0), sets(4))
    grad_down = weight_grad(sets(2), sets(1))
    if not share:
        grad_gate_w, grad_up_w, grad_down = (
            lax.psum(values.astype(LOW), "rep").astype(WIDE)
            for values in (grad_gate_w, grad_up_w, grad_down)
        )
    return (
        output, grad_input, grad_gain_attn, grad_gain_query, grad_gain_key,
        sum_in[:, :wide], sum_in[:, wide : 2 * wide], sum_in[:, 2 * wide :], sum_out,
        grad_gain_moe, grad_router, grad_gate_w, grad_up_w, grad_down,
    )


def solution(mesh):
    rows, flat, cols = (P(("rep", "shard"), None), P(), P(None, "shard"))
    lead, experts = (P("shard", None), P("shard", None, None))
    return jax.shard_map(
        local,
        mesh=mesh,
        in_specs=(
            rows, P(("rep", "shard")), rows, flat, flat, flat, cols, cols, cols, lead,
            flat, flat, experts, experts, experts, rows,
        ),
        out_specs=(
            rows, rows, flat, flat, flat, cols, cols, cols, lead,
            flat, flat, experts, experts, experts,
        ),
        check_vma=False,
    )
```

time: 2260 us -> 1350 us (0.60)
  waiting for transfers between devices: 1580 us -> 729 us
  Pallas kernels: 0 us -> 489 us
  matrix products: 263 us -> 0.15 us
  local copies, waits for them, and re-layouts: 191 us -> 45.9 us
  other arithmetic: 125 us -> 44.2 us
  blocking collectives: 52.3 us -> 0 us
    all_to_all x4 -> x0, waiting for transfers between devices: 701 us -> none  [the longest x1 197 us: local(): lax.all_to_all(send_rows.reshape(expert_count, CAP, model_width), 'shard'...]
    psum x2 -> x0, waiting for transfers between devices: 564 us -> none  [the longest x1 478 us: local(): lax.psum(grad_query_w.astype(jnp.bfloat16), 'rep').astype(jnp.float32)]
    pallas_call x0 -> x10, Pallas kernels: none -> 489 us  [the longest x3 210 us: expert_acts(): pl.pallas_call(functools.partial(expert_kernel, counts, batch), grid=(own...]
    ppermute x0 -> x29, waiting for transfers between devices: none -> 387 us  [the longest x20 374 us: flip_replica(): return lax.ppermute(values, 'rep', [(i, i ^ bits) for i in range(replicas)])]
    dot_general x30 -> x1, matrix products: 263 us -> 0.15 us  [dot_nn(): lax.dot_general(a, b, (((1,), (0,)), ((), ())), preferred_element_type=WIDE)]
    all_gather x2 -> x4, waiting for transfers between devices: 150 us -> 252 us  [the longest x1 87.8 us: local(): packets = lax.all_gather(packet, 'shard', axis=0)]
    reduce_scatter x2 -> x4, waiting for transfers between devices: 169 us -> 87.5 us  [scatter_sum(): lax.psum_scatter(parts.reshape(-1, width), 'shard', scatter_dimension=0,...]
    convert_element_type x6 -> x0, local copies, waits for them, and re-layouts: 48.5 us -> none  [the longest x1 27.9 us: local(): expert_out = jnp.einsum('erf,efd->erd', joined, w_down, preferred_element...]
  transfers between devices with their start and end apart: 10 -> 37, of which waited for: 10 -> 17; matrix products, arithmetic and copies ran while one was open for 12% -> 5% of each run, Pallas kernels for 0% -> 24%
where the time goes in v1:
time: 1350 us
  waiting for transfers between devices  729 us (54%)
  Pallas kernels  489 us (36%)
  local copies, waits for them, and re-layouts  45.9 us (3%)
  other arithmetic  44.2 us (3%)
  starting transfers between devices  25.5 us (2%)
  between operations  16 us (1%)
    ppermute x20, waiting for transfers between devices, flip_replica(): return lax.ppermute(values, 'rep', [(i, i ^ bits) for i in range(replicas)])  374 us
    pallas_call x3, Pallas kernels, expert_acts(): pl.pallas_call(functools.partial(expert_kernel, counts, batch), grid=(own...  210 us
    pallas_call x3, Pallas kernels, weight_grad(): pl.pallas_call(kernel, grid=(own, right_cols // right_tile, left_cols //...  152 us
    all_gather x1, waiting for transfers between devices, local(): packets = lax.all_gather(packet, 'shard', axis=0)  87.8 us
    reduce_scatter x4, waiting for transfers between devices, scatter_sum(): lax.psum_scatter(parts.reshape(-1, width), 'shard', scatter_dimension=0,...  87.5 us
    all_gather x1, waiting for transfers between devices, local(): rows_all = lax.all_gather(moe_low, 'shard', axis=0)  82.6 us
    all_gather x1, waiting for transfers between devices, local(): cots = lax.all_gather(cot_packet, 'shard', axis=0)  81.9 us
    pallas_call x2, Pallas kernels, spread_call(): pl.pallas_call(kernel, grid=(count // batch,), in_specs=[pl.BlockSpec(mem...  62.9 us
  transfers between devices with their start and end apart: 37, of which 17 were waited for; matrix products, arithmetic and copies ran while one was open for 5% of the time, Pallas kernels for 24%

profile of v1, /device:TPU:0, one launch (start us, length us, event | category | flops | bytes accessed | tf_op | source)
XLA Modules:
  0.0 1349.6 jit_solution(8541794927681803943)
XLA Ops:
  8.0 1.5 fusion.10
  10.4 1.4 broadcast_select_fusion
  12.2 1.7 fusion.16
  15.3 87.8 %all-gather.9.cloned.1.call-done = bf16[2176,2048]{1,0:T(8,128)(2,1)} async-done(((bf16[272,2048]{1,0:T(8,128)(2,1)}), bf16[2176,2048]{1,0:T(8,128)(2,1)}) %all-gather.9.cloned.1.call-update) | async-done | bytes 8912912 | tf_op jit(solution)/shard_map/all_gather | solution.py:485
  103.1 22.4 %attend_forward.1 = (bf16[8,256,2048]{2,1,0:T(8,128)(2,1)}, f32[8,256,256]{2,1,0:T(8,128)}, f32[8,256,256]{2,1,0:T(8,128)}, bf16[8,256,256]{2,1,0:T(8,128)(2,1)}, bf16[8,256,256]{2,1,0:T(8,128)(2,1)}) custom-call(bf16[8,272,2048]{2,1,0:T(8,128)(2,1)} %bitcast.77, bf16[2048,256]{1,0:T(8,128)(2,1)} %wq.3, bf16[2048,256]{1,0:T(8,128)(2,1)} %wk.3, ...), custom_call_target="tpu_custom_call" | custom-call | flops 1048576 | bytes 65536 | tf_op jit(solution)/shard_map/attend_forward/pallas_call | solution.py:118
  126.3 87.5 %reduce-scatter.5.cloned.1.call-done = bf16[256,2048]{1,0:T(8,128)(2,1)} async-done(((bf16[2048,2048]{1,0:T(8,128)(2,1)}), bf16[256,2048]{1,0:T(8,128)(2,1)}) %reduce-scatter.5.cloned.1.call-update) | async-done | bytes 1048592 | tf_op jit(solution)/shard_map/reduce_scatter | solution.py:469
  213.8 1.7 multiply_reduce_fusion.2
  215.5 1.5 multiply_convert_fusion
  218.9 81.9 %all-gather.13.cloned.1.call-done = bf16[2176,2048]{1,0:T(8,128)(2,1)} async-done(((bf16[272,2048]{1,0:T(8,128)(2,1)}), bf16[2176,2048]{1,0:T(8,128)(2,1)}) %all-gather.13.cloned.1.call-update) | async-done | bytes 8912912 | tf_op jit(solution)/shard_map/all_gather | solution.py:489
  300.8 82.6 %all-gather.11.cloned.1.call-done = bf16[2048,2048]{1,0:T(8,128)(2,1)} async-done(((bf16[256,2048]{1,0:T(8,128)(2,1)}), bf16[2048,2048]{1,0:T(8,128)(2,1)}) %all-gather.11.cloned.1.call-update) | async-done | bytes 8388624 | tf_op jit(solution)/shard_map/all_gather | solution.py:496
  383.4 56.7 %expert_acts.3 = (bf16[2,1152,2048]{2,1,0:T(8,128)(2,1)}, bf16[2,1152,2048]{2,1,0:T(8,128)(2,1)}, bf16[2,1152,1024]{2,1,0:T(8,128)(2,1)}, bf16[2,1152,1024]{2,1,...) custom-call(s32[2]{0:T(128)} %iota_add_fusion.ex_ref, bf16[2,2048,1024]{2,1,0:T(8,128)(2,1)} %wg.7, ...), custom_call_target="tpu_custom_call" | custom-call | flops 1048576 | bytes 65536 | tf_op jit(solution)/shard_map/expert_acts/pallas_call | solution.py:303
  440.1 42.3 %expert_pull.1 = (bf16[8,256,2048]{2,1,0:T(8,128)(2,1)}, f32[2048,16]{1,0:T(8,128)}) custom-call(s32[2]{0:T(128)} %iota_add_fusion.ex_ref, bf16[8,256,2048]{2,1,0:T(8,128)(2,1)} %bitcast.75, bf16[8,272,2048]{2,1,0:T(8,128)(2,1)} %bitcast.71, bf16[2,1152,1024]{2,1,0:T(8,128)(2,1)} %get-tuple-element.172.dg_ref.refs_3_, ...), custom_call_target="tpu_custom_call" | custom-call | flops 1048576 | bytes 65536 | tf_op jit(solution)/shard_map/expert_pull/pallas_call | solution.py:384
  482.5 5.2 dynamic-slice_bitcast_fusion
  487.6 1.4 collective-permute-start.2
  489.0 1.5 collective-permute-start.3
  490.5 4.8 dynamic-slice_bitcast_fusion.1
  496.4 20.6 %expert_mix.1 = bf16[8,256,2048]{2,1,0:T(8,128)(2,1)} custom-call(s32[2]{0:T(128)} %iota_add_fusion.ex_ref, bf16[8,272,2048]{2,1,0:T(8,128)(2,1)} %bitcast.73, bf16[2,1152,1024]{2,1,0:T(8,128)(2,1)} %get-tuple-element.178.m_ref.refs_0_, bf16[2,1024,2048]{2,1,0:T(8,128)(2,1)} %wd.7), custom_call_target="tpu_custom_call" | custom-call | flops 1048576 | bytes 65536 | tf_op jit(solution)/shard_map/expert_mix/pallas_call | solution.py:384
  517.0 69.9 %collective-permute-done.2.refs_2_ = bf16[4,272,2048]{2,1,0:T(8,128)(2,1)} collective-permute-done((bf16[4,272,2048]{2,1,0:T(8,128)(2,1)}, bf16[4,272,2048]{2,1,0:T(8,128)(2,1)}, u32[]{:S(2)}, u32[]{:S(2)}) %collective-permute-start.2) | collective-permute-done | bytes 4456480 | tf_op jit(solution)/shard_map/ppermute | solution.py:454
  587.0 1.4 collective-permute-done.3.refs_3_
  588.4 87.8 %collective-permute-done.refs_0_ = bf16[4,256,2048]{2,1,0:T(8,128)(2,1)} collective-permute-done((bf16[4,256,2048]{2,1,0:T(8,128)(2,1)}, bf16[4,256,2048]{2,1,0:T(8,128)(2,1)}, u32[]{:S(2)}, u32[]{:S(2)}) %collective-permute-start) | collective-permute-done | bytes 4194336 | tf_op jit(solution)/shard_map/ppermute | solution.py:454
  677.3 56.9 %expert_acts.4 = (bf16[2,1152,2048]{2,1,0:T(8,128)(2,1)}, bf16[2,1152,2048]{2,1,0:T(8,128)(2,1)}, bf16[2,1152,1024]{2,1,0:T(8,128)(2,1)}, bf16[2,1152,1024]{2,1,...) custom-call(s32[2]{0:T(128)} %iota_add_fusion.ex_ref, bf16[2,2048,1024]{2,1,0:T(8,128)(2,1)} %wg.7, ...), custom_call_target="tpu_custom_call" | custom-call | flops 1048576 | bytes 65536 | tf_op jit(solution)/shard_map/expert_acts/pallas_call | solution.py:303
  734.2 1.5 convert_element_type.95
  737.1 1.9 fusion.27
  739.1 1.5 collective-permute-start.8
  740.6 1.5 collective-permute-start.4
  742.6 96.8 %collective-permute-done.8.refs_4_ = bf16[4,272,2048]{2,1,0:T(8,128)(2,1)S(1)} collective-permute-done((bf16[4,272,2048]{2,1,0:T(8,128)(2,1)}, bf16[4,272,2048]{2,1,0:T(8,128)(2,1)S(1)}, u32[]{:S(2)}, u32[]{:S(2)}) %collective-permute-start.8) | collective-permute-done | bytes 4456480 | tf_op jit(solution)/shard_map/ppermute | solution.py:454
  839.4 2.1 copy-done.5
  842.0 85.3 %collective-permute-done.4.refs_0_ = bf16[4,256,2048]{2,1,0:T(8,128)(2,1)S(1)} collective-permute-done((bf16[4,256,2048]{2,1,0:T(8,128)(2,1)}, bf16[4,256,2048]{2,1,0:T(8,128)(2,1)S(1)}, u32[]{:S(2)}, u32[]{:S(2)}) %collective-permute-start.4) | collective-permute-done | bytes 4194336 | tf_op jit(solution)/shard_map/ppermute | solution.py:454
  927.9 12.0 collective-permute-done.6.refs_2_
  941.8 1.3 copy-done.11
  944.5 2.1 copy-done.7
  946.6 96.1 %expert_acts.5 = (bf16[2,2304,2048]{2,1,0:T(8,128)(2,1)}, bf16[2,2304,2048]{2,1,0:T(8,128)(2,1)}, bf16[2,2304,1024]{2,1,0:T(8,128)(2,1)}, bf16[2,2304,1024]{2,1,...) custom-call(s32[2]{0:T(128)} %iota_add_fusion.ex_ref, bf16[2,2048,1024]{2,1,0:T(8,128)(2,1)} %wg.7, ...), custom_call_target="tpu_custom_call" | custom-call | flops 1048576 | bytes 65536 | tf_op jit(solution)/shard_map/expert_acts/pallas_call | solution.py:303
  1042.7 42.4 %attend_backward.1 = (bf16[8,256,2048]{2,1,0:T(8,128)(2,1)}, f32[2048,768]{1,0:T(8,128)}, f32[256,2048]{1,0:T(8,128)}, f32[1,128]{1,0:T(1,128)}, f32[1,128]{1,0:T(1,128)}, /*index=5*/f32[1,2048]{1,0:T(1,128)}) custom-call(bf16[8,256,2048]{2,1,0:T(8,128)(2,1)} %bitcast.85, bf16[8,272,2048]{2,1,0:T(8,128)(2,1)} %bitcast.78, ...), custom_call_target="tpu_custom_call" | custom-call | flops 1048576 | bytes 65536 | tf_op jit(solution)/shard_map/attend_backward/pallas_call | solution.py:193
  1085.9 1.5 reshape.146
  1087.5 2.0 convert_element_type.108
  1091.8 1.5 collective-permute-start.24
  1093.3 1.6 collective-permute-start.25
  1099.4 1.6 constant_dynamic-update-slice_fusion
  1101.4 3.2 convert_element_type.100
  1104.6 4.2 collective-permute-done.12
  1109.8 1.4 collective-permute-start.13
  1111.9 1.3 fusion.21
  1115.1 1.6 dynamic-slice_bitcast_fusion.4
  1117.4 1.5 collective-permute-start.18
  1118.8 1.4 collective-permute-start.19
  1120.3 1.4 collective-permute-start.27
  1123.4 50.5 %weight_grad.4 = f32[2,2048,1024]{2,1,0:T(8,128)} custom-call(bf16[2,1152,2048]{2,1,0:T(8,128)(2,1)} %get-tuple-element.169.refs_0_, bf16[2,1152,2048]{2,1,0:T(8,128)(2,1)} %get-tuple-element.170.refs_1_, bf16[2,2304,2048]{2,1,0:T(8,128)(2,1)} %get-tuple-element.171.refs_2_, bf16[2,1152,1024]{2,1,0:T(8,128)(2,1)} %get-tuple-element.175.du_ref.refs_3_, ...), custom_call_target="tpu_custom_call" | custom-call | flops 1048576 | bytes 65536 | tf_op jit(solution)/shard_map/weight_grad/pallas_call | solution.py:409
  1173.9 50.2 %weight_grad.3 = f32[2,2048,1024]{2,1,0:T(8,128)} custom-call(bf16[2,1152,2048]{2,1,0:T(8,128)(2,1)} %get-tuple-element.169.refs_0_, bf16[2,1152,2048]{2,1,0:T(8,128)(2,1)} %get-tuple-element.170.refs_1_, bf16[2,2304,2048]{2,1,0:T(8,128)(2,1)} %get-tuple-element.171.refs_2_, bf16[2,1152,1024]{2,1,0:T(8,128)(2,1)} %get-tuple-element.172.dg_ref.refs_3_, ...), custom_call_target="tpu_custom_call" | custom-call | flops 1048576 | bytes 65536 | tf_op jit(solution)/shard_map/weight_grad/pallas_call | solution.py:409
  1224.2 51.2 %weight_grad.5 = f32[2,1024,2048]{2,1,0:T(8,128)} custom-call(bf16[2,1152,1024]{2,1,0:T(8,128)(2,1)} %get-tuple-element.178.m_ref.refs_0_, bf16[2,1152,1024]{2,1,0:T(8,128)(2,1)} %get-tuple-element.179.refs_1_, bf16[2,2304,1024]{2,1,0:T(8,128)(2,1)} %get-tuple-element.180.refs_2_, bf16[2,1152,2048]{2,1,0:T(8,128)(2,1)} %get-tuple-element.181.refs_3_, ...), custom_call_target="tpu_custom_call" | custom-call | flops 1048576 | bytes 65536 | tf_op jit(solution)/shard_map/weight_grad/pallas_call | solution.py:409
  1276.1 2.1 pad_maximum_fusion.1
  1278.3 2.8 gather_fusion.1
  1283.7 3.1 fusion.14
  1286.8 1.4 collective-permute-start.20
  1288.1 1.4 collective-permute-start.21
  1290.3 1.6 fusion.18
  1293.2 2.2 copy.51
  1296.5 11.1 collective-permute-done.20
  1307.6 15.4 %collective-permute-done.21 = bf16[512,768]{1,0:T(8,128)(2,1)} collective-permute-done((bf16[512,768]{1,0:T(8,128)(2,1)}, bf16[512,768]{1,0:T(8,128)(2,1)}, u32[]{:S(2)}, u32[]{:S(2)}) %collective-permute-start.21) | collective-permute-done | bytes 786464 | tf_op jit(solution)/shard_map/ppermute | solution.py:454
  1322.9 3.5 pad_maximum_fusion
  1326.4 4.3 gather_fusion
  1330.7 2.2 fusion
  1332.9 2.8 fusion.28
  1335.8 1.8 fusion.6
  1337.7 4.6 fusion.9
  (161 shorter events, 34.3 us)
Async XLA Ops:
  7.2 4.6 copy-start
  7.2 4.6 copy-start.22
  7.2 95.9 %all-gather.9.cloned.1.call-start = ((), (), s32[]{:S(2)}) async-start(), calls=%async_computation.8 | async-start | bytes 10027008 | tf_op jit(solution)/shard_map/all_gather | solution.py:485
  8.0 729.1 %copy-start.32 = (pred[256]{0:T(512)(128)(4,1)}, pred[256]{0:T(512)(128)(4,1)S(1)}, u32[]{:S(2)}) copy-start(pred[256]{0:T(512)(128)(4,1)S(1)} %iota_compare_fusion.4) | copy-start | bytes 772
  9.5 2.6 copy-start.27
  13.9 199.9 %reduce-scatter.5.cloned.1.call-start = ((), (), s32[]{:S(2)}) async-start(), calls=%async_computation.4 | async-start | bytes 9437184 | tf_op jit(solution)/shard_map/reduce_scatter | solution.py:469
  125.5 90.0 %copy-start.21 = (f32[2048]{0:T(1024)S(1)}, f32[2048]{0:T(1024)}, u32[]{:S(2)}) copy-start(f32[2048]{0:T(1024)} %param.26) | copy-start | bytes 24580
  125.5 175.2 %all-gather.13.cloned.1.call-start = ((), (), s32[]{:S(2)}) async-start(), calls=%async_computation.10 | async-start | bytes 10027008 | tf_op jit(solution)/shard_map/all_gather | solution.py:489
  126.3 257.1 %all-gather.11.cloned.1.call-start = ((), (), s32[]{:S(2)}) async-start(), calls=%async_computation.9 | async-start | bytes 9437184 | tf_op jit(solution)/shard_map/all_gather | solution.py:496
  215.5 521.6 %copy-start.25 = (f32[256]{0:T(256)}, f32[256]{0:T(256)S(1)}, u32[]{:S(2)}) copy-start(f32[256]{0:T(256)S(1)} %add_rsqrt_fusion) | copy-start | bytes 3076
  217.1 517.1 %reduce-scatter.7.cloned.1.call-start = ((), (), s32[]{:S(2)}) async-start(), calls=%async_computation.5 | async-start | bytes 9437184 | tf_op jit(solution)/shard_map/reduce_scatter | solution.py:469
  482.4 560.3 %all-gather.15.cloned.1.call-start = ((), (), s32[]{:S(2)}) async-start(), calls=%async_computation.11 | async-start | bytes 9437184 | tf_op jit(solution)/shard_map/all_gather | solution.py:520
  487.6 99.3 %collective-permute-start.2 = (bf16[4,272,2048]{2,1,0:T(8,128)(2,1)}, bf16[4,272,2048]{2,1,0:T(8,128)(2,1)}, u32[]{:S(2)}, u32[]{:S(2)}) collective-permute-start(bf16[4,272,2048]{2,1,0:T(8,128)(2,1)} %dynamic-slice_bitcast_fusion), channel_id=1, source_target_pairs={{0,8},{8,0},{16,24},{24,16},{1,9},{9,1},{17,25},{25,17},{2,10},{10... | collective-permute-start | bytes 13369352 | tf_op jit(solution)/shard_map/ppermute | solution.py:454
  489.0 99.4 %collective-permute-start.3 = (bf16[4,272,2048]{2,1,0:T(8,128)(2,1)}, bf16[4,272,2048]{2,1,0:T(8,128)(2,1)}, u32[]{:S(2)}, u32[]{:S(2)}) collective-permute-start(bf16[4,272,2048]{2,1,0:T(8,128)(2,1)} %dynamic-slice_bitcast_fusion), channel_id=1, source_target_pairs={{0,16},{8,24},{16,0},{24,8},{1,17},{9,25},{17,1},{25,9},{2,18},{10... | collective-permute-start | bytes 13369352 | tf_op jit(solution)/shard_map/ppermute | solution.py:454
  495.2 180.9 %collective-permute-start = (bf16[4,256,2048]{2,1,0:T(8,128)(2,1)}, bf16[4,256,2048]{2,1,0:T(8,128)(2,1)}, u32[]{:S(2)}, u32[]{:S(2)}) collective-permute-start(bf16[4,256,2048]{2,1,0:T(8,128)(2,1)} %dynamic-slice_bitcast_fusion.1), channel_id=1, source_target_pairs={{0,8},{8,0},{16,24},{24,16},{1,9},{9,1},{17,25},{25,17},{2,10},{10... | collective-permute-start | bytes 12582920 | tf_op jit(solution)/shard_map/ppermute | solution.py:454
  495.8 181.5 %collective-permute-start.1 = (bf16[4,256,2048]{2,1,0:T(8,128)(2,1)}, bf16[4,256,2048]{2,1,0:T(8,128)(2,1)}, u32[]{:S(2)}, u32[]{:S(2)}) collective-permute-start(bf16[4,256,2048]{2,1,0:T(8,128)(2,1)} %dynamic-slice_bitcast_fusion.1), channel_id=1, source_target_pairs={{0,16},{8,24},{16,0},{24,8},{1,17},{9,25},{17,1},{25,9},{2,18},{10... | collective-permute-start | bytes 12582920 | tf_op jit(solution)/shard_map/ppermute | solution.py:454
  737.1 1.9 copy-start.29
  739.0 596.8 %reduce-scatter.11.cloned.1.call-start = ((), (), s32[]{:S(2)}) async-start(), calls=%async_computation.7 | async-start | bytes 9437184 | tf_op jit(solution)/shard_map/reduce_scatter | solution.py:469
  739.1 100.3 %collective-permute-start.8 = (bf16[4,272,2048]{2,1,0:T(8,128)(2,1)}, bf16[4,272,2048]{2,1,0:T(8,128)(2,1)S(1)}, u32[]{:S(2)}, u32[]{:S(2)}) collective-permute-start(bf16[4,272,2048]{2,1,0:T(8,128)(2,1)} %dynamic-slice_bitcast_fusion), channel_id=1, source_target_pairs={{0,24},{8,16},{16,8},{24,0},{1,25},{9,17},{17,9},{25,1},{2,26},{10... | collective-permute-start | bytes 13369352 | tf_op jit(solution)/shard_map/ppermute | solution.py:454
  740.6 186.7 %collective-permute-start.4 = (bf16[4,256,2048]{2,1,0:T(8,128)(2,1)}, bf16[4,256,2048]{2,1,0:T(8,128)(2,1)S(1)}, u32[]{:S(2)}, u32[]{:S(2)}) collective-permute-start(bf16[4,256,2048]{2,1,0:T(8,128)(2,1)} %dynamic-slice_bitcast_fusion.1), channel_id=1, source_target_pairs={{0,24},{8,16},{16,8},{24,0},{1,25},{9,17},{17,9},{25,1},{2,26},{10... | collective-permute-start | bytes 12582920 | tf_op jit(solution)/shard_map/ppermute | solution.py:454
  742.1 185.3 %collective-permute-start.5 = (bf16[4,256,2048]{2,1,0:T(8,128)(2,1)}, bf16[4,256,2048]{2,1,0:T(8,128)(2,1)S(1)}, u32[]{:S(2)}, u32[]{:S(2)}) collective-permute-start(bf16[4,256,2048]{2,1,0:T(8,128)(2,1)} %collective-permute-done.refs_0_), channel_id=1, source_target_pairs={{0,1},{1,0},{2,3},{3,2},{4,5},{5,4},{6,7},{7,6},{8,9},{9,8},{10,11... | collective-permute-start | bytes 12582920 | tf_op jit(solution)/shard_map/ppermute | solution.py:457
  742.1 198.4 %collective-permute-start.10 = (bf16[4,272,2048]{2,1,0:T(8,128)(2,1)}, bf16[4,272,2048]{2,1,0:T(8,128)(2,1)S(1)}, u32[]{:S(2)}, u32[]{:S(2)}) collective-permute-start(bf16[4,272,2048]{2,1,0:T(8,128)(2,1)} %collective-permute-done.3.refs_3_), channel_id=1, source_target_pairs={{0,1},{1,0},{2,3},{3,2},{4,5},{5,4},{6,7},{7,6},{8,9},{9,8},{10,11... | collective-permute-start | bytes 13369352 | tf_op jit(solution)/shard_map/ppermute | solution.py:457
  839.4 2.1 copy-start.5
  841.5 99.0 %collective-permute-start.11 = (bf16[4,272,2048]{2,1,0:T(8,128)(2,1)S(1)}, bf16[4,272,2048]{2,1,0:T(8,128)(2,1)S(1)}, u32[]{:S(2)}, u32[]{:S(2)}) collective-permute-start(bf16[4,272,2048]{2,1,0:T(8,128)(2,1)S(1)} %collective-permute-done.8.refs_4_), channel_id=1, source_target_pairs={{0,1},{1,0},{2,3},{3,2},{4,5},{5,4},{6,7},{7,6},{8,9},{9,8},{10,11... | collective-permute-start | bytes 13369352 | tf_op jit(solution)/shard_map/ppermute | solution.py:457
  841.5 105.1 %collective-permute-start.9 = (bf16[4,272,2048]{2,1,0:T(8,128)(2,1)}, bf16[4,272,2048]{2,1,0:T(8,128)(2,1)}, u32[]{:S(2)}, u32[]{:S(2)}) collective-permute-start(bf16[4,272,2048]{2,1,0:T(8,128)(2,1)} %collective-permute-done.2.refs_2_), channel_id=1, source_target_pairs={{0,1},{1,0},{2,3},{3,2},{4,5},{5,4},{6,7},{7,6},{8,9},{9,8},{10,11... | collective-permute-start | bytes 13369352 | tf_op jit(solution)/shard_map/ppermute | solution.py:457
  927.3 13.2 copy-start.8
  927.3 12.5 collective-permute-start.6
  927.4 13.2 copy-start.9
  927.4 13.1 collective-permute-start.7
  939.9 2.0 copy-start.10
  940.5 2.7 copy-start.11
  940.5 4.0 copy-start.6
  944.5 2.1 copy-start.7
  1085.2 252.5 %reduce-scatter.9.cloned.1.call-start = ((), (), s32[]{:S(2)}) async-start(), calls=%async_computation.6 | async-start | bytes 9437184 | tf_op jit(solution)/shard_map/reduce_scatter | solution.py:469
  1087.5 7.4 copy-start.31
  1087.5 8.0 copy-start.35
  1087.5 9.3 copy-start.34
  1087.5 10.6 copy-start.24
  1091.4 19.9 %collective-permute-start.23 = (bf16[64,2048]{1,0:T(8,128)(2,1)}, bf16[64,2048]{1,0:T(8,128)(2,1)S(1)}, u32[]{:S(2)}, u32[]{:S(2)}) collective-permute-start(bf16[64,2048]{1,0:T(8,128)(2,1)} %get-tuple-element.222), channel_id=1, source_target_pairs={{0,8},{8,0},{16,24},{24,16},{1,9},{9,1},{17,25},{25,17},{2,10},{10... | collective-permute-start | bytes 786440 | tf_op jit(solution)/shard_map/ppermute | solution.py:454
  1091.8 19.4 %collective-permute-start.24 = (bf16[64,2048]{1,0:T(8,128)(2,1)}, bf16[64,2048]{1,0:T(8,128)(2,1)}, u32[]{:S(2)}, u32[]{:S(2)}) collective-permute-start(bf16[64,2048]{1,0:T(8,128)(2,1)} %get-tuple-element.224), channel_id=1, source_target_pairs={{0,16},{8,24},{16,0},{24,8},{1,17},{9,25},{17,1},{25,9},{2,18},{10... | collective-permute-start | bytes 786440 | tf_op jit(solution)/shard_map/ppermute | solution.py:454
  1093.3 18.6 %collective-permute-start.25 = (bf16[64,2048]{1,0:T(8,128)(2,1)}, bf16[64,2048]{1,0:T(8,128)(2,1)}, u32[]{:S(2)}, u32[]{:S(2)}) collective-permute-start(bf16[64,2048]{1,0:T(8,128)(2,1)} %get-tuple-element.223), channel_id=1, source_target_pairs={{0,24},{8,16},{16,8},{24,0},{1,25},{9,17},{17,9},{25,1},{2,26},{10... | collective-permute-start | bytes 786440 | tf_op jit(solution)/shard_map/ppermute | solution.py:454
  1101.0 7.8 collective-permute-start.12
  1104.6 12.1 copy-start.3
  1109.8 5.3 collective-permute-start.13
  1113.3 8.4 collective-permute-start.26
  1115.1 5.2 collective-permute-start.14
  1116.7 166.9 %collective-permute-start.17 = (bf16[512,768]{1,0:T(8,128)(2,1)}, bf16[512,768]{1,0:T(8,128)(2,1)}, u32[]{:S(2)}, u32[]{:S(2)}) collective-permute-start(bf16[512,768]{1,0:T(8,128)(2,1)} %get-tuple-element.217), channel_id=1, source_target_pairs={{0,8},{8,0},{16,24},{24,16},{1,9},{9,1},{17,25},{25,17},{2,10},{10... | collective-permute-start | bytes 2359304 | tf_op jit(solution)/shard_map/ppermute | solution.py:454
  1117.4 166.3 %collective-permute-start.18 = (bf16[512,768]{1,0:T(8,128)(2,1)}, bf16[512,768]{1,0:T(8,128)(2,1)}, u32[]{:S(2)}, u32[]{:S(2)}) collective-permute-start(bf16[512,768]{1,0:T(8,128)(2,1)} %get-tuple-element.219), channel_id=1, source_target_pairs={{0,16},{8,24},{16,0},{24,8},{1,17},{9,25},{17,1},{25,9},{2,18},{10... | collective-permute-start | bytes 2359304 | tf_op jit(solution)/shard_map/ppermute | solution.py:454
  1118.8 164.8 %collective-permute-start.19 = (bf16[512,768]{1,0:T(8,128)(2,1)}, bf16[512,768]{1,0:T(8,128)(2,1)}, u32[]{:S(2)}, u32[]{:S(2)}) collective-permute-start(bf16[512,768]{1,0:T(8,128)(2,1)} %get-tuple-element.218), channel_id=1, source_target_pairs={{0,24},{8,16},{16,8},{24,0},{1,25},{9,17},{17,9},{25,1},{2,26},{10... | collective-permute-start | bytes 2359304 | tf_op jit(solution)/shard_map/ppermute | solution.py:454
  1120.2 2.9 copy-start.19
  1120.3 155.8 %collective-permute-start.27 = (bf16[64,2048]{1,0:T(8,128)(2,1)S(1)}, bf16[64,2048]{1,0:T(8,128)(2,1)}, u32[]{:S(2)}, u32[]{:S(2)}) collective-permute-start(bf16[64,2048]{1,0:T(8,128)(2,1)S(1)} %fusion.21), channel_id=1, source_target_pairs={{0,16},{8,24},{16,0},{24,8},{1,17},{9,25},{17,1},{25,9},{2,18},{10... | collective-permute-start | bytes 786440 | tf_op jit(solution)/shard_map/ppermute | solution.py:454
  1122.4 153.7 %collective-permute-start.28 = (bf16[64,2048]{1,0:T(8,128)(2,1)S(1)}, bf16[64,2048]{1,0:T(8,128)(2,1)}, u32[]{:S(2)}, u32[]{:S(2)}) collective-permute-start(bf16[64,2048]{1,0:T(8,128)(2,1)S(1)} %fusion.21), channel_id=1, source_target_pairs={{0,24},{8,16},{16,8},{24,0},{1,25},{9,17},{17,9},{25,1},{2,26},{10... | collective-permute-start | bytes 786440 | tf_op jit(solution)/shard_map/ppermute | solution.py:454
  1224.1 51.3 %copy-start.15 = (f32[37120]{0:T(1024)S(1)}, f32[37120]{0:T(1024)}, u32[]{:S(2)}) copy-start(f32[37120]{0:T(1024)} %copy-done.14) | copy-start | bytes 445444
  1224.1 51.3 %copy-start.20 = (f32[37120]{0:T(1024)S(1)}, f32[37120]{0:T(1024)}, u32[]{:S(2)}) copy-start(f32[37120]{0:T(1024)} %copy-done.19) | copy-start | bytes 445444
  1224.2 52.0 %copy-start.18 = (bf16[64,2048]{1,0:T(8,128)(2,1)S(1)}, bf16[64,2048]{1,0:T(8,128)(2,1)}, u32[]{:S(2)}) copy-start(bf16[64,2048]{1,0:T(8,128)(2,1)} %copy-done.17) | copy-start | bytes 786436
  1276.1 5.5 collective-permute-start.15
  1281.1 9.2 copy-start.13
  1282.6 9.2 collective-permute-start.16
  1286.8 20.8 %collective-permute-start.20 = (bf16[512,768]{1,0:T(8,128)(2,1)}, bf16[512,768]{1,0:T(8,128)(2,1)}, u32[]{:S(2)}, u32[]{:S(2)}) collective-permute-start(bf16[512,768]{1,0:T(8,128)(2,1)} %fusion.14), channel_id=1, source_target_pairs={{0,8},{8,0},{16,24},{24,16},{1,9},{9,1},{17,25},{25,17},{2,10},{10... | collective-permute-start | bytes 2359304 | tf_op jit(solution)/shard_map/ppermute | solution.py:454
  1288.1 34.8 %collective-permute-start.21 = (bf16[512,768]{1,0:T(8,128)(2,1)}, bf16[512,768]{1,0:T(8,128)(2,1)}, u32[]{:S(2)}, u32[]{:S(2)}) collective-permute-start(bf16[512,768]{1,0:T(8,128)(2,1)} %fusion.14), channel_id=1, source_target_pairs={{0,16},{8,24},{16,0},{24,8},{1,17},{9,25},{17,1},{25,9},{2,18},{10... | collective-permute-start | bytes 2359304 | tf_op jit(solution)/shard_map/ppermute | solution.py:454
  1289.6 33.3 %collective-permute-start.22 = (bf16[512,768]{1,0:T(8,128)(2,1)}, bf16[512,768]{1,0:T(8,128)(2,1)}, u32[]{:S(2)}, u32[]{:S(2)}) collective-permute-start(bf16[512,768]{1,0:T(8,128)(2,1)} %fusion.14), channel_id=1, source_target_pairs={{0,24},{8,16},{16,8},{24,0},{1,25},{9,17},{17,9},{25,1},{2,26},{10... | collective-permute-start | bytes 2359304 | tf_op jit(solution)/shard_map/ppermute | solution.py:454
  1332.9 2.9 copy-start.28
  1335.8 1.9 copy-start.30
  1335.8 1.9 copy-start.33
  (9 other events, 12.4 us)
Sparse Core Ops, SparseCore 0:
  14.0 89.0 all-gather.8
  125.6 88.0 reduce-scatter.4
  216.0 84.7 all-gather.12
  302.8 80.5 all-gather.10
  482.5 88.1 reduce-scatter.6
  739.2 79.6 all-gather.14
  1085.3 87.2 reduce-scatter.10
  1174.9 87.9 reduce-scatter.8

commit v2 on v1

--- a/solution.py
+++ b/solution.py
@@ -210,33 +210,39 @@
     return (slots == ranks).astype(LOW)
 
 
-def expert_kernel(counts, batch, ex_ref, wg, wu, wd, wr, *refs):
-    sources = len(counts)
-    rows_in, cots_in = (refs[:sources], refs[sources : 2 * sources])
-    x_ref, y_ref, m_ref, dg_ref, du_ref, dgate_ref, rows_buf, cots_buf, sems = refs[2 * sources :]
-    steps = sum(counts) // batch
+UNIT = 2
+
+
+def expert_kernel(row_counts, cot_counts, batch, ex_ref, wg, wu, wd, wr, *refs):
+    first, second = (len(row_counts), len(row_counts) + len(cot_counts))
+    rows_in, cots_in = (refs[:first], refs[first:second])
+    x_ref, y_ref, m_ref, dg_ref, du_ref, dgate_ref, rows_buf, cots_buf, sems = refs[second:]
+    steps, units = (sum(row_counts) // batch, batch // UNIT)
     turn = pl.program_id(0) * steps + pl.program_id(1)
     slot = lax.rem(turn, 2)
     row_count = rows_buf.shape[2]
 
-    def copies(source, offset, place):
-        span = pl.ds(offset, batch)
-        return (
-            pltpu.make_async_copy(rows_in[source].at[span], rows_buf.at[place], sems.at[0, place]),
-            pltpu.make_async_copy(cots_in[source].at[span], cots_buf.at[place], sems.at[1, place]),
+    def copy(kind, source, offset, place, part):
+        buffer = (rows_buf, cots_buf)[kind]
+        return pltpu.make_async_copy(
+            source.at[pl.ds(offset, UNIT)],
+            buffer.at[place, pl.ds(part * UNIT, UNIT)],
+            sems.at[kind, place, part],
         )
 
     def fetch(step, place):
-        begin = 0
-        for source, count in enumerate(counts):
-            size = count // batch
-
-            @pl.when((step >= begin) & (step < begin + size))
-            def _(source=source, begin=begin):
-                for copy in copies(source, (step - begin) * batch, place):
-                    copy.start()
-
-            begin += size
+        for part in range(units):
+            unit = step * units + part
+            for kind, sources, counts in ((0, rows_in, row_counts), (1, cots_in, cot_counts)):
+                begin = 0
+                for source, count in zip(sources, counts):
+                    size = count // UNIT
+
+                    @pl.when((unit >= begin) & (unit < begin + size))
+                    def _(source=source, begin=begin):
+                        copy(kind, source, (unit - begin) * UNIT, place, part).start()
+
+                    begin += size
 
     @pl.when(turn == 0)
     def _():
@@ -246,8 +252,9 @@
     def _():
         fetch(lax.rem(turn + 1, steps), 1 - slot)
 
-    for copy in copies(0, 0, slot):
-        copy.wait()
+    for part in range(units):
+        copy(0, rows_in[0], 0, slot, part).wait()
+        copy(1, cots_in[0], 0, slot, part).wait()
     hidden = wg.shape[-1]
     expert = ex_ref[pl.program_id(0)]
     for seq in range(batch):
@@ -282,8 +289,8 @@
 
 def expert_acts(ids, rows, cots, wg, wu, wd, wr, batch=4):
     row_count, width = rows[0].shape[1:]
-    counts = tuple(array.shape[0] for array in rows)
-    count = sum(counts)
+    row_counts, cot_counts = ([array.shape[0] for array in arrays] for arrays in (rows, cots))
+    count = sum(row_counts)
     own, _, hidden = wg.shape
     out_rows = batch * CAP
 
@@ -301,7 +308,7 @@
     any_spec = pl.BlockSpec(memory_space=pl.ANY)
     columns = (width, width, hidden, hidden, hidden, 128)
     return pl.pallas_call(
-        functools.partial(expert_kernel, counts, batch),
+        functools.partial(expert_kernel, row_counts, cot_counts, batch),
         grid=(own, count // batch),
         in_specs=[
             pl.BlockSpec(memory_space=pltpu.SMEM),
@@ -310,13 +317,13 @@
             weight_spec(wd),
             pl.BlockSpec(wr.shape, lambda e, i: (0, 0)),
         ]
-        + [any_spec] * (2 * len(counts)),
+        + [any_spec] * (len(rows) + len(cots)),
         out_specs=[act_spec(cols) for cols in columns],
         out_shape=tuple(acts(cols) for cols in columns[:5]) + (acts(128, WIDE),),
         scratch_shapes=[
             pltpu.VMEM((2, batch) + rows[0].shape[1:], LOW),
             pltpu.VMEM((2, batch) + cots[0].shape[1:], LOW),
-            pltpu.SemaphoreType.DMA((2, 2)),
+            pltpu.SemaphoreType.DMA((2, 2, batch // UNIT)),
         ],
         compiler_params=pltpu.CompilerParams(vmem_limit_bytes=VMEM_BYTES),
         cost_estimate=COST,
@@ -425,6 +432,426 @@
     )(*lefts, *rights)
 
 
+CHUNKS = 4
+NEAR_LINES = 128
+
+
+def front_kernel(
+    replicas, groups,
+    packet, cot, tokens, wq, wk, wv, wo, gq, gk, cos_ref, sin_ref, gain_ref,
+    packets, qr_ref, kr_ref, v_ref, o_ref, hidden, rows_all, cots, fx, fy, fd, px, py, pd,
+    nb, mine, pair_out, pair_in, line_r, line_l, low,
+    n1_send, n1_recv, n1_pair, n2_send, n2_recv, n2_pair, cz_send, cz_recv, cz_pair,
+    xy_send, xy_recv, dg_send, dg_recv, fl_send, fl_recv,
+    po_send, po_recv, lr_send, lr_recv, ll_send, ll_recv, keep_sem, own_sem,
+):
+    rail = groups // 2
+    rep, shard = (lax.axis_index("rep"), lax.axis_index("shard"))
+    place, core = (shard // 2, shard % 2)
+    rows = tokens.shape[0]
+    step_rows = rows // CHUNKS
+    last = rail - 1
+    right, left, partner = ((rep, shard + 2), (rep, shard - 2), (rep, shard + 1 - 2 * core))
+    over_x = (rep + 1 - 2 * (rep % 2), shard)
+    over_y = ((rep + 2) % replicas, shard)
+
+    def remote(source, target, send, recv, device):
+        return pltpu.make_async_remote_copy(
+            source, target, send, recv, device_id=device, device_id_type=pl.DeviceIdType.MESH
+        )
+
+    def each(size, body):
+        def step(i, carry):
+            body(i)
+            return carry
+
+        lax.fori_loop(0, size, step, 0)
+
+    class Flood:
+        def __init__(self, view, send, recv, pair, own):
+            self.view, self.send, self.recv, self.pair, self.own = (view, send, recv, pair, own)
+
+        def copy(self, way, q, own=False):
+            slot = 2 * q + core
+            source = self.own if own else self.view.at[slot]
+            recv = self.pair.at[q] if way == 2 else self.recv.at[q]
+            device = (right, left, partner)[way]
+            return remote(source, self.view.at[slot], self.send.at[way, q], recv, device)
+
+        def start_line(self):
+            @pl.when(place < last)
+            def _():
+                self.copy(0, place, True).start()
+
+            @pl.when(place > 0)
+            def _():
+                self.copy(1, place, True).start()
+
+        def start_pair(self):
+            self.copy(2, place, True).start()
+
+        def onward(self, d, more=None):
+            @pl.when((d > 0) & (place - d >= 0))
+            def _():
+                q = place - d
+                self.copy(0, q).wait_recv()
+
+                @pl.when(place < last)
+                def _():
+                    self.copy(0, q).start()
+
+                self.copy(2, q).start()
+                if more is not None:
+                    more(q)
+
+            @pl.when((d > 0) & (place + d <= last))
+            def _():
+                q = place + d
+                self.copy(1, q).wait_recv()
+
+                @pl.when(place > 0)
+                def _():
+                    self.copy(1, q).start()
+
+                self.copy(2, q).start()
+                if more is not None:
+                    more(q)
+
+        def wait_pair(self, q):
+            slot = 2 * q + 1 - core
+            remote(
+                self.view.at[slot], self.view.at[slot], self.send.at[2, q], self.pair.at[q], partner
+            ).wait_recv()
+
+        def finish(self, pairs):
+            def body(q):
+                @pl.when((place < last) & (q <= place))
+                def _():
+                    self.copy(0, q).wait_send()
+
+                @pl.when((place > 0) & (q >= place))
+                def _():
+                    self.copy(1, q).wait_send()
+
+                self.copy(2, q).wait_send()
+                if pairs:
+                    self.wait_pair(q)
+
+            each(rail, body)
+
+    flood_n1 = Flood(nb, n1_send, n1_recv, n1_pair, packet)
+    flood_n2 = Flood(rows_all, n2_send, n2_recv, n2_pair, low)
+    flood_cot = Flood(cots, cz_send, cz_recv, cz_pair, cot)
+
+    def cross(way, q, own=False):
+        source = cot if own else cots.at[2 * q + core]
+        target, device = ((fx, over_x), (fy, over_y))[way]
+        return remote(source, target.at[q], xy_send.at[way, q], xy_recv.at[way, q], device)
+
+    def cross_both(q):
+        cross(0, q).start()
+        cross(1, q).start()
+
+    def diagonal(way, q):
+        source, device = ((fx, over_y), (fy, over_x))[way]
+        span = (pl.ds(0, NEAR_LINES), pl.ds(NEAR_LINES, cot.shape[0] - NEAR_LINES))[way]
+        return remote(
+            source.at[q, span], fd.at[q, span], dg_send.at[way, q], dg_recv.at[way, q], device
+        )
+
+    def flip(which, q):
+        source, target = ((fx, px), (fy, py), (fd, pd))[which]
+        return remote(
+            source.at[q], target.at[q], fl_send.at[which, q], fl_recv.at[which, q], partner
+        )
+
+    def at_distance(d, body):
+        if d < 0 or d > last:
+            return
+        if d == 0:
+            body(place)
+            return
+
+        @pl.when(place - d >= 0)
+        def _():
+            body(place - d)
+
+        @pl.when(place + d <= last)
+        def _():
+            body(place + d)
+
+    def take_cross(q):
+        for way in (0, 1):
+            cross(way, q).wait_recv()
+            diagonal(way, q).start()
+            flip(way, q).start()
+
+    def take_diagonal(q):
+        for way in (0, 1):
+            diagonal(way, q).wait_recv()
+        flip(2, q).start()
+
+    def event(d):
+        if 1 <= d <= last:
+            flood_cot.onward(d, cross_both)
+        at_distance(d - 1, take_cross)
+        at_distance(d - 2, take_diagonal)
+
+    barrier = pltpu.get_barrier_semaphore()
+
+    def greet(device):
+        pl.semaphore_signal(
+            barrier, inc=1, device_id=device, device_id_type=pl.DeviceIdType.MESH
+        )
+
+    for device in (partner, over_x, over_y):
+        greet(device)
+
+    @pl.when(place < last)
+    def _():
+        greet(right)
+
+    @pl.when(place > 0)
+    def _():
+        greet(left)
+
+    inner = (place > 0) & (place < last)
+
+    @pl.when(inner)
+    def _():
+        pl.semaphore_wait(barrier, 5)
+
+    @pl.when(jnp.logical_not(inner))
+    def _():
+        pl.semaphore_wait(barrier, 4)
+
+    flood_n1.start_line()
+    flood_n1.start_pair()
+    own_block = pltpu.make_async_copy(packet, nb.at[shard], own_sem.at[0])
+    own_block.start()
+    own_cot = pltpu.make_async_copy(cot, cots.at[shard], own_sem.at[1])
+    own_cot.start()
+    cross(0, place, True).start()
+    cross(1, place, True).start()
+    flood_cot.start_pair()
+    own_block.wait()
+
+    def partial_out(q):
+        return remote(
+            pair_out.at[q], pair_in.at[q], po_send.at[q], po_recv.at[q], partner
+        )
+
+    def line(q, chunk, to_right):
+        span = pl.ds(pl.multiple_of(chunk * step_rows, step_rows), step_rows)
+        target, send, recv, device = (
+            (line_r, lr_send, lr_recv, right) if to_right else (line_l, ll_send, ll_recv, left)
+        )
+        return remote(
+            mine.at[q, span], target.at[q, span], send.at[q, chunk], recv.at[q, chunk], device
+        )
+
+    def add_up(q, chunk, extras):
+        span = pl.ds(pl.multiple_of(chunk * step_rows, step_rows), step_rows)
+        total = mine[q, span].astype(WIDE) + pair_in[q, span].astype(WIDE)
+        for extra in extras:
+            total = total + extra[q, span].astype(WIDE)
+        return total
+
+    def forward_line(q, to_right, first):
+        partial_out(q).wait_recv()
+
+        def body(chunk):
+            extras = []
+            if not first:
+                line(q, chunk, to_right).wait_recv()
+                extras = [line_r if to_right else line_l]
+            span = pl.ds(pl.multiple_of(chunk * step_rows, step_rows), step_rows)
+            mine[q, span] = add_up(q, chunk, extras).astype(LOW)
+            line(q, chunk, to_right).start()
+
+        each(CHUNKS, body)
+
+    def keep_copy(slot):
+        return pltpu.make_async_copy(nb.at[slot], packets.at[slot], keep_sem.at[slot])
+
+    def one_distance(d):
+        flood_n1.onward(d)
+
+        def one_block(k):
+            side, other = (k % 2, k // 2)
+            q = place + (2 * side - 1) * d
+
+            @pl.when((q >= 0) & (q <= last) & ((d > 0) | (side == 0)))
+            def _():
+                @pl.when(other == 1)
+                def _():
+                    flood_n1.wait_pair(q)
+
+                slot = 2 * q + core + other * (1 - 2 * core)
+                keep_copy(slot).start()
+                length = nb[slot, rows:, rows : rows + 128].astype(WIDE)[0:1, 0:1]
+
+                def keep(query_raw, key_raw, value, joined):
+                    qr_ref[slot], kr_ref[slot] = (query_raw, key_raw)
+                    v_ref[slot], o_ref[slot] = (value, joined)
+
+                part = attend_block(
+                    nb[slot, :rows], length, wq, wk, wv, wo, gq[...], gk[...],
+                    cos_ref[...], sin_ref[...], keep,
+                )
+
+                @pl.when(other == 0)
+                def _():
+                    mine[q] = part
+
+                @pl.when(other == 1)
+                def _():
+                    pair_out[q] = part
+                    partial_out(q).start()
+
+        each(4, one_block)
+
+        @pl.when((place == 0) & (d > 0))
+        def _():
+            forward_line(d, True, True)
+
+        @pl.when((place == last) & (d > 0))
+        def _():
+            forward_line(last - d, False, True)
+
+    each(rail, one_distance)
+    flood_cot.start_line()
+
+    def rest_right():
+        def body(j):
+            @pl.when((place > 0) & (place + j <= last))
+            def _():
+                forward_line(place + j, True, False)
+
+        each(last, lambda i: body(i + 1))
+
+    def rest_left():
+        def body(j):
+            @pl.when((place < last) & (place - j >= 0))
+            def _():
+                forward_line(place - j, False, False)
+
+        each(last, lambda i: body(i + 1))
+
+    near_end = place < rail // 2
+    pl.when(near_end)(rest_right)
+    pl.when(jnp.logical_not(near_end))(rest_left)
+    event(1)
+    pl.when(near_end)(rest_left)
+    pl.when(jnp.logical_not(near_end))(rest_right)
+
+    partial_out(place).wait_recv()
+
+    def finish_rows(chunk):
+        @pl.when(place > 0)
+        def _():
+            line(place, chunk, True).wait_recv()
+
+        @pl.when(place < last)
+        def _():
+            line(place, chunk, False).wait_recv()
+
+        span = pl.ds(pl.multiple_of(chunk * step_rows, step_rows), step_rows)
+        total = tokens[span].astype(WIDE) + add_up(place, chunk, [])
+        from_left = jnp.where(place > 0, line_r[place, span].astype(WIDE), 0.0)
+        from_right = jnp.where(place < last, line_l[place, span].astype(WIDE), 0.0)
+        total = total + from_left + from_right
+        hidden[span] = total
+        scale = lax.rsqrt(jnp.mean(total * total, axis=-1, keepdims=True) + EPS_NORM)
+        low[span] = (total * scale * gain_ref[...]).astype(LOW)
+
+    each(CHUNKS, finish_rows)
+    flood_n2.start_line()
+    flood_n2.start_pair()
+    own_low = pltpu.make_async_copy(low, rows_all.at[shard], own_sem.at[2])
+    own_low.start()
+
+    event(2)
+    for d in range(1, rail):
+        flood_n2.onward(d)
+        event(d + 2)
+
+    flood_n1.finish(False)
+    flood_n2.finish(True)
+    flood_cot.finish(True)
+    own_cot.wait()
+    own_low.wait()
+
+    def settle(q):
+        keep_copy(2 * q).wait()
+        keep_copy(2 * q + 1).wait()
+        partial_out(q).wait_send()
+        for way in (0, 1):
+            cross(way, q).wait_send()
+            diagonal(way, q).wait_send()
+        for which in (0, 1, 2):
+            flip(which, q).wait_send()
+            flip(which, q).wait_recv()
+
+        def chunk_sends(chunk):
+            @pl.when((place < last) & (q > place))
+            def _():
+                line(q, chunk, True).wait_send()
+
+            @pl.when((place > 0) & (q < place))
+            def _():
+                line(q, chunk, False).wait_send()
+
+        each(CHUNKS, chunk_sends)
+
+    each(rail, settle)
+
+
+def front(replicas, groups, packet, cot, tokens, wq, wk, wv, wo, gq, gk, cos_tab, sin_tab, gain):
+    lines, width = packet.shape
+    rows, wide, rail = (tokens.shape[0], wq.shape[1], groups // 2)
+    any_spec, fast = (pl.BlockSpec(memory_space=pl.ANY), pl.BlockSpec(memory_space=pltpu.VMEM))
+
+    def shape(*dims, kind=LOW):
+        return jax.ShapeDtypeStruct(dims, kind)
+
+    far = [shape(rail, lines, width)] * 6
+    block = pltpu.VMEM((rail, rows, width), LOW)
+    dma = pltpu.SemaphoreType.DMA
+    return pl.pallas_call(
+        functools.partial(front_kernel, replicas, groups),
+        in_specs=[any_spec] * 2 + [fast] * 10,
+        out_specs=[any_spec] + [fast] * 5 + [any_spec] * 8,
+        out_shape=[
+            shape(groups, lines, width),
+            shape(groups, rows, wide, kind=WIDE),
+            shape(groups, rows, wide, kind=WIDE),
+            shape(groups, rows, wide),
+            shape(groups, rows, wide),
+            shape(rows, width, kind=WIDE),
+            shape(groups, rows, width),
+            shape(groups, lines, width),
+        ]
+        + far,
+        scratch_shapes=[
+            pltpu.VMEM((groups, lines, width), LOW),
+            block, block, block, block, block,
+            pltpu.VMEM((rows, width), LOW),
+        ]
+        + [dma((3, rail)), dma((rail,)), dma((rail,))] * 3
+        + [dma((2, rail))] * 4
+        + [dma((3, rail))] * 2
+        + [dma((rail,))] * 2
+        + [dma((rail, CHUNKS))] * 4
+        + [dma((groups,)), dma((3,))],
+        compiler_params=pltpu.CompilerParams(
+            vmem_limit_bytes=VMEM_BYTES, collective_id=0, has_side_effects=True
+        ),
+        cost_estimate=COST,
+        name="front",
+    )(packet, cot, tokens, wq, wk, wv, wo, gq, gk, cos_tab, sin_tab, gain)
+
+
 def rms_parts(values):
     scale = lax.rsqrt(jnp.mean(values * values, axis=-1, keepdims=True) + EPS_NORM)
     return (values * scale, scale)
@@ -456,15 +883,6 @@
     def flip_shard(values, bits):
         return lax.ppermute(values, "shard", [(i, i ^ bits) for i in range(groups)])
 
-    def own_rail(blocks):
-        pairs = blocks.reshape((groups // 2, 2) + blocks.shape[1:])
-        return lax.dynamic_index_in_dim(pairs, lax.axis_index("shard") % 2, axis=1, keepdims=False)
-
-    def foreign(blocks):
-        rail = own_rail(blocks)
-        mine = [flip_replica(rail, bits) for bits in (1, 2, 3)]
-        return mine + [flip_shard(values, 1) for values in mine]
-
     def scatter_sum(parts):
         return lax.psum_scatter(
             parts.reshape(-1, width), "shard", scatter_dimension=0, tiled=True
@@ -482,36 +900,60 @@
     )
     plain_in, scale_in = rms_parts(inputs)
     packet = jnp.concatenate([(plain_in * gain_attn).astype(LOW), lines], axis=0)
-    packets = lax.all_gather(packet, "shard", axis=0)
     cot_low = jnp.where(row_mask, out_grad, 0.0)
     cot_packet = jnp.concatenate([cot_low, lines], axis=0)
-    cot_packet, packets = after((cot_packet, packets))
-    cots = lax.all_gather(cot_packet, "shard", axis=0)
-
     heads = (w_query, w_key, w_value, w_out, gain_q, gain_k, cos_tab, sin_tab)
-    part, *kept = attend_forward(packets, *heads)
-    hidden = inputs + scatter_sum(part)
-    plain_mid, scale_mid = rms_parts(hidden)
-    moe_low = (plain_mid * gain_moe).astype(LOW)
-    rows_all = lax.all_gather(moe_low, "shard", axis=0)
-
-    share = replicas == 4
+    share = replicas == 4 and groups == 8
+    if share:
+        packets, *kept = front(
+            replicas, groups, packet, cot_packet, tokens, *heads, gain_moe.reshape(1, -1)
+        )
+        kept, (hidden, rows_all, cots), far_cots = (kept[:4], kept[4:7], kept[7:])
+        plain_mid, scale_mid = rms_parts(hidden)
+        pairs = rows_all.reshape((groups // 2, 2) + rows_all.shape[1:])
+        core = lax.axis_index("shard") % 2
+        near = [
+            lax.dynamic_index_in_dim(part, core, 1, keepdims=False) for part in (pairs[:2], pairs[2:])
+        ]
+        rows_all, near = after((rows_all, near))
+    else:
+        packets = lax.all_gather(packet, "shard", axis=0)
+        cot_packet, packets = after((cot_packet, packets))
+        cots = lax.all_gather(cot_packet, "shard", axis=0)
+        part, *kept = attend_forward(packets, *heads)
+        hidden = inputs + scatter_sum(part)
+        plain_mid, scale_mid = rms_parts(hidden)
+        rows_all = lax.all_gather((plain_mid * gain_moe).astype(LOW), "shard", axis=0)
+
     acts = [expert_acts(ids, [rows_all], [cots], w_gate, w_up, w_down, w_router)]
     if share:
-        far_rows, far_cots = (foreign(rows_all), foreign(cots))
+        over = [flip_replica(near[0], bits) for bits in (1, 2)]
+        acts, over = after((acts, over))
+        over_x, over_y = ([over[0]], [over[1]])
     _, _, gated, grad_gate_act, grad_up_act, dgates = acts[0]
     router_shape = (jax.ShapeDtypeStruct(w_router.shape, WIDE),)
     pull_part, grad_router = spread_call(
         pull_kernel, "expert_pull", ids, (rows_all,), cots,
         (grad_gate_act, grad_up_act, dgates), (w_gate, w_up, w_router), router_shape,
     )
+    if share:
+        over = [flip_replica(near[1], bits) for bits in (1, 2)]
+        pull_part, over = after((pull_part, over))
+        over_x, over_y = (over_x + [over[0]], over_y + [over[1]])
     grad_moe_in = scatter_sum(pull_part)
     gated, pull_part = after((gated, pull_part))
+    if share:
+        diagonal = [flip_replica(over_x[0], 2), flip_replica(over_y[1], 1)]
+        flipped = [flip_shard(values, 1) for values in over_x + over_y]
+        near, pull_part = after((over_x + over_y, pull_part))
+        acts.append(expert_acts(ids, near, far_cots[0:2], w_gate, w_up, w_down, w_router))
+        acts, diagonal, flipped = after((acts, diagonal, flipped))
+        gated, acts = after((gated, acts))
+        diagonal_flipped = [flip_shard(values, 1) for values in diagonal]
     (mix_part,) = spread_call(mix_kernel, "expert_mix", ids, (), cots, (gated,), (w_down,), ())
     if share:
-        near, far_cots[0:2], mix_part = after((far_rows[0:2], far_cots[0:2], mix_part))
-        acts.append(expert_acts(ids, near, far_cots[0:2], w_gate, w_up, w_down, w_router))
-        grad_moe_in, acts = after((grad_moe_in, acts))
+        mix_part, diagonal_flipped = after((mix_part, diagonal_flipped))
+        grad_moe_in, mix_part = after((grad_moe_in, mix_part))
 
     grad_out = cot_low.astype(WIDE)
     grad_hidden = grad_out + rms_back(plain_mid, scale_mid, gain_moe, grad_moe_in)
@@ -519,64 +961,81 @@
     branch_low = grad_hidden.astype(LOW)
     upper = lax.all_gather(branch_low, "shard", axis=0)
     if share:
-        rest, branch_low = after((far_rows[2:], branch_low))
-        acts.append(expert_acts(ids, rest, far_cots[2:], w_gate, w_up, w_down, w_router))
+        rest, branch_low = after((diagonal + flipped + diagonal_flipped, branch_low))
+        rest_cots = [far_cots[2], far_cots[3], far_cots[4], far_cots[5]]
+        acts.append(expert_acts(ids, rest, rest_cots, w_gate, w_up, w_down, w_router))
         upper, acts = after((upper, acts))
-    part, gw_in, gw_out, sum_q, sum_k, sum_n = attend_backward(upper, packets, kept, *heads)
     mix_part, upper = after((mix_part, upper))
     mixture = scatter_sum(mix_part)
-    output = (hidden + mixture).astype(LOW)
-
-    acts, part = after((acts, part))
-    grad_normed = scatter_sum(part)
-    grad_input = grad_hidden + rms_back(plain_in, scale_in, gain_attn, grad_normed)
-
-    def replica_sum(values):
-        if replicas != 4:
-            return lax.psum(values.astype(LOW), "rep")
-        me = lax.axis_index("rep")
-        pieces = values.astype(LOW).reshape((replicas, -1) + values.shape[1:])
-
-        def piece(place):
-            return lax.dynamic_index_in_dim(pieces, place, axis=0, keepdims=False)
-
-        total = piece(me).astype(WIDE)
-        for bits in (1, 2, 3):
-            total = total + flip_replica(piece(me ^ bits), bits).astype(WIDE)
-        low = total.astype(LOW)
-        found = jnp.stack([low] + [flip_replica(low, bits) for bits in (1, 2, 3)])
-        order = me ^ jnp.arange(replicas, dtype=jnp.int32)
-        return jnp.take(found, order, axis=0).reshape(values.shape)
-
-    sum_in, sum_out = (replica_sum(gw_in).astype(WIDE), replica_sum(gw_out).astype(WIDE))
+    part, gw_in, gw_out, sum_q, sum_k, sum_n = attend_backward(upper, packets, kept, *heads)
+
+    def sets(place):
+        return [act[place] for act in acts]
+
+    def exchange(values, axis, count):
+        flip = flip_replica if axis == "rep" else flip_shard
+        return [values] + [flip(values, bits) for bits in range(1, count)]
+
+    def in_order(found, axis):
+        order = lax.axis_index(axis) ^ jnp.arange(len(found), dtype=jnp.int32)
+        return jnp.take(jnp.stack(found), order, axis=0)
+
     small = jnp.concatenate(
         [sum_n[0] / gain_attn, sum_q[0], sum_k[0], gain_moe_sum, grad_router.reshape(-1)]
     )
-    for axis, size, flip in (("rep", replicas, flip_replica), ("shard", groups, flip_shard)):
-        if size & (size - 1):
-            small = lax.psum(small, axis)
-        else:
-            bits = 1
-            while bits < size:
-                small = small + flip(small, bits)
-                bits *= 2
+    if share:
+        me = lax.axis_index("rep")
+
+        def quarters(values):
+            return values.astype(LOW).reshape((replicas, -1) + values.shape[1:])
+
+        def traded(values):
+            pieces = quarters(values)
+            found = [
+                lax.dynamic_index_in_dim(pieces, me ^ bits, axis=0, keepdims=False)
+                for bits in range(replicas)
+            ]
+            return found[:1] + [flip_replica(found[bits], bits) for bits in range(1, replicas)]
+
+        trades = [traded(gw_in), traded(gw_out), exchange(small, "rep", replicas)]
+        acts, gw_in = after((acts, gw_in))
+        grad_gate_w = weight_grad(sets(0), sets(3))
+        grad_gate_w, trades, part, mixture = after((grad_gate_w, trades, part, mixture))
+        grad_normed = scatter_sum(part)
+        lows = [sum(piece.astype(WIDE) for piece in trade).astype(LOW) for trade in trades[:2]]
+        small = jnp.sum(in_order(trades[2], "rep"), axis=0)
+        acts, lows, small = after((acts, lows, small))
+        shared = [exchange(low, "rep", replicas) for low in lows] + [exchange(small, "shard", groups)]
+        grad_up_w = weight_grad(sets(0), sets(4))
+        grad_up_w, shared, acts = after((grad_up_w, shared, acts))
+        sum_in, sum_out = (
+            in_order(pieces, "rep").reshape(values.shape).astype(WIDE)
+            for pieces, values in zip(shared[:2], (gw_in, gw_out))
+        )
+        small = jnp.sum(in_order(shared[2], "shard"), axis=0)
+        grad_down = weight_grad(sets(2), sets(1))
+    else:
+        grad_normed = scatter_sum(part)
+        over_reps = lax.psum(
+            (gw_in.astype(LOW), gw_out.astype(LOW))
+            + tuple(
+                weight_grad(sets(left), sets(right)).astype(LOW)
+                for left, right in ((0, 3), (0, 4), (2, 1))
+            ),
+            "rep",
+        )
+        sum_in, sum_out, grad_gate_w, grad_up_w, grad_down = (
+            values.astype(WIDE) for values in over_reps
+        )
+        small = lax.psum(small, ("rep", "shard"))
+    output = (hidden + mixture).astype(LOW)
+    grad_input = grad_hidden + rms_back(plain_in, scale_in, gain_attn, grad_normed)
     edges = [0, width, width + head_dim, width + 2 * head_dim, 2 * width + 2 * head_dim]
     grad_gain_attn, grad_gain_query, grad_gain_key, grad_gain_moe = (
         small[a:b] for a, b in zip(edges[:-1], edges[1:])
     )
     grad_router = small[edges[-1] :].reshape(w_router.shape)
 
-    def sets(place):
-        return [act[place] for act in acts]
-
-    grad_gate_w = weight_grad(sets(0), sets(3))
-    grad_up_w = weight_grad(sets(0), sets(4))
-    grad_down = weight_grad(sets(2), sets(1))
-    if not share:
-        grad_gate_w, grad_up_w, grad_down = (
-            lax.psum(values.astype(LOW), "rep").astype(WIDE)
-            for values in (grad_gate_w, grad_up_w, grad_down)
-        )
     return (
         output, grad_input, grad_gain_attn, grad_gain_query, grad_gain_key,
         sum_in[:, :wide], sum_in[:, wide : 2 * wide], sum_in[:, 2 * wide :], sum_out,

time: 1350 us -> 1040 us (0.77)
  waiting for transfers between devices: 729 us -> 136 us
  Pallas kernels: 489 us -> 761 us
    ppermute x20 -> x21, waiting for transfers between devices: 374 us -> 86.3 us  [flip_replica(): return lax.ppermute(values, 'rep', [(i, i ^ bits) for i in range(replicas)])]
    pallas_call x4, Pallas kernels: 232 us -> 504 us  [the longest x1 293 us: front(): pl.pallas_call(functools.partial(front_kernel, replicas, groups), in_spec...]
    all_gather x3 -> x0, waiting for transfers between devices: 252 us -> none  [the longest x1 87.8 us: local(): packets = lax.all_gather(packet, 'shard', axis=0)]
    reduce_scatter x4 -> x3, waiting for transfers between devices: 87.5 us -> 0.05 us  [scatter_sum(): lax.psum_scatter(parts.reshape(-1, width), 'shard', scatter_dimension=0,...]
    ppermute x9 -> x13, waiting for transfers between devices: 13.2 us -> 49.7 us  [flip_shard(): return lax.ppermute(values, 'shard', [(i, i ^ bits) for i in range(groups)])]
  transfers between devices with their start and end apart: 37 -> 38, of which waited for: 17 -> 7; matrix products, arithmetic and copies ran while one was open for 5% -> 5% of each run, Pallas kernels for 24% -> 46%
where the time goes in v2:
time: 1040 us; the launch traced here: 1030 us
  Pallas kernels  761 us (73%)
  waiting for transfers between devices  136 us (13%)
  local copies, waits for them, and re-layouts  46.8 us (4%)
  other arithmetic  39 us (4%)
  starting transfers between devices  28 us (3%)
  between operations  15.9 us (2%)
    pallas_call x1, Pallas kernels, front(): pl.pallas_call(functools.partial(front_kernel, replicas, groups), in_spec...  293 us
    pallas_call x3, Pallas kernels, expert_acts(): pl.pallas_call(functools.partial(expert_kernel, row_counts, cot_counts, b...  210 us
    pallas_call x3, Pallas kernels, weight_grad(): pl.pallas_call(kernel, grid=(own, right_cols // right_tile, left_cols //...  151 us
    ppermute x21, waiting for transfers between devices, flip_replica(): return lax.ppermute(values, 'rep', [(i, i ^ bits) for i in range(replicas)])  86.3 us
    pallas_call x2, Pallas kernels, spread_call(): pl.pallas_call(kernel, grid=(count // batch,), in_specs=[pl.BlockSpec(mem...  63.1 us
    ppermute x13, waiting for transfers between devices, flip_shard(): return lax.ppermute(values, 'shard', [(i, i ^ bits) for i in range(groups)])  49.7 us
    pallas_call x1, Pallas kernels, attend_backward(): pl.pallas_call(attend_back_kernel, grid=(count,), in_specs=[first_spec(ar...  43.2 us
    ppermute x21, starting transfers between devices, flip_replica(): return lax.ppermute(values, 'rep', [(i, i ^ bits) for i in range(replicas)])  24.1 us
  transfers between devices with their start and end apart: 38, of which 7 were waited for; matrix products, arithmetic and copies ran while one was open for 5% of the time, Pallas kernels for 46%

profile of v2, /device:TPU:0, one launch (start us, length us, event | category | flops | bytes accessed | tf_op | source)
XLA Modules:
  0.0 1027.5 jit_solution(13374736295267697422)
XLA Ops:
  8.5 1.5 fusion.10
  10.9 1.4 broadcast_select_fusion
  12.6 0.9 pad_maximum_fusion.3
  13.5 1.6 fusion.12
  15.1 293.2 %front.1 = (bf16[8,272,2048]{2,1,0:T(8,128)(2,1)}, f32[8,256,256]{2,1,0:T(8,128)}, f32[8,256,256]{2,1,0:T(8,128)}, bf16[8,256,256]{2,1,0:T(8,128)(2,1)}, bf16[8,...) custom-call(bf16[272,2048]{1,0:T(8,128)(2,1)} %get-tuple-element.430, ...), custom_call_target="tpu_custom_call" | custom-call | flops 1048576 | bytes 65536 | tf_op jit(solution)/shard_map/front/pallas_call | solution.py:821
  308.3 6.1 fusion.22
  314.4 3.3 dynamic-slice_bitcast_fusion
  317.8 1.5 dynamic-slice_bitcast_fusion.1
  319.8 1.5 collective-permute-start.1
  321.2 1.5 collective-permute-start.2
  323.3 1.0 copy.47.wr
  324.8 56.8 %expert_acts.3 = (bf16[2,1152,2048]{2,1,0:T(8,128)(2,1)}, bf16[2,1152,2048]{2,1,0:T(8,128)(2,1)}, bf16[2,1152,1024]{2,1,0:T(8,128)(2,1)}, bf16[2,1152,1024]{2,1,...) custom-call(s32[2]{0:T(128)} %iota_add_fusion.ex_ref, bf16[2,2048,1024]{2,1,0:T(8,128)(2,1)} %wg.7, ...), custom_call_target="tpu_custom_call" | custom-call | flops 1048576 | bytes 65536 | tf_op jit(solution)/shard_map/expert_acts/pallas_call | solution.py:310
  381.6 42.8 %expert_pull.1 = (bf16[8,256,2048]{2,1,0:T(8,128)(2,1)}, f32[2048,16]{1,0:T(8,128)}) custom-call(s32[2]{0:T(128)} %iota_add_fusion.ex_ref, bf16[8,256,2048]{2,1,0:T(8,128)(2,1)} %get-tuple-element.199.refs_0_.rows_ref, bf16[8,272,2048]{2,1,0:T(8,128)(2,1)} %get-tuple-element.200.refs_1_.cot_ref, bf16[2,1152,1024]{2,1,0:T(8,128)(2,1)} %get-tuple-element.308.dg_ref.refs_3_, ...), custom_call_target="tpu_custom_call" | custom-call | flops 1048576 | bytes 65536 | tf_op jit(solution)/shard_map/expert_pull/pallas_call | solution.py:391
  425.6 1.5 collective-permute-start.4
  427.1 44.5 %collective-permute-done.5.refs_1_ = bf16[2,256,2048]{2,1,0:T(8,128)(2,1)S(1)} collective-permute-done((bf16[2,256,2048]{2,1,0:T(8,128)(2,1)}, bf16[2,256,2048]{2,1,0:T(8,128)(2,1)S(1)}, u32[]{:S(2)}, u32[]{:S(2)}) %collective-permute-start.5) | collective-permute-done | bytes 2097184 | tf_op jit(solution)/shard_map/ppermute | solution.py:881
  471.6 1.3 copy-done.10
  472.9 56.2 %expert_acts.4 = (bf16[2,1152,2048]{2,1,0:T(8,128)(2,1)}, bf16[2,1152,2048]{2,1,0:T(8,128)(2,1)}, bf16[2,1152,1024]{2,1,0:T(8,128)(2,1)}, bf16[2,1152,1024]{2,1,...) custom-call(s32[2]{0:T(128)} %iota_add_fusion.ex_ref, bf16[2,2048,1024]{2,1,0:T(8,128)(2,1)} %wg.7, ...), custom_call_target="tpu_custom_call" | custom-call | flops 1048576 | bytes 65536 | tf_op jit(solution)/shard_map/expert_acts/pallas_call | solution.py:310
  529.9 20.3 %expert_mix.1 = bf16[8,256,2048]{2,1,0:T(8,128)(2,1)} custom-call(s32[2]{0:T(128)} %iota_add_fusion.ex_ref, bf16[8,272,2048]{2,1,0:T(8,128)(2,1)} %get-tuple-element.200.refs_1_.cot_ref, bf16[2,1152,1024]{2,1,0:T(8,128)(2,1)} %get-tuple-element.374.m_ref.refs_0_, bf16[2,1024,2048]{2,1,0:T(8,128)(2,1)} %wd.7), custom_call_target="tpu_custom_call" | custom-call | flops 1048576 | bytes 65536 | tf_op jit(solution)/shard_map/expert_mix/pallas_call | solution.py:391
  550.3 1.5 convert_element_type.81
  553.8 1.7 fusion.21
  555.6 97.5 %expert_acts.5 = (bf16[2,2304,2048]{2,1,0:T(8,128)(2,1)}, bf16[2,2304,2048]{2,1,0:T(8,128)(2,1)}, bf16[2,2304,1024]{2,1,0:T(8,128)(2,1)}, bf16[2,2304,1024]{2,1,...) custom-call(s32[2]{0:T(128)} %iota_add_fusion.ex_ref, bf16[2,2048,1024]{2,1,0:T(8,128)(2,1)} %wg.7, ...), custom_call_target="tpu_custom_call" | custom-call | flops 1048576 | bytes 65536 | tf_op jit(solution)/shard_map/expert_acts/pallas_call | solution.py:310
  653.2 1.1 copy-done.13
  654.6 43.2 %attend_backward.1 = (bf16[8,256,2048]{2,1,0:T(8,128)(2,1)}, f32[2048,768]{1,0:T(8,128)}, f32[256,2048]{1,0:T(8,128)}, f32[1,128]{1,0:T(1,128)}, f32[1,128]{1,0:T(1,128)}, /*index=5*/f32[1,2048]{1,0:T(1,128)}) custom-call(bf16[8,256,2048]{2,1,0:T(8,128)(2,1)} %bitcast.73, bf16[8,272,2048]{2,1,0:T(8,128)(2,1)} %get-tuple-element.299.pk_ref, ...), custom_call_target="tpu_custom_call" | custom-call | flops 1048576 | bytes 65536 | tf_op jit(solution)/shard_map/attend_backward/pallas_call | solution.py:193
  697.8 3.1 convert_element_type.83
  701.0 1.7 dynamic-slice_bitcast_fusion.2
  703.3 1.5 collective-permute-start.13
  704.8 1.4 collective-permute-start.14
  707.0 1.5 collective-permute-start.19
  708.6 0.9 dynamic-slice_bitcast_fusion.6
  709.5 33.2 %collective-permute-done.18 = f32[37120]{0:T(1024)S(1)} collective-permute-done((f32[37120]{0:T(1024)S(1)}, f32[37120]{0:T(1024)S(1)}, u32[]{:S(2)}, u32[]{:S(2)}) %collective-permute-start.18) | collective-permute-done | bytes 148512 | tf_op jit(solution)/shard_map/ppermute | solution.py:881
  743.6 2.7 collective-permute-start.20
  746.3 8.7 collective-permute-done.20
  755.6 1.2 collective-permute-start.17
  756.8 50.1 %weight_grad.3 = f32[2,2048,1024]{2,1,0:T(8,128)} custom-call(bf16[2,1152,2048]{2,1,0:T(8,128)(2,1)} %get-tuple-element.341.refs_0_, bf16[2,1152,2048]{2,1,0:T(8,128)(2,1)} %get-tuple-element.342.refs_1_, bf16[2,2304,2048]{2,1,0:T(8,128)(2,1)} %get-tuple-element.343.refs_2_, bf16[2,1152,1024]{2,1,0:T(8,128)(2,1)} %get-tuple-element.308.dg_ref.refs_3_, ...), custom_call_target="tpu_custom_call" | custom-call | flops 1048576 | bytes 65536 | tf_op jit(solution)/shard_map/weight_grad/pallas_call | solution.py:416
  807.0 2.8 convert_element_type.85
  812.0 1.0 stack.74
  813.0 1.1 stack.75
  814.7 1.0 gather_fusion
  815.7 1.1 select_reduce_fusion.1
  816.8 2.3 add_convert_fusion.1
  819.2 1.4 add_convert_fusion.2
  820.8 1.8 collective-permute-start.29
  822.6 1.7 collective-permute-start.21
  824.9 8.4 collective-permute-done.28
  833.2 1.7 collective-permute-start.23
  834.9 11.3 %collective-permute-done.29 = f32[37120]{0:T(1024)S(1)} collective-permute-done((f32[37120]{0:T(1024)S(1)}, f32[37120]{0:T(1024)S(1)}, u32[]{:S(2)}, u32[]{:S(2)}) %collective-permute-start.29) | collective-permute-done | bytes 148512 | tf_op jit(solution)/shard_map/ppermute | solution.py:884
  847.0 18.7 %collective-permute-done.31 = f32[37120]{0:T(1024)S(1)} collective-permute-done((f32[37120]{0:T(1024)S(1)}, f32[37120]{0:T(1024)S(1)}, u32[]{:S(2)}, u32[]{:S(2)}) %collective-permute-start.31) | collective-permute-done | bytes 148512 | tf_op jit(solution)/shard_map/ppermute | solution.py:884
  865.8 1.6 collective-permute-start.24
  868.2 11.3 %collective-permute-done.33 = f32[37120]{0:T(1024)S(1)} collective-permute-done((f32[37120]{0:T(1024)S(1)}, f32[37120]{0:T(1024)S(1)}, u32[]{:S(2)}, u32[]{:S(2)}) %collective-permute-start.33) | collective-permute-done | bytes 148512 | tf_op jit(solution)/shard_map/ppermute | solution.py:884
  880.1 1.3 collective-permute-start.26
  881.6 50.1 %weight_grad.4 = f32[2,2048,1024]{2,1,0:T(8,128)} custom-call(bf16[2,1152,2048]{2,1,0:T(8,128)(2,1)} %get-tuple-element.341.refs_0_, bf16[2,1152,2048]{2,1,0:T(8,128)(2,1)} %get-tuple-element.342.refs_1_, bf16[2,2304,2048]{2,1,0:T(8,128)(2,1)} %get-tuple-element.343.refs_2_, bf16[2,1152,1024]{2,1,0:T(8,128)(2,1)} %get-tuple-element.344.du_ref.refs_3_, ...), custom_call_target="tpu_custom_call" | custom-call | flops 1048576 | bytes 65536 | tf_op jit(solution)/shard_map/weight_grad/pallas_call | solution.py:416
  931.8 1.2 pad_maximum_fusion.1
  933.0 1.7 gather_fusion.3
  934.7 3.2 pad_maximum_fusion
  938.0 4.5 gather_fusion.2
  948.0 3.6 stack.85
  951.6 1.9 gather_fusion.1
  953.4 1.7 select_reduce_fusion
  955.5 1.0 copy.51
  956.4 51.2 %weight_grad.5 = f32[2,1024,2048]{2,1,0:T(8,128)} custom-call(bf16[2,1152,1024]{2,1,0:T(8,128)(2,1)} %get-tuple-element.374.m_ref.refs_0_, bf16[2,1152,1024]{2,1,0:T(8,128)(2,1)} %get-tuple-element.375.refs_1_, bf16[2,2304,1024]{2,1,0:T(8,128)(2,1)} %get-tuple-element.376.refs_2_, bf16[2,1152,2048]{2,1,0:T(8,128)(2,1)} %get-tuple-element.377.refs_3_, ...), custom_call_target="tpu_custom_call" | custom-call | flops 1048576 | bytes 65536 | tf_op jit(solution)/shard_map/weight_grad/pallas_call | solution.py:416
  1008.7 1.6 fusion.14
  1011.2 2.8 fusion.23
  1014.1 1.9 fusion.6
  1016.0 4.4 fusion.9
  (216 shorter events, 24.6 us)
Async XLA Ops:
  7.2 543.1 %reduce-scatter.4.cloned.1.call-start = ((), (), s32[]{:S(2)}) async-start(), calls=%async_computation.3 | async-start | bytes 9437184 | tf_op jit(solution)/shard_map/reduce_scatter | solution.py:887
  8.5 544.0 %copy-start.51 = (pred[256]{0:T(512)(128)(4,1)}, pred[256]{0:T(512)(128)(4,1)S(1)}, u32[]{:S(2)}) copy-start(pred[256]{0:T(512)(128)(4,1)S(1)} %iota_compare_fusion.4) | copy-start | bytes 772
  317.8 5.5 copy-start.43
  319.2 62.4 %collective-permute-start = (bf16[2,256,2048]{2,1,0:T(8,128)(2,1)}, bf16[2,256,2048]{2,1,0:T(8,128)(2,1)S(1)}, u32[]{:S(2)}, u32[]{:S(2)}) collective-permute-start(bf16[2,256,2048]{2,1,0:T(8,128)(2,1)} %dynamic-slice_bitcast_fusion.1), channel_id=1, source_target_pairs={{0,8},{8,0},{16,24},{24,16},{1,9},{9,1},{17,25},{25,17},{2,10},{10... | collective-permute-start | bytes 6291464 | tf_op jit(solution)/shard_map/ppermute | solution.py:881
  319.8 61.8 %collective-permute-start.1 = (bf16[2,256,2048]{2,1,0:T(8,128)(2,1)}, bf16[2,256,2048]{2,1,0:T(8,128)(2,1)}, u32[]{:S(2)}, u32[]{:S(2)}) collective-permute-start(bf16[2,256,2048]{2,1,0:T(8,128)(2,1)} %dynamic-slice_bitcast_fusion.1), channel_id=1, source_target_pairs={{0,16},{8,24},{16,0},{24,8},{1,17},{9,25},{17,1},{25,9},{2,18},{10... | collective-permute-start | bytes 6291464 | tf_op jit(solution)/shard_map/ppermute | solution.py:881
  321.2 103.2 %collective-permute-start.2 = (bf16[2,256,2048]{2,1,0:T(8,128)(2,1)}, bf16[2,256,2048]{2,1,0:T(8,128)(2,1)}, u32[]{:S(2)}, u32[]{:S(2)}) collective-permute-start(bf16[2,256,2048]{2,1,0:T(8,128)(2,1)} %dynamic-slice_bitcast_fusion), channel_id=1, source_target_pairs={{0,8},{8,0},{16,24},{24,16},{1,9},{9,1},{17,25},{25,17},{2,10},{10... | collective-permute-start | bytes 6291464 | tf_op jit(solution)/shard_map/ppermute | solution.py:881
  322.7 101.7 %collective-permute-start.3 = (bf16[2,256,2048]{2,1,0:T(8,128)(2,1)}, bf16[2,256,2048]{2,1,0:T(8,128)(2,1)}, u32[]{:S(2)}, u32[]{:S(2)}) collective-permute-start(bf16[2,256,2048]{2,1,0:T(8,128)(2,1)} %dynamic-slice_bitcast_fusion), channel_id=1, source_target_pairs={{0,16},{8,24},{16,0},{24,8},{1,17},{9,25},{17,1},{25,9},{2,18},{10... | collective-permute-start | bytes 6291464 | tf_op jit(solution)/shard_map/ppermute | solution.py:881
  381.6 42.8 %copy-start.11 = (bf16[2,256,2048]{2,1,0:T(8,128)(2,1)}, bf16[2,256,2048]{2,1,0:T(8,128)(2,1)S(1)}, u32[]{:S(2)}) copy-start(bf16[2,256,2048]{2,1,0:T(8,128)(2,1)S(1)} %collective-permute-done.refs_0_) | copy-start | bytes 6291460
  424.4 228.6 %all-gather.3.cloned.1.call-start = ((), (), s32[]{:S(2)}) async-start(), calls=%async_computation.6 | async-start | bytes 9437184 | tf_op jit(solution)/shard_map/all_gather | solution.py:962
  424.5 47.0 %collective-permute-start.5 = (bf16[2,256,2048]{2,1,0:T(8,128)(2,1)}, bf16[2,256,2048]{2,1,0:T(8,128)(2,1)S(1)}, u32[]{:S(2)}, u32[]{:S(2)}) collective-permute-start(bf16[2,256,2048]{2,1,0:T(8,128)(2,1)} %collective-permute-done.3.refs_3_), channel_id=1, source_target_pairs={{0,8},{8,0},{16,24},{24,16},{1,9},{9,1},{17,25},{25,17},{2,10},{10... | collective-permute-start | bytes 6291464 | tf_op jit(solution)/shard_map/ppermute | solution.py:881
  425.1 104.0 %collective-permute-start.9 = (bf16[2,256,2048]{2,1,0:T(8,128)(2,1)}, bf16[2,256,2048]{2,1,0:T(8,128)(2,1)}, u32[]{:S(2)}, u32[]{:S(2)}) collective-permute-start(bf16[2,256,2048]{2,1,0:T(8,128)(2,1)} %collective-permute-done.3.refs_3_), channel_id=1, source_target_pairs={{0,1},{1,0},{2,3},{3,2},{4,5},{5,4},{6,7},{7,6},{8,9},{9,8},{10,11... | collective-permute-start | bytes 6291464 | tf_op jit(solution)/shard_map/ppermute | solution.py:884
  425.1 104.0 %collective-permute-start.7 = (bf16[2,256,2048]{2,1,0:T(8,128)(2,1)}, bf16[2,256,2048]{2,1,0:T(8,128)(2,1)}, u32[]{:S(2)}, u32[]{:S(2)}) collective-permute-start(bf16[2,256,2048]{2,1,0:T(8,128)(2,1)} %collective-permute-done.2.refs_1_), channel_id=1, source_target_pairs={{0,1},{1,0},{2,3},{3,2},{4,5},{5,4},{6,7},{7,6},{8,9},{9,8},{10,11... | collective-permute-start | bytes 6291464 | tf_op jit(solution)/shard_map/ppermute | solution.py:884
  425.6 103.5 %collective-permute-start.4 = (bf16[2,256,2048]{2,1,0:T(8,128)(2,1)}, bf16[2,256,2048]{2,1,0:T(8,128)(2,1)}, u32[]{:S(2)}, u32[]{:S(2)}) collective-permute-start(bf16[2,256,2048]{2,1,0:T(8,128)(2,1)} %copy-done.11), channel_id=1, source_target_pairs={{0,16},{8,24},{16,0},{24,8},{1,17},{9,25},{17,1},{25,9},{2,18},{10... | collective-permute-start | bytes 6291464 | tf_op jit(solution)/shard_map/ppermute | solution.py:881
  427.1 102.0 %collective-permute-start.6 = (bf16[2,256,2048]{2,1,0:T(8,128)(2,1)}, bf16[2,256,2048]{2,1,0:T(8,128)(2,1)}, u32[]{:S(2)}, u32[]{:S(2)}) collective-permute-start(bf16[2,256,2048]{2,1,0:T(8,128)(2,1)} %copy-done.11), channel_id=1, source_target_pairs={{0,1},{1,0},{2,3},{3,2},{4,5},{5,4},{6,7},{7,6},{8,9},{9,8},{10,11... | collective-permute-start | bytes 6291464 | tf_op jit(solution)/shard_map/ppermute | solution.py:884
  471.5 57.6 %collective-permute-start.8 = (bf16[2,256,2048]{2,1,0:T(8,128)(2,1)}, bf16[2,256,2048]{2,1,0:T(8,128)(2,1)}, u32[]{:S(2)}, u32[]{:S(2)}) collective-permute-start(bf16[2,256,2048]{2,1,0:T(8,128)(2,1)} %collective-permute-done.1.refs_2_), channel_id=1, source_target_pairs={{0,1},{1,0},{2,3},{3,2},{4,5},{5,4},{6,7},{7,6},{8,9},{9,8},{10,11... | collective-permute-start | bytes 6291464 | tf_op jit(solution)/shard_map/ppermute | solution.py:884
  472.9 56.8 %copy-start = (f32[256,2048]{1,0:T(8,128)S(1)}, f32[256,2048]{1,0:T(8,128)}, u32[]{:S(2)}) copy-start(f32[256,2048]{1,0:T(8,128)} %get-tuple-element.197) | copy-start | bytes 6291460
  529.1 21.1 %collective-permute-start.10 = (bf16[2,256,2048]{2,1,0:T(8,128)(2,1)}, bf16[2,256,2048]{2,1,0:T(8,128)(2,1)}, u32[]{:S(2)}, u32[]{:S(2)}) collective-permute-start(bf16[2,256,2048]{2,1,0:T(8,128)(2,1)} %collective-permute-done.4.refs_0_), channel_id=1, source_target_pairs={{0,1},{1,0},{2,3},{3,2},{4,5},{5,4},{6,7},{7,6},{8,9},{9,8},{10,11... | collective-permute-start | bytes 6291464 | tf_op jit(solution)/shard_map/ppermute | solution.py:884
  529.2 21.1 %collective-permute-start.11 = (bf16[2,256,2048]{2,1,0:T(8,128)(2,1)}, bf16[2,256,2048]{2,1,0:T(8,128)(2,1)}, u32[]{:S(2)}, u32[]{:S(2)}) collective-permute-start(bf16[2,256,2048]{2,1,0:T(8,128)(2,1)} %copy-done.10), channel_id=1, source_target_pairs={{0,1},{1,0},{2,3},{3,2},{4,5},{5,4},{6,7},{7,6},{8,9},{9,8},{10,11... | collective-permute-start | bytes 6291464 | tf_op jit(solution)/shard_map/ppermute | solution.py:884
  529.9 22.6 %copy-start.46 = (f32[256]{0:T(256)}, f32[256]{0:T(256)S(1)}, u32[]{:S(2)}) copy-start(f32[256]{0:T(256)S(1)} %add_rsqrt_fusion) | copy-start | bytes 3076
  555.5 251.4 %reduce-scatter.6.cloned.1.call-start = ((), (), s32[]{:S(2)}) async-start(), calls=%async_computation.4 | async-start | bytes 9437184 | tf_op jit(solution)/shard_map/reduce_scatter | solution.py:887
  653.1 360.9 %reduce-scatter.8.cloned.1.call-start = ((), (), s32[]{:S(2)}) async-start(), calls=%async_computation.5 | async-start | bytes 9437184 | tf_op jit(solution)/shard_map/reduce_scatter | solution.py:887
  700.9 5.3 copy-start.50
  700.9 5.3 copy-start.55
  701.0 5.3 copy-start.54
  701.0 7.5 copy-start.12
  702.7 107.1 %collective-permute-start.12 = (bf16[512,768]{1,0:T(8,128)(2,1)}, bf16[512,768]{1,0:T(8,128)(2,1)S(1)}, u32[]{:S(2)}, u32[]{:S(2)}) collective-permute-start(bf16[512,768]{1,0:T(8,128)(2,1)} %get-tuple-element.417), channel_id=1, source_target_pairs={{0,8},{8,0},{16,24},{24,16},{1,9},{9,1},{17,25},{25,17},{2,10},{10... | collective-permute-start | bytes 2359304 | tf_op jit(solution)/shard_map/ppermute | solution.py:881
  703.3 106.5 %collective-permute-start.13 = (bf16[512,768]{1,0:T(8,128)(2,1)}, bf16[512,768]{1,0:T(8,128)(2,1)}, u32[]{:S(2)}, u32[]{:S(2)}) collective-permute-start(bf16[512,768]{1,0:T(8,128)(2,1)} %get-tuple-element.416), channel_id=1, source_target_pairs={{0,16},{8,24},{16,0},{24,8},{1,17},{9,25},{17,1},{25,9},{2,18},{10... | collective-permute-start | bytes 2359304 | tf_op jit(solution)/shard_map/ppermute | solution.py:881
  704.8 105.0 %collective-permute-start.14 = (bf16[512,768]{1,0:T(8,128)(2,1)}, bf16[512,768]{1,0:T(8,128)(2,1)}, u32[]{:S(2)}, u32[]{:S(2)}) collective-permute-start(bf16[512,768]{1,0:T(8,128)(2,1)} %get-tuple-element.415), channel_id=1, source_target_pairs={{0,24},{8,16},{16,8},{24,0},{1,25},{9,17},{17,9},{25,1},{2,26},{10... | collective-permute-start | bytes 2359304 | tf_op jit(solution)/shard_map/ppermute | solution.py:881
  706.3 37.3 %copy-start.20 = (f32[37120]{0:T(1024)}, f32[37120]{0:T(1024)S(1)}, u32[]{:S(2)}) copy-start(f32[37120]{0:T(1024)S(1)} %constant_dynamic-update-slice_fusion) | copy-start | bytes 445444
  706.3 36.4 %collective-permute-start.18 = (f32[37120]{0:T(1024)S(1)}, f32[37120]{0:T(1024)S(1)}, u32[]{:S(2)}, u32[]{:S(2)}) collective-permute-start(f32[37120]{0:T(1024)S(1)} %constant_dynamic-update-slice_fusion), channel_id=1, source_target_pairs={{0,8},{8,0},{16,24},{24,16},{1,9},{9,1},{17,25},{25,17},{2,10},{10... | collective-permute-start | bytes 445448 | tf_op jit(solution)/shard_map/ppermute | solution.py:881
  707.0 36.7 %collective-permute-start.19 = (f32[37120]{0:T(1024)S(1)}, f32[37120]{0:T(1024)S(1)}, u32[]{:S(2)}, u32[]{:S(2)}) collective-permute-start(f32[37120]{0:T(1024)S(1)} %constant_dynamic-update-slice_fusion), channel_id=1, source_target_pairs={{0,16},{8,24},{16,0},{24,8},{1,17},{9,25},{17,1},{25,9},{2,18},{10... | collective-permute-start | bytes 445448 | tf_op jit(solution)/shard_map/ppermute | solution.py:881
  743.3 12.3 %collective-permute-start.15 = (bf16[64,2048]{1,0:T(8,128)(2,1)S(1)}, bf16[64,2048]{1,0:T(8,128)(2,1)S(1)}, u32[]{:S(2)}, u32[]{:S(2)}) collective-permute-start(bf16[64,2048]{1,0:T(8,128)(2,1)S(1)} %get-tuple-element.423), channel_id=1, source_target_pairs={{0,8},{8,0},{16,24},{24,16},{1,9},{9,1},{17,25},{25,17},{2,10},{10... | collective-permute-start | bytes 786440 | tf_op jit(solution)/shard_map/ppermute | solution.py:881
  743.6 12.0 %copy-start.34 = (f32[37120]{0:T(1024)}, f32[37120]{0:T(1024)S(1)}, u32[]{:S(2)}) copy-start(f32[37120]{0:T(1024)S(1)} %collective-permute-done.19) | copy-start | bytes 445444
  743.6 11.4 %collective-permute-start.20 = (f32[37120]{0:T(1024)S(1)}, f32[37120]{0:T(1024)S(1)}, u32[]{:S(2)}, u32[]{:S(2)}) collective-permute-start(f32[37120]{0:T(1024)S(1)} %constant_dynamic-update-slice_fusion), channel_id=1, source_target_pairs={{0,24},{8,16},{16,8},{24,0},{1,25},{9,17},{17,9},{25,1},{2,26},{10... | collective-permute-start | bytes 445448 | tf_op jit(solution)/shard_map/ppermute | solution.py:881
  755.0 54.8 %collective-permute-start.16 = (bf16[64,2048]{1,0:T(8,128)(2,1)}, bf16[64,2048]{1,0:T(8,128)(2,1)}, u32[]{:S(2)}, u32[]{:S(2)}) collective-permute-start(bf16[64,2048]{1,0:T(8,128)(2,1)} %get-tuple-element.422), channel_id=1, source_target_pairs={{0,16},{8,24},{16,0},{24,8},{1,17},{9,25},{17,1},{25,9},{2,18},{10... | collective-permute-start | bytes 786440 | tf_op jit(solution)/shard_map/ppermute | solution.py:881
  755.6 51.4 %copy-start.18 = (bf16[64,2048]{1,0:T(8,128)(2,1)}, bf16[64,2048]{1,0:T(8,128)(2,1)S(1)}, u32[]{:S(2)}) copy-start(bf16[64,2048]{1,0:T(8,128)(2,1)S(1)} %collective-permute-done.15) | copy-start | bytes 786436
  755.6 54.2 %collective-permute-start.17 = (bf16[64,2048]{1,0:T(8,128)(2,1)}, bf16[64,2048]{1,0:T(8,128)(2,1)}, u32[]{:S(2)}, u32[]{:S(2)}) collective-permute-start(bf16[64,2048]{1,0:T(8,128)(2,1)} %get-tuple-element.421), channel_id=1, source_target_pairs={{0,24},{8,16},{16,8},{24,0},{1,25},{9,17},{17,9},{25,1},{2,26},{10... | collective-permute-start | bytes 786440 | tf_op jit(solution)/shard_map/ppermute | solution.py:881
  816.8 50.6 %copy-start.16 = (f32[37120]{0:T(1024)}, f32[37120]{0:T(1024)S(1)}, u32[]{:S(2)}) copy-start(f32[37120]{0:T(1024)S(1)} %select_reduce_fusion.1) | copy-start | bytes 445444
  816.8 51.3 %copy-start.53 = (pred[4]{0:T(512)(128)(4,1)S(1)}, pred[4]{0:T(512)(128)(4,1)}, u32[]{:S(2)}) copy-start(pred[4]{0:T(512)(128)(4,1)} %compare_and_fusion) | copy-start | bytes 16
  819.1 112.6 %copy-start.9 = (bf16[512,768]{1,0:T(8,128)(2,1)}, bf16[512,768]{1,0:T(8,128)(2,1)S(1)}, u32[]{:S(2)}) copy-start(bf16[512,768]{1,0:T(8,128)(2,1)S(1)} %add_convert_fusion.1) | copy-start | bytes 2359300
  820.6 111.1 %copy-start.14 = (bf16[64,2048]{1,0:T(8,128)(2,1)}, bf16[64,2048]{1,0:T(8,128)(2,1)S(1)}, u32[]{:S(2)}) copy-start(bf16[64,2048]{1,0:T(8,128)(2,1)S(1)} %add_convert_fusion.2) | copy-start | bytes 786436
  820.6 3.7 collective-permute-start.27
  820.7 12.5 %collective-permute-start.28 = (f32[37120]{0:T(1024)S(1)}, f32[37120]{0:T(1024)S(1)}, u32[]{:S(2)}, u32[]{:S(2)}) collective-permute-start(f32[37120]{0:T(1024)S(1)} %select_reduce_fusion.1), channel_id=1, source_target_pairs={{0,2},{1,3},{2,0},{3,1},{4,6},{5,7},{6,4},{7,5},{8,10},{9,11},{10,... | collective-permute-start | bytes 445448 | tf_op jit(solution)/shard_map/ppermute | solution.py:884
  820.8 25.5 %collective-permute-start.29 = (f32[37120]{0:T(1024)S(1)}, f32[37120]{0:T(1024)S(1)}, u32[]{:S(2)}, u32[]{:S(2)}) collective-permute-start(f32[37120]{0:T(1024)S(1)} %select_reduce_fusion.1), channel_id=1, source_target_pairs={{0,3},{1,2},{2,1},{3,0},{4,7},{5,6},{6,5},{7,4},{8,11},{9,10},{10,... | collective-permute-start | bytes 445448 | tf_op jit(solution)/shard_map/ppermute | solution.py:884
  822.6 23.7 %collective-permute-start.30 = (f32[37120]{0:T(1024)S(1)}, f32[37120]{0:T(1024)S(1)}, u32[]{:S(2)}, u32[]{:S(2)}) collective-permute-start(f32[37120]{0:T(1024)S(1)} %select_reduce_fusion.1), channel_id=1, source_target_pairs={{0,4},{1,5},{2,6},{3,7},{4,0},{5,1},{6,2},{7,3},{8,12},{9,13},{10,... | collective-permute-start | bytes 445448 | tf_op jit(solution)/shard_map/ppermute | solution.py:884
  822.6 109.2 %collective-permute-start.21 = (bf16[512,768]{1,0:T(8,128)(2,1)S(1)}, bf16[512,768]{1,0:T(8,128)(2,1)}, u32[]{:S(2)}, u32[]{:S(2)}) collective-permute-start(bf16[512,768]{1,0:T(8,128)(2,1)S(1)} %add_convert_fusion.1), channel_id=1, source_target_pairs={{0,8},{8,0},{16,24},{24,16},{1,9},{9,1},{17,25},{25,17},{2,10},{10... | collective-permute-start | bytes 2359304 | tf_op jit(solution)/shard_map/ppermute | solution.py:881
  824.3 43.1 %copy-start.22 = (f32[37120]{0:T(1024)}, f32[37120]{0:T(1024)S(1)}, u32[]{:S(2)}) copy-start(f32[37120]{0:T(1024)S(1)} %collective-permute-done.27) | copy-start | bytes 445444
  824.3 107.4 %collective-permute-start.22 = (bf16[512,768]{1,0:T(8,128)(2,1)S(1)}, bf16[512,768]{1,0:T(8,128)(2,1)}, u32[]{:S(2)}, u32[]{:S(2)}) collective-permute-start(bf16[512,768]{1,0:T(8,128)(2,1)S(1)} %add_convert_fusion.1), channel_id=1, source_target_pairs={{0,16},{8,24},{16,0},{24,8},{1,17},{9,25},{17,1},{25,9},{2,18},{10... | collective-permute-start | bytes 2359304 | tf_op jit(solution)/shard_map/ppermute | solution.py:881
  833.2 34.2 %copy-start.24 = (f32[37120]{0:T(1024)}, f32[37120]{0:T(1024)S(1)}, u32[]{:S(2)}) copy-start(f32[37120]{0:T(1024)S(1)} %collective-permute-done.28) | copy-start | bytes 445444
  833.2 98.6 %collective-permute-start.23 = (bf16[512,768]{1,0:T(8,128)(2,1)S(1)}, bf16[512,768]{1,0:T(8,128)(2,1)}, u32[]{:S(2)}, u32[]{:S(2)}) collective-permute-start(bf16[512,768]{1,0:T(8,128)(2,1)S(1)} %add_convert_fusion.1), channel_id=1, source_target_pairs={{0,24},{8,16},{16,8},{24,0},{1,25},{9,17},{17,9},{25,1},{2,26},{10... | collective-permute-start | bytes 2359304 | tf_op jit(solution)/shard_map/ppermute | solution.py:881
  846.2 21.2 %copy-start.26 = (f32[37120]{0:T(1024)}, f32[37120]{0:T(1024)S(1)}, u32[]{:S(2)}) copy-start(f32[37120]{0:T(1024)S(1)} %collective-permute-done.29) | copy-start | bytes 445444
  846.2 19.5 %collective-permute-start.31 = (f32[37120]{0:T(1024)S(1)}, f32[37120]{0:T(1024)S(1)}, u32[]{:S(2)}, u32[]{:S(2)}) collective-permute-start(f32[37120]{0:T(1024)S(1)} %select_reduce_fusion.1), channel_id=1, source_target_pairs={{0,5},{1,4},{2,7},{3,6},{4,1},{5,0},{6,3},{7,2},{8,13},{9,12},{10,... | collective-permute-start | bytes 445448 | tf_op jit(solution)/shard_map/ppermute | solution.py:884
  846.2 21.2 %copy-start.28 = (f32[37120]{0:T(1024)}, f32[37120]{0:T(1024)S(1)}, u32[]{:S(2)}) copy-start(f32[37120]{0:T(1024)S(1)} %collective-permute-done.30) | copy-start | bytes 445444
  846.3 21.1 %collective-permute-start.32 = (f32[37120]{0:T(1024)S(1)}, f32[37120]{0:T(1024)S(1)}, u32[]{:S(2)}, u32[]{:S(2)}) collective-permute-start(f32[37120]{0:T(1024)S(1)} %select_reduce_fusion.1), channel_id=1, source_target_pairs={{0,6},{1,7},{2,4},{3,5},{4,2},{5,3},{6,0},{7,1},{8,14},{9,15},{10,... | collective-permute-start | bytes 445448 | tf_op jit(solution)/shard_map/ppermute | solution.py:884
  865.8 14.3 %collective-permute-start.24 = (bf16[64,2048]{1,0:T(8,128)(2,1)S(1)}, bf16[64,2048]{1,0:T(8,128)(2,1)S(1)}, u32[]{:S(2)}, u32[]{:S(2)}) collective-permute-start(bf16[64,2048]{1,0:T(8,128)(2,1)S(1)} %add_convert_fusion.2), channel_id=1, source_target_pairs={{0,8},{8,0},{16,24},{24,16},{1,9},{9,1},{17,25},{25,17},{2,10},{10... | collective-permute-start | bytes 786440 | tf_op jit(solution)/shard_map/ppermute | solution.py:881
  868.1 11.3 %collective-permute-start.33 = (f32[37120]{0:T(1024)S(1)}, f32[37120]{0:T(1024)S(1)}, u32[]{:S(2)}, u32[]{:S(2)}) collective-permute-start(f32[37120]{0:T(1024)S(1)} %select_reduce_fusion.1), channel_id=1, source_target_pairs={{0,7},{1,6},{2,5},{3,4},{4,3},{5,2},{6,1},{7,0},{8,15},{9,14},{10,... | collective-permute-start | bytes 445448 | tf_op jit(solution)/shard_map/ppermute | solution.py:884
  879.4 52.3 %collective-permute-start.25 = (bf16[64,2048]{1,0:T(8,128)(2,1)S(1)}, bf16[64,2048]{1,0:T(8,128)(2,1)}, u32[]{:S(2)}, u32[]{:S(2)}) collective-permute-start(bf16[64,2048]{1,0:T(8,128)(2,1)S(1)} %add_convert_fusion.2), channel_id=1, source_target_pairs={{0,16},{8,24},{16,0},{24,8},{1,17},{9,25},{17,1},{25,9},{2,18},{10... | collective-permute-start | bytes 786440 | tf_op jit(solution)/shard_map/ppermute | solution.py:881
  880.1 51.6 %collective-permute-start.26 = (bf16[64,2048]{1,0:T(8,128)(2,1)S(1)}, bf16[64,2048]{1,0:T(8,128)(2,1)}, u32[]{:S(2)}, u32[]{:S(2)}) collective-permute-start(bf16[64,2048]{1,0:T(8,128)(2,1)S(1)} %add_convert_fusion.2), channel_id=1, source_target_pairs={{0,24},{8,16},{16,8},{24,0},{1,25},{9,17},{17,9},{25,1},{2,26},{10... | collective-permute-start | bytes 786440 | tf_op jit(solution)/shard_map/ppermute | solution.py:881
  937.9 5.4 copy-start.25
  938.0 6.2 copy-start.27
  938.0 6.9 copy-start.29
  938.0 7.7 copy-start.31
  938.0 8.5 copy-start.36
  956.4 52.3 %copy-start.8 = (bf16[4,64,2048]{2,1,0:T(8,128)(2,1)S(1)}, bf16[4,64,2048]{2,1,0:T(8,128)(2,1)}, u32[]{:S(2)}) copy-start(bf16[4,64,2048]{2,1,0:T(8,128)(2,1)} %gather_fusion.3) | copy-start | bytes 3145732
  (30 other events, 70.1 us)
Sparse Core Ops, SparseCore 0:
  424.6 86.8 reduce-scatter.3
  555.7 79.2 all-gather.2
  653.2 86.9 reduce-scatter.5
  810.0 100.8 reduce-scatter.7

commit v3 on v2

--- a/solution.py
+++ b/solution.py
@@ -1,4 +1,5 @@
 import functools
+import math
 
 import jax
 import jax.numpy as jnp
@@ -130,7 +131,7 @@
 def attend_back_kernel(
     da_ref, pk_ref, qr_ref, kr_ref, v_ref, o_ref,
     wq, wk, wv, wo, gq, gk, cos_ref, sin_ref,
-    part_ref, gw_in, gw_out, gain_q, gain_k, gain_n,
+    part_ref, gw_ref, gain_q, gain_k, gain_n, gw_sum,
 ):
     rows = pk_ref.shape[1] - LINES
     head_dim = gq.shape[-1]
@@ -140,12 +141,13 @@
 
     @pl.when(pl.program_id(0) == 0)
     def _():
-        for ref in (gw_in, gw_out, gain_q, gain_k, gain_n):
+        for ref in (gw_sum, gain_q, gain_k, gain_n):
             ref[...] = jnp.zeros_like(ref)
 
     upper = da_ref[0]
     grad_joined = dot_nt(upper, wo[...]).astype(LOW)
-    gw_out[...] += dot_tn(o_ref[0], upper)
+    wide = qr_ref.shape[-1]
+    gw_sum[:, 3 * wide :] += dot_tn(upper, o_ref[0])
     grads_q, grads_k, grads_v = ([], [], [])
     for head in range(qr_ref.shape[-1] // head_dim):
         span = slice(head * head_dim, (head + 1) * head_dim)
@@ -168,7 +170,6 @@
         gain_k[...] += head_gain_k
         grads_q.append(grad_q.astype(LOW))
         grads_k.append(grad_k.astype(LOW))
-    wide = qr_ref.shape[-1]
     grads = jnp.concatenate(grads_q + grads_k + grads_v, axis=-1)
     part = (
         dot_nt(grads[:, :wide], wq[...])
@@ -178,7 +179,11 @@
     normed = pk_ref[0, :rows]
     part_ref[0] = part.astype(LOW)
     gain_n[...] += jnp.sum(part * normed.astype(WIDE), axis=0, keepdims=True)
-    gw_in[...] += dot_tn(normed, grads)
+    gw_sum[:, : 3 * wide] += dot_tn(normed, grads)
+
+    @pl.when(pl.program_id(0) == pl.num_programs(0) - 1)
+    def _():
+        gw_ref[...] = gw_sum[...].astype(LOW)
 
 
 def attend_backward(upper, packets, kept, wq, wk, wv, wo, gq, gk, cos_tab, sin_tab):
@@ -187,8 +192,10 @@
     blocks = (upper, packets) + tuple(kept)
     fixed = (wq, wk, wv, wo, gq, gk, cos_tab, sin_tab)
     sums = tuple(
-        jax.ShapeDtypeStruct(shape, WIDE)
-        for shape in ((width, 3 * wide), wo.shape, gq.shape, gk.shape, (1, width))
+        jax.ShapeDtypeStruct(shape, kind)
+        for shape, kind in (
+            ((width, 4 * wide), LOW), (gq.shape, WIDE), (gk.shape, WIDE), ((1, width), WIDE)
+        )
     )
     return pl.pallas_call(
         attend_back_kernel,
@@ -196,6 +203,7 @@
         in_specs=[first_spec(array) for array in blocks] + [whole_spec(array) for array in fixed],
         out_specs=[first_spec(upper)] + [whole_spec(array) for array in sums],
         out_shape=(jax.ShapeDtypeStruct((count, rows, width), LOW),) + sums,
+        scratch_shapes=[pltpu.VMEM((width, 4 * wide), WIDE)],
         compiler_params=pltpu.CompilerParams(vmem_limit_bytes=VMEM_BYTES),
         cost_estimate=COST,
         name="attend_backward",
@@ -210,13 +218,71 @@
     return (slots == ranks).astype(LOW)
 
 
+class Trades:
+    def __init__(self, trades):
+        self.trades = trades
+        self.axes = sorted({(axis, size) for _, axis, size, _ in trades})
+        self.arrays = [array for array, _, _, _ in trades]
+        self.in_specs = [pl.BlockSpec(memory_space=pltpu.VMEM) for _ in trades]
+        self.out_specs = [pl.BlockSpec(memory_space=pl.ANY) for _ in trades]
+        self.out_shapes = [
+            jax.ShapeDtypeStruct(array.shape if pieces else (size,) + array.shape, array.dtype)
+            for array, _, size, pieces in trades
+        ]
+        self.scratch = [
+            pltpu.SemaphoreType.DMA((size,)) for _, _, size, _ in trades for _ in range(2)
+        ]
+
+    def bind(self, sources, targets, sems):
+        self.sources, self.targets, self.sems = (sources, targets, sems)
+
+    def device(self, axis, size, bits):
+        return {axis: lax.rem(lax.axis_index(axis) + bits, size)}
+
+    def copies(self):
+        for number, (_, axis, size, pieces) in enumerate(self.trades):
+            me = lax.axis_index(axis)
+            send, recv = (self.sems[2 * number], self.sems[2 * number + 1])
+            target = self.targets[number].at[me]
+            for bits in range(size):
+                source = self.sources[number]
+                source = source.at[lax.rem(me + bits, size)] if pieces else source
+                if bits == 0:
+                    yield pltpu.make_async_copy(source, target, send.at[0])
+                else:
+                    yield pltpu.make_async_remote_copy(
+                        source, target, send.at[bits], recv.at[bits],
+                        device_id=self.device(axis, size, bits),
+                        device_id_type=pl.DeviceIdType.MESH,
+                    )
+
+    def start(self):
+        barrier = pltpu.get_barrier_semaphore()
+        for axis, size in self.axes:
+            for bits in range(1, size):
+                pl.semaphore_signal(
+                    barrier, inc=1, device_id=self.device(axis, size, bits),
+                    device_id_type=pl.DeviceIdType.MESH,
+                )
+        pl.semaphore_wait(barrier, sum(size - 1 for _, size in self.axes))
+        for copy in self.copies():
+            copy.start()
+
+    def finish(self):
+        for copy in self.copies():
+            copy.wait()
+
+
 UNIT = 2
 
 
-def expert_kernel(row_counts, cot_counts, batch, ex_ref, wg, wu, wd, wr, *refs):
+def expert_kernel(row_counts, cot_counts, batch, trades, ex_ref, wg, wu, wd, wr, *refs):
     first, second = (len(row_counts), len(row_counts) + len(cot_counts))
     rows_in, cots_in = (refs[:first], refs[first:second])
-    x_ref, y_ref, m_ref, dg_ref, du_ref, dgate_ref, rows_buf, cots_buf, sems = refs[second:]
+    third, number = (second + len(trades.trades), len(trades.trades))
+    x_ref, y_ref, m_ref, dg_ref, du_ref, dgate_ref = refs[third : third + 6]
+    rows_buf, cots_buf, sems = refs[third + 6 + number : third + 9 + number]
+    trades.bind(refs[second:third], refs[third + 6 : third + 6 + number], refs[third + 9 + number :])
     steps, units = (sum(row_counts) // batch, batch // UNIT)
     turn = pl.program_id(0) * steps + pl.program_id(1)
     slot = lax.rem(turn, 2)
@@ -247,6 +313,8 @@
     @pl.when(turn == 0)
     def _():
         fetch(turn, slot)
+        if number:
+            trades.start()
 
     @pl.when(turn + 1 < pl.num_programs(0) * steps)
     def _():
@@ -285,9 +353,15 @@
         dg_ref[0, :, span] = (grad * up_act * (sig + silu * (1.0 - sig))).astype(LOW)
         du_ref[0, :, span] = (grad * silu).astype(LOW)
     dgate_ref[0] = jnp.broadcast_to(dgate, dgate_ref.shape[1:])
-
-
-def expert_acts(ids, rows, cots, wg, wu, wd, wr, batch=4):
+    if number:
+
+        @pl.when(turn == pl.num_programs(0) * steps - 1)
+        def _():
+            trades.finish()
+
+
+def expert_acts(ids, rows, cots, wg, wu, wd, wr, batch=4, trades=(), collective=None):
+    trades = Trades(trades)
     row_count, width = rows[0].shape[1:]
     row_counts, cot_counts = ([array.shape[0] for array in arrays] for arrays in (rows, cots))
     count = sum(row_counts)
@@ -308,7 +382,7 @@
     any_spec = pl.BlockSpec(memory_space=pl.ANY)
     columns = (width, width, hidden, hidden, hidden, 128)
     return pl.pallas_call(
-        functools.partial(expert_kernel, row_counts, cot_counts, batch),
+        functools.partial(expert_kernel, row_counts, cot_counts, batch, trades),
         grid=(own, count // batch),
         in_specs=[
             pl.BlockSpec(memory_space=pltpu.SMEM),
@@ -317,18 +391,24 @@
             weight_spec(wd),
             pl.BlockSpec(wr.shape, lambda e, i: (0, 0)),
         ]
-        + [any_spec] * (len(rows) + len(cots)),
-        out_specs=[act_spec(cols) for cols in columns],
-        out_shape=tuple(acts(cols) for cols in columns[:5]) + (acts(128, WIDE),),
+        + [any_spec] * (len(rows) + len(cots))
+        + trades.in_specs,
+        out_specs=[act_spec(cols) for cols in columns] + trades.out_specs,
+        out_shape=[acts(cols) for cols in columns[:5]] + [acts(128, WIDE)] + trades.out_shapes,
         scratch_shapes=[
             pltpu.VMEM((2, batch) + rows[0].shape[1:], LOW),
             pltpu.VMEM((2, batch) + cots[0].shape[1:], LOW),
             pltpu.SemaphoreType.DMA((2, 2, batch // UNIT)),
-        ],
-        compiler_params=pltpu.CompilerParams(vmem_limit_bytes=VMEM_BYTES),
+        ]
+        + trades.scratch,
+        compiler_params=pltpu.CompilerParams(
+            vmem_limit_bytes=VMEM_BYTES,
+            collective_id=collective,
+            has_side_effects=collective is not None,
+        ),
         cost_estimate=COST,
         name="expert_acts",
-    )(ids, wg, wu, wd, wr, *rows, *cots)
+    )(ids, wg, wu, wd, wr, *rows, *cots, *trades.arrays)
 
 
 def pull_kernel(ex_ref, rows_ref, cot_ref, dg_ref, du_ref, dgate_ref, wg, wu, wr, part_ref, router):
@@ -363,7 +443,7 @@
             grad_logits += at_rows * prob * (chosen - probs)
         low_logits = grad_logits.astype(LOW)
         part_ref[seq] = (total + dot_nt(low_logits, wr[...])).astype(LOW)
-        router[...] += dot_tn(rows_ref[seq], low_logits)
+        router[...] += dot_tn(low_logits, rows_ref[seq])
 
 
 def mix_kernel(ex_ref, cot_ref, m_ref, wd, part_ref):
@@ -404,15 +484,17 @@
     )(ids, *by_seq, cots, *by_slot, *fixed)
 
 
-def weight_grad(lefts, rights):
+def weight_grad(lefts, rights, start=None):
     own, _, left_cols = lefts[0].shape
     right_cols = rights[0].shape[-1]
     sets = len(lefts)
     left_tile, right_tile = (min(512, left_cols), min(1024, right_cols))
 
     def kernel(*refs):
-        refs[2 * sets][0] = sum(dot_tn(refs[i][0], refs[sets + i][0]) for i in range(sets))
-
+        total = sum(dot_tn(refs[i][0], refs[sets + i][0]) for i in range(sets))
+        refs[-1][0] = total if start is None else total + refs[2 * sets][0]
+
+    out_spec = pl.BlockSpec((1, left_tile, right_tile), lambda e, r, l: (e, l, r))
     return pl.pallas_call(
         kernel,
         grid=(own, right_cols // right_tile, left_cols // left_tile),
@@ -423,13 +505,15 @@
         + [
             pl.BlockSpec((1, array.shape[1], right_tile), lambda e, r, l: (e, 0, r))
             for array in rights
-        ],
-        out_specs=pl.BlockSpec((1, left_tile, right_tile), lambda e, r, l: (e, l, r)),
+        ]
+        + [out_spec] * (start is not None),
+        out_specs=out_spec,
         out_shape=jax.ShapeDtypeStruct((own, left_cols, right_cols), WIDE),
+        input_output_aliases={} if start is None else {2 * sets: 0},
         compiler_params=pltpu.CompilerParams(vmem_limit_bytes=VMEM_BYTES),
         cost_estimate=COST,
         name="weight_grad",
-    )(*lefts, *rights)
+    )(*lefts, *rights, *([] if start is None else [start]))
 
 
 CHUNKS = 4
@@ -909,7 +993,6 @@
             replicas, groups, packet, cot_packet, tokens, *heads, gain_moe.reshape(1, -1)
         )
         kept, (hidden, rows_all, cots), far_cots = (kept[:4], kept[4:7], kept[7:])
-        plain_mid, scale_mid = rms_parts(hidden)
         pairs = rows_all.reshape((groups // 2, 2) + rows_all.shape[1:])
         core = lax.axis_index("shard") % 2
         near = [
@@ -927,28 +1010,27 @@
 
     acts = [expert_acts(ids, [rows_all], [cots], w_gate, w_up, w_down, w_router)]
     if share:
-        over = [flip_replica(near[0], bits) for bits in (1, 2)]
-        acts, over = after((acts, over))
-        over_x, over_y = ([over[0]], [over[1]])
+        early, late = ([flip_replica(part, bits) for bits in (1, 2)] for part in near)
+        acts, early = after((acts, early))
     _, _, gated, grad_gate_act, grad_up_act, dgates = acts[0]
-    router_shape = (jax.ShapeDtypeStruct(w_router.shape, WIDE),)
+    router_shape = (jax.ShapeDtypeStruct(w_router.shape[::-1], WIDE),)
     pull_part, grad_router = spread_call(
         pull_kernel, "expert_pull", ids, (rows_all,), cots,
         (grad_gate_act, grad_up_act, dgates), (w_gate, w_up, w_router), router_shape,
     )
     if share:
-        over = [flip_replica(near[1], bits) for bits in (1, 2)]
-        pull_part, over = after((pull_part, over))
-        over_x, over_y = (over_x + [over[0]], over_y + [over[1]])
+        early_flipped = [flip_shard(values, 1) for values in early]
+        pull_part, late, early_flipped = after((pull_part, late, early_flipped))
     grad_moe_in = scatter_sum(pull_part)
     gated, pull_part = after((gated, pull_part))
     if share:
-        diagonal = [flip_replica(over_x[0], 2), flip_replica(over_y[1], 1)]
-        flipped = [flip_shard(values, 1) for values in over_x + over_y]
-        near, pull_part = after((over_x + over_y, pull_part))
+        diagonal = [flip_replica(early[0], 2), flip_replica(late[1], 1)]
+        late_flipped = [flip_shard(values, 1) for values in late]
+        near, pull_part = after(([early[0], late[0], early[1], late[1]], pull_part))
         acts.append(expert_acts(ids, near, far_cots[0:2], w_gate, w_up, w_down, w_router))
-        acts, diagonal, flipped = after((acts, diagonal, flipped))
+        acts, diagonal, late_flipped = after((acts, diagonal, late_flipped))
         gated, acts = after((gated, acts))
+        flipped = [early_flipped[0], late_flipped[0], early_flipped[1], late_flipped[1]]
         diagonal_flipped = [flip_shard(values, 1) for values in diagonal]
     (mix_part,) = spread_call(mix_kernel, "expert_mix", ids, (), cots, (gated,), (w_down,), ())
     if share:
@@ -956,89 +1038,87 @@
         grad_moe_in, mix_part = after((grad_moe_in, mix_part))
 
     grad_out = cot_low.astype(WIDE)
+    if share:
+        hidden, grad_moe_in = after((hidden, grad_moe_in))
+        plain_mid, scale_mid = rms_parts(hidden)
     grad_hidden = grad_out + rms_back(plain_mid, scale_mid, gain_moe, grad_moe_in)
     gain_moe_sum = jnp.sum(grad_moe_in * plain_mid, axis=0)
     branch_low = grad_hidden.astype(LOW)
     upper = lax.all_gather(branch_low, "shard", axis=0)
     if share:
-        rest, branch_low = after((diagonal + flipped + diagonal_flipped, branch_low))
-        rest_cots = [far_cots[2], far_cots[3], far_cots[4], far_cots[5]]
-        acts.append(expert_acts(ids, rest, rest_cots, w_gate, w_up, w_down, w_router))
-        upper, acts = after((upper, acts))
+        acts, branch_low = after((acts, branch_low))
+        started = [
+            weight_grad([act[left] for act in acts], [act[right] for act in acts])
+            for left, right in ((0, 3), (0, 4), (2, 1))
+        ]
+        upper, started = after((upper, started))
     mix_part, upper = after((mix_part, upper))
     mixture = scatter_sum(mix_part)
-    part, gw_in, gw_out, sum_q, sum_k, sum_n = attend_backward(upper, packets, kept, *heads)
+    part, gw_low, sum_q, sum_k, sum_n = attend_backward(upper, packets, kept, *heads)
 
     def sets(place):
         return [act[place] for act in acts]
 
-    def exchange(values, axis, count):
-        flip = flip_replica if axis == "rep" else flip_shard
-        return [values] + [flip(values, bits) for bits in range(1, count)]
-
-    def in_order(found, axis):
-        order = lax.axis_index(axis) ^ jnp.arange(len(found), dtype=jnp.int32)
-        return jnp.take(jnp.stack(found), order, axis=0)
-
     small = jnp.concatenate(
-        [sum_n[0] / gain_attn, sum_q[0], sum_k[0], gain_moe_sum, grad_router.reshape(-1)]
+        [
+            grad_router,
+            gain_moe_sum[None],
+            sum_n / gain_attn,
+            jnp.pad(
+                jnp.concatenate([sum_q, sum_k], axis=1), ((0, 0), (0, width - 2 * head_dim))
+            ),
+            jnp.zeros((5, width), WIDE),
+        ]
     )
     if share:
-        me = lax.axis_index("rep")
-
-        def quarters(values):
-            return values.astype(LOW).reshape((replicas, -1) + values.shape[1:])
-
-        def traded(values):
-            pieces = quarters(values)
-            found = [
-                lax.dynamic_index_in_dim(pieces, me ^ bits, axis=0, keepdims=False)
-                for bits in range(replicas)
-            ]
-            return found[:1] + [flip_replica(found[bits], bits) for bits in range(1, replicas)]
-
-        trades = [traded(gw_in), traded(gw_out), exchange(small, "rep", replicas)]
-        acts, gw_in = after((acts, gw_in))
-        grad_gate_w = weight_grad(sets(0), sets(3))
-        grad_gate_w, trades, part, mixture = after((grad_gate_w, trades, part, mixture))
+        experts = (w_gate, w_up, w_down, w_router)
+        pieces = gw_low.reshape((replicas, -1) + gw_low.shape[1:])
+        *act, traded, smalls = expert_acts(
+            ids, flipped, far_cots[3:5], *experts,
+            trades=((pieces, "rep", replicas, True), (small, "rep", replicas, False)), collective=1,
+        )
+        act, traded, smalls, part, mixture = after((act, traded, smalls, part, mixture))
+        acts = [act]
         grad_normed = scatter_sum(part)
-        lows = [sum(piece.astype(WIDE) for piece in trade).astype(LOW) for trade in trades[:2]]
-        small = jnp.sum(in_order(trades[2], "rep"), axis=0)
-        acts, lows, small = after((acts, lows, small))
-        shared = [exchange(low, "rep", replicas) for low in lows] + [exchange(small, "shard", groups)]
-        grad_up_w = weight_grad(sets(0), sets(4))
-        grad_up_w, shared, acts = after((grad_up_w, shared, acts))
-        sum_in, sum_out = (
-            in_order(pieces, "rep").reshape(values.shape).astype(WIDE)
-            for pieces, values in zip(shared[:2], (gw_in, gw_out))
-        )
-        small = jnp.sum(in_order(shared[2], "shard"), axis=0)
-        grad_down = weight_grad(sets(2), sets(1))
+        low = jnp.sum(traded.astype(WIDE), axis=0).astype(LOW)
+        small = jnp.sum(smalls, axis=0)
+        *act, found, smalls = expert_acts(
+            ids, diagonal + diagonal_flipped, [far_cots[2], far_cots[5]], *experts,
+            trades=((low, "rep", replicas, False), (small, "shard", groups, False)), collective=2,
+        )
+        acts.append(act)
+        gw_sum = found.reshape(gw_low.shape)
+        small = jnp.sum(smalls, axis=0)
+        grad_gate_w, grad_up_w, grad_down = (
+            weight_grad(sets(left), sets(right), begun)
+            for (left, right), begun in zip(((0, 3), (0, 4), (2, 1)), started)
+        )
     else:
         grad_normed = scatter_sum(part)
         over_reps = lax.psum(
-            (gw_in.astype(LOW), gw_out.astype(LOW))
+            (gw_low,)
             + tuple(
                 weight_grad(sets(left), sets(right)).astype(LOW)
                 for left, right in ((0, 3), (0, 4), (2, 1))
             ),
             "rep",
         )
-        sum_in, sum_out, grad_gate_w, grad_up_w, grad_down = (
-            values.astype(WIDE) for values in over_reps
-        )
+        gw_sum = over_reps[0]
+        grad_gate_w, grad_up_w, grad_down = (values.astype(WIDE) for values in over_reps[1:])
         small = lax.psum(small, ("rep", "shard"))
+    grads_q, grads_k, grads_v, grads_o = (
+        gw_sum[:, i * wide : (i + 1) * wide].astype(WIDE) for i in range(4)
+    )
+    grad_router = small[:expert_count].T
+    grad_gain_moe, grad_gain_attn = (small[expert_count], small[expert_count + 1])
+    grad_gain_query, grad_gain_key = (
+        small[expert_count + 2, i * head_dim : (i + 1) * head_dim] for i in range(2)
+    )
     output = (hidden + mixture).astype(LOW)
     grad_input = grad_hidden + rms_back(plain_in, scale_in, gain_attn, grad_normed)
-    edges = [0, width, width + head_dim, width + 2 * head_dim, 2 * width + 2 * head_dim]
-    grad_gain_attn, grad_gain_query, grad_gain_key, grad_gain_moe = (
-        small[a:b] for a, b in zip(edges[:-1], edges[1:])
-    )
-    grad_router = small[edges[-1] :].reshape(w_router.shape)
-
     return (
         output, grad_input, grad_gain_attn, grad_gain_query, grad_gain_key,
-        sum_in[:, :wide], sum_in[:, wide : 2 * wide], sum_in[:, 2 * wide :], sum_out,
+        grads_q, grads_k, grads_v, grads_o.T,
         grad_gain_moe, grad_router, grad_gate_w, grad_up_w, grad_down,
     )
 

time: 1040 us -> 928 us (0.89)
  waiting for transfers between devices: 136 us -> 5.56 us
  Pallas kernels: 761 us -> 827 us
  local copies, waits for them, and re-layouts: 46.8 us -> 20.6 us
  starting transfers between devices: 28 us -> 7.9 us
    ppermute x21 -> x6, waiting for transfers between devices: 86.3 us -> 0.02 us  [flip_replica(): return lax.ppermute(values, 'rep', [(i, i ^ bits) for i in range(replicas)])]
    ppermute x13 -> x6, waiting for transfers between devices: 49.7 us -> 0.02 us  [flip_shard(): return lax.ppermute(values, 'shard', [(i, i ^ bits) for i in range(groups)])]
    pallas_call x3 -> x6, Pallas kernels: 151 us -> 186 us  [weight_grad(): pl.pallas_call(kernel, grid=(own, right_cols // right_tile, left_cols //...]
    pallas_call x3 -> x4, Pallas kernels: 210 us -> 239 us  [expert_acts(): pl.pallas_call(functools.partial(expert_kernel, row_counts, cot_counts, b...]
    ppermute x21 -> x6, starting transfers between devices: 24.1 us -> 6.12 us  [flip_replica(): return lax.ppermute(values, 'rep', [(i, i ^ bits) for i in range(replicas)])]
    another operation x13 -> x0, local copies, waits for them, and re-layouts: 11.3 us -> none  [in_order(): return jnp.take(jnp.stack(found), order, axis=0)]
  transfers between devices with their start and end apart: 38 -> 16, of which waited for: 7 -> 1; matrix products, arithmetic and copies ran while one was open for 5% -> 2% of each run, Pallas kernels for 46% -> 58%
where the time goes in v3:
time: 928 us; the launch traced here: 912 us
  Pallas kernels  827 us (89%)
  other arithmetic  36.5 us (4%)
  local copies, waits for them, and re-layouts  20.6 us (2%)
  between operations  15.1 us (2%)
    pallas_call x1, Pallas kernels, front(): pl.pallas_call(functools.partial(front_kernel, replicas, groups), in_spec...  293 us
    pallas_call x4, Pallas kernels, expert_acts(): pl.pallas_call(functools.partial(expert_kernel, row_counts, cot_counts, b...  239 us
    pallas_call x6, Pallas kernels, weight_grad(): pl.pallas_call(kernel, grid=(own, right_cols // right_tile, left_cols //...  186 us
    pallas_call x2, Pallas kernels, spread_call(): pl.pallas_call(kernel, grid=(count // batch,), in_specs=[pl.BlockSpec(mem...  61.3 us
    pallas_call x1, Pallas kernels, attend_backward(): pl.pallas_call(attend_back_kernel, grid=(count,), in_specs=[first_spec(ar...  46.4 us
  transfers between devices with their start and end apart: 16, of which 1 were waited for; matrix products, arithmetic and copies ran while one was open for 2% of the time, Pallas kernels for 58%

profile of v3, /device:TPU:0, one launch (start us, length us, event | category | flops | bytes accessed | tf_op | source)
XLA Modules:
  0.0 912.5 jit_solution(11711055560722290222)
XLA Ops:
  7.3 0.5 fusion.16
  8.5 1.5 fusion.9
  10.0 0.7 fusion.15
  10.7 0.1 fusion.12
  10.9 1.4 broadcast_select_fusion
  12.3 0.3 fusion.4
  12.6 0.8 pad_maximum_fusion
  13.4 1.6 fusion.11
  15.0 293.3 %front.1 = (bf16[8,272,2048]{2,1,0:T(8,128)(2,1)}, f32[8,256,256]{2,1,0:T(8,128)}, f32[8,256,256]{2,1,0:T(8,128)}, bf16[8,256,256]{2,1,0:T(8,128)(2,1)}, bf16[8,...) custom-call(bf16[272,2048]{1,0:T(8,128)(2,1)} %get-tuple-element.277, ...), custom_call_target="tpu_custom_call" | custom-call | flops 1048576 | bytes 65536 | tf_op jit(solution)/shard_map/front/pallas_call | solution.py:905
  308.3 6.1 fusion.19
  314.4 3.3 dynamic-slice_bitcast_fusion
  317.8 1.5 dynamic-slice_bitcast_fusion.1
  319.2 0.6 collective-permute-start
  319.8 1.5 collective-permute-start.1
  321.3 1.4 collective-permute-start.2
  322.7 0.6 collective-permute-start.3
  323.3 1.0 copy.44.wr
  324.3 0.5 iota_add_fusion.ex_ref
  324.8 56.8 %expert_acts.4 = (bf16[2,1152,2048]{2,1,0:T(8,128)(2,1)}, bf16[2,1152,2048]{2,1,0:T(8,128)(2,1)}, bf16[2,1152,1024]{2,1,0:T(8,128)(2,1)}, bf16[2,1152,1024]{2,1,...) custom-call(s32[2]{0:T(128)} %iota_add_fusion.ex_ref, bf16[2,2048,1024]{2,1,0:T(8,128)(2,1)} %wg.9, ...), custom_call_target="tpu_custom_call" | custom-call | flops 1048576 | bytes 65536 | tf_op jit(solution)/shard_map/expert_acts/pallas_call | solution.py:384
  381.7 0.1 collective-permute-start.4
  381.7 0.5 collective-permute-start.5
  382.2 40.7 %expert_pull.1 = (bf16[8,256,2048]{2,1,0:T(8,128)(2,1)}, f32[16,2048]{1,0:T(8,128)}) custom-call(s32[2]{0:T(128)} %iota_add_fusion.ex_ref, bf16[8,256,2048]{2,1,0:T(8,128)(2,1)} %get-tuple-element.140.refs_0_.rows_ref, bf16[8,272,2048]{2,1,0:T(8,128)(2,1)} %get-tuple-element.141.refs_1_.cot_ref, bf16[2,1152,1024]{2,1,0:T(8,128)(2,1)} %get-tuple-element.210.dg_ref.refs_2_, ...), custom_call_target="tpu_custom_call" | custom-call | flops 1048576 | bytes 65536 | tf_op jit(solution)/shard_map/expert_pull/pallas_call | solution.py:471
  423.0 1.3 copy-done.8
  424.3 1.5 collective-permute-start.6
  425.7 0.6 collective-permute-start.7
  426.3 0.5 collective-permute-start.9
  426.8 55.7 %expert_acts.5 = (bf16[2,1152,2048]{2,1,0:T(8,128)(2,1)}, bf16[2,1152,2048]{2,1,0:T(8,128)(2,1)}, bf16[2,1152,1024]{2,1,0:T(8,128)(2,1)}, bf16[2,1152,1024]{2,1,...) custom-call(s32[2]{0:T(128)} %iota_add_fusion.ex_ref, bf16[2,2048,1024]{2,1,0:T(8,128)(2,1)} %wg.9, ...), custom_call_target="tpu_custom_call" | custom-call | flops 1048576 | bytes 65536 | tf_op jit(solution)/shard_map/expert_acts/pallas_call | solution.py:384
  482.6 0.1 collective-permute-start.10
  482.7 0.5 collective-permute-start.11
  483.2 0.7 copy-done.7
  483.9 20.6 %expert_mix.1 = bf16[8,256,2048]{2,1,0:T(8,128)(2,1)} custom-call(s32[2]{0:T(128)} %iota_add_fusion.ex_ref, bf16[8,272,2048]{2,1,0:T(8,128)(2,1)} %get-tuple-element.141.refs_1_.cot_ref, bf16[2,1152,1024]{2,1,0:T(8,128)(2,1)} %get-tuple-element.214.m_ref.refs_0_, bf16[2,1024,2048]{2,1,0:T(8,128)(2,1)} %wd.9), custom_call_target="tpu_custom_call" | custom-call | flops 1048576 | bytes 65536 | tf_op jit(solution)/shard_map/expert_mix/pallas_call | solution.py:471
  504.6 5.4 reduce-scatter.4.cloned.1.call-done
  510.0 1.5 convert_element_type.52
  511.5 0.2 multiply_reduce_fusion.2
  511.8 0.7 multiply_reduce_fusion
  512.4 0.4 copy-done.1
  512.8 0.7 copy-done.5
  513.5 1.7 fusion.18
  515.2 0.0 reduce-scatter.6.cloned.1.call-start
  515.3 28.9 %weight_grad.7.refs_4_ = f32[2,2048,1024]{2,1,0:T(8,128)} custom-call(bf16[2,1152,2048]{2,1,0:T(8,128)(2,1)} %get-tuple-element.208.refs_0_, bf16[2,1152,2048]{2,1,0:T(8,128)(2,1)} %get-tuple-element.209.refs_1_, bf16[2,1152,1024]{2,1,0:T(8,128)(2,1)} %get-tuple-element.212.du_ref.refs_2_, bf16[2,1152,1024]{2,1,0:T(8,128)(2,1)} %get-tuple-element.213.refs_3_), custom_call_target="tpu_custom_call" | custom-call | flops 1048576 | bytes 65536 | tf_op jit(solution)/shard_map/weight_grad/pallas_call | solution.py:498
  544.2 28.9 %weight_grad.6.refs_4_ = f32[2,2048,1024]{2,1,0:T(8,128)} custom-call(bf16[2,1152,2048]{2,1,0:T(8,128)(2,1)} %get-tuple-element.208.refs_0_, bf16[2,1152,2048]{2,1,0:T(8,128)(2,1)} %get-tuple-element.209.refs_1_, bf16[2,1152,1024]{2,1,0:T(8,128)(2,1)} %get-tuple-element.210.dg_ref.refs_2_, bf16[2,1152,1024]{2,1,0:T(8,128)(2,1)} %get-tuple-element.211.refs_3_), custom_call_target="tpu_custom_call" | custom-call | flops 1048576 | bytes 65536 | tf_op jit(solution)/shard_map/weight_grad/pallas_call | solution.py:498
  573.1 30.6 %weight_grad.8.refs_4_ = f32[2,1024,2048]{2,1,0:T(8,128)} custom-call(bf16[2,1152,1024]{2,1,0:T(8,128)(2,1)} %get-tuple-element.214.m_ref.refs_0_, bf16[2,1152,1024]{2,1,0:T(8,128)(2,1)} %get-tuple-element.215.refs_1_, bf16[2,1152,2048]{2,1,0:T(8,128)(2,1)} %get-tuple-element.216.refs_2_, bf16[2,1152,2048]{2,1,0:T(8,128)(2,1)} %get-tuple-element.217.refs_3_), custom_call_target="tpu_custom_call" | custom-call | flops 1048576 | bytes 65536 | tf_op jit(solution)/shard_map/weight_grad/pallas_call | solution.py:498
  603.8 46.4 %attend_backward.1 = (bf16[8,256,2048]{2,1,0:T(8,128)(2,1)}, bf16[2048,1024]{1,0:T(8,128)(2,1)}, f32[1,128]{1,0:T(1,128)}, f32[1,128]{1,0:T(1,128)}, f32[1,2048]{1,0:T(1,128)}) custom-call(bf16[8,256,2048]{2,1,0:T(8,128)(2,1)} %bitcast.40, bf16[8,272,2048]{2,1,0:T(8,128)(2,1)} %get-tuple-element.220.pk_ref, f32[8,256,256]{2,1,0:T(8,128)} %get-tuple-element.221.qr_ref, ...), custom_call_target="tpu_custom_call" | custom-call | flops 1048576 | bytes 65536 | tf_op jit(solution)/shard_map/attend_backward/pallas_call | solution.py:200
  650.2 0.7 div.18
  650.9 0.7 fusion.17
  651.6 1.3 concatenate.27.refs_7_
  653.0 64.9 %expert_acts.6 = (bf16[2,1152,2048]{2,1,0:T(8,128)(2,1)}, bf16[2,1152,2048]{2,1,0:T(8,128)(2,1)}, bf16[2,1152,1024]{2,1,0:T(8,128)(2,1)}, bf16[2,1152,1024]{2,1,...) custom-call(s32[2]{0:T(128)} %iota_add_fusion.ex_ref, ...), custom_call_target="tpu_custom_call" | custom-call | flops 1048576 | bytes 65536 | tf_op jit(solution)/shard_map/expert_acts/pallas_call | solution.py:384
  717.9 2.8 convert_element_type.55
  720.8 1.1 copy-done.9
  721.9 0.7 reduce_sum.81.refs_7_
  722.6 4.4 reduce_sum.80.refs_6_
  727.0 61.9 %expert_acts.7 = (bf16[2,1152,2048]{2,1,0:T(8,128)(2,1)}, bf16[2,1152,2048]{2,1,0:T(8,128)(2,1)}, bf16[2,1152,1024]{2,1,0:T(8,128)(2,1)}, bf16[2,1152,1024]{2,1,...) custom-call(s32[2]{0:T(128)} %iota_add_fusion.ex_ref, ...), custom_call_target="tpu_custom_call" | custom-call | flops 1048576 | bytes 65536 | tf_op jit(solution)/shard_map/expert_acts/pallas_call | solution.py:384
  788.9 5.1 fusion.20
  793.9 1.4 copy.52
  795.4 1.5 reduce_sum.82
  796.9 31.3 %weight_grad.10 = f32[2,2048,1024]{2,1,0:T(8,128)} custom-call(bf16[2,1152,2048]{2,1,0:T(8,128)(2,1)} %get-tuple-element.249.refs_0_, bf16[2,1152,2048]{2,1,0:T(8,128)(2,1)} %get-tuple-element.250.refs_1_, bf16[2,1152,1024]{2,1,0:T(8,128)(2,1)} %get-tuple-element.254.refs_2_, ...), custom_call_target="tpu_custom_call", output_to_operand_aliasing={{}: (4, {})} | custom-call | flops 1048576 | bytes 65536 | tf_op jit(solution)/shard_map/weight_grad/pallas_call | solution.py:498
  828.1 31.4 %weight_grad.9 = f32[2,2048,1024]{2,1,0:T(8,128)} custom-call(bf16[2,1152,2048]{2,1,0:T(8,128)(2,1)} %get-tuple-element.249.refs_0_, bf16[2,1152,2048]{2,1,0:T(8,128)(2,1)} %get-tuple-element.250.refs_1_, bf16[2,1152,1024]{2,1,0:T(8,128)(2,1)} %get-tuple-element.251.refs_2_, ...), custom_call_target="tpu_custom_call", output_to_operand_aliasing={{}: (4, {})} | custom-call | flops 1048576 | bytes 65536 | tf_op jit(solution)/shard_map/weight_grad/pallas_call | solution.py:498
  859.5 35.2 %weight_grad.11 = f32[2,1024,2048]{2,1,0:T(8,128)} custom-call(bf16[2,1152,1024]{2,1,0:T(8,128)(2,1)} %get-tuple-element.257.refs_0_, bf16[2,1152,1024]{2,1,0:T(8,128)(2,1)} %get-tuple-element.258.refs_1_, bf16[2,1152,2048]{2,1,0:T(8,128)(2,1)} %get-tuple-element.259.refs_2_, ...), custom_call_target="tpu_custom_call", output_to_operand_aliasing={{}: (4, {})} | custom-call | flops 1048576 | bytes 65536 | tf_op jit(solution)/shard_map/weight_grad/pallas_call | solution.py:498
  894.7 0.5 slice_bitcast_fusion.1
  895.2 0.6 fusion.21
  895.8 0.7 slice_bitcast_fusion
  896.5 2.8 convert_bitcast_fusion
  899.3 1.9 fusion.5
  901.2 4.4 fusion.8
  (57 shorter events, 0.3 us)
Async XLA Ops:
  7.2 5.1 copy-start.3
  7.2 5.1 copy-start.11
  7.2 502.8 %reduce-scatter.4.cloned.1.call-start = ((), (), s32[]{:S(2)}) async-start(), calls=%async_computation.3 | async-start | bytes 9437184 | tf_op jit(solution)/shard_map/reduce_scatter | solution.py:971
  10.0 2.6 copy-start.14
  314.4 3.3 copy-start.6
  317.8 5.5 copy-start.13
  319.2 62.4 %collective-permute-start = (bf16[2,256,2048]{2,1,0:T(8,128)(2,1)}, bf16[2,256,2048]{2,1,0:T(8,128)(2,1)}, u32[]{:S(2)}, u32[]{:S(2)}) collective-permute-start(bf16[2,256,2048]{2,1,0:T(8,128)(2,1)} %dynamic-slice_bitcast_fusion.1), channel_id=1, source_target_pairs={{0,8},{8,0},{16,24},{24,16},{1,9},{9,1},{17,25},{25,17},{2,10},{10... | collective-permute-start | bytes 6291464 | tf_op jit(solution)/shard_map/ppermute | solution.py:965
  319.8 61.9 %collective-permute-start.1 = (bf16[2,256,2048]{2,1,0:T(8,128)(2,1)}, bf16[2,256,2048]{2,1,0:T(8,128)(2,1)}, u32[]{:S(2)}, u32[]{:S(2)}) collective-permute-start(bf16[2,256,2048]{2,1,0:T(8,128)(2,1)} %dynamic-slice_bitcast_fusion.1), channel_id=1, source_target_pairs={{0,16},{8,24},{16,0},{24,8},{1,17},{9,25},{17,1},{25,9},{2,18},{10... | collective-permute-start | bytes 6291464 | tf_op jit(solution)/shard_map/ppermute | solution.py:965
  321.3 101.6 %collective-permute-start.2 = (bf16[2,256,2048]{2,1,0:T(8,128)(2,1)}, bf16[2,256,2048]{2,1,0:T(8,128)(2,1)S(1)}, u32[]{:S(2)}, u32[]{:S(2)}) collective-permute-start(bf16[2,256,2048]{2,1,0:T(8,128)(2,1)} %dynamic-slice_bitcast_fusion), channel_id=1, source_target_pairs={{0,8},{8,0},{16,24},{24,16},{1,9},{9,1},{17,25},{25,17},{2,10},{10... | collective-permute-start | bytes 6291464 | tf_op jit(solution)/shard_map/ppermute | solution.py:965
  322.7 100.2 %collective-permute-start.3 = (bf16[2,256,2048]{2,1,0:T(8,128)(2,1)}, bf16[2,256,2048]{2,1,0:T(8,128)(2,1)}, u32[]{:S(2)}, u32[]{:S(2)}) collective-permute-start(bf16[2,256,2048]{2,1,0:T(8,128)(2,1)} %dynamic-slice_bitcast_fusion), channel_id=1, source_target_pairs={{0,16},{8,24},{16,0},{24,8},{1,17},{9,25},{17,1},{25,9},{2,18},{10... | collective-permute-start | bytes 6291464 | tf_op jit(solution)/shard_map/ppermute | solution.py:965
  381.7 41.3 %collective-permute-start.4 = (bf16[2,256,2048]{2,1,0:T(8,128)(2,1)}, bf16[2,256,2048]{2,1,0:T(8,128)(2,1)}, u32[]{:S(2)}, u32[]{:S(2)}) collective-permute-start(bf16[2,256,2048]{2,1,0:T(8,128)(2,1)} %collective-permute-done.refs_0_), channel_id=1, source_target_pairs={{0,1},{1,0},{2,3},{3,2},{4,5},{5,4},{6,7},{7,6},{8,9},{9,8},{10,11... | collective-permute-start | bytes 6291464 | tf_op jit(solution)/shard_map/ppermute | solution.py:968
  381.7 41.2 %collective-permute-start.5 = (bf16[2,256,2048]{2,1,0:T(8,128)(2,1)}, bf16[2,256,2048]{2,1,0:T(8,128)(2,1)}, u32[]{:S(2)}, u32[]{:S(2)}) collective-permute-start(bf16[2,256,2048]{2,1,0:T(8,128)(2,1)} %collective-permute-done.1.refs_2_), channel_id=1, source_target_pairs={{0,1},{1,0},{2,3},{3,2},{4,5},{5,4},{6,7},{7,6},{8,9},{9,8},{10,11... | collective-permute-start | bytes 6291464 | tf_op jit(solution)/shard_map/ppermute | solution.py:968
  422.9 1.3 copy-start.8
  424.3 179.5 %all-gather.3.cloned.1.call-start = ((), (), s32[]{:S(2)}) async-start(), calls=%async_computation.6 | async-start | bytes 9437184 | tf_op jit(solution)/shard_map/all_gather | solution.py:1047
  424.3 58.3 %collective-permute-start.6 = (bf16[2,256,2048]{2,1,0:T(8,128)(2,1)}, bf16[2,256,2048]{2,1,0:T(8,128)(2,1)}, u32[]{:S(2)}, u32[]{:S(2)}) collective-permute-start(bf16[2,256,2048]{2,1,0:T(8,128)(2,1)} %collective-permute-done.refs_0_), channel_id=1, source_target_pairs={{0,16},{8,24},{16,0},{24,8},{1,17},{9,25},{17,1},{25,9},{2,18},{10... | collective-permute-start | bytes 6291464 | tf_op jit(solution)/shard_map/ppermute | solution.py:965
  425.7 56.9 %collective-permute-start.7 = (bf16[2,256,2048]{2,1,0:T(8,128)(2,1)}, bf16[2,256,2048]{2,1,0:T(8,128)(2,1)}, u32[]{:S(2)}, u32[]{:S(2)}) collective-permute-start(bf16[2,256,2048]{2,1,0:T(8,128)(2,1)} %collective-permute-done.3.refs_3_), channel_id=1, source_target_pairs={{0,8},{8,0},{16,24},{24,16},{1,9},{9,1},{17,25},{25,17},{2,10},{10... | collective-permute-start | bytes 6291464 | tf_op jit(solution)/shard_map/ppermute | solution.py:965
  426.3 56.3 %collective-permute-start.8 = (bf16[2,256,2048]{2,1,0:T(8,128)(2,1)}, bf16[2,256,2048]{2,1,0:T(8,128)(2,1)S(1)}, u32[]{:S(2)}, u32[]{:S(2)}) collective-permute-start(bf16[2,256,2048]{2,1,0:T(8,128)(2,1)} %copy-done.8), channel_id=1, source_target_pairs={{0,1},{1,0},{2,3},{3,2},{4,5},{5,4},{6,7},{7,6},{8,9},{9,8},{10,11... | collective-permute-start | bytes 6291464 | tf_op jit(solution)/shard_map/ppermute | solution.py:968
  426.3 56.3 %collective-permute-start.9 = (bf16[2,256,2048]{2,1,0:T(8,128)(2,1)}, bf16[2,256,2048]{2,1,0:T(8,128)(2,1)}, u32[]{:S(2)}, u32[]{:S(2)}) collective-permute-start(bf16[2,256,2048]{2,1,0:T(8,128)(2,1)} %collective-permute-done.3.refs_3_), channel_id=1, source_target_pairs={{0,1},{1,0},{2,3},{3,2},{4,5},{5,4},{6,7},{7,6},{8,9},{9,8},{10,11... | collective-permute-start | bytes 6291464 | tf_op jit(solution)/shard_map/ppermute | solution.py:968
  482.6 1.3 copy-start.7
  482.6 21.9 %collective-permute-start.10 = (bf16[2,256,2048]{2,1,0:T(8,128)(2,1)}, bf16[2,256,2048]{2,1,0:T(8,128)(2,1)}, u32[]{:S(2)}, u32[]{:S(2)}) collective-permute-start(bf16[2,256,2048]{2,1,0:T(8,128)(2,1)} %collective-permute-done.6.refs_0_), channel_id=1, source_target_pairs={{0,1},{1,0},{2,3},{3,2},{4,5},{5,4},{6,7},{7,6},{8,9},{9,8},{10,11... | collective-permute-start | bytes 6291464 | tf_op jit(solution)/shard_map/ppermute | solution.py:968
  482.7 21.9 %collective-permute-start.11 = (bf16[2,256,2048]{2,1,0:T(8,128)(2,1)}, bf16[2,256,2048]{2,1,0:T(8,128)(2,1)}, u32[]{:S(2)}, u32[]{:S(2)}) collective-permute-start(bf16[2,256,2048]{2,1,0:T(8,128)(2,1)} %collective-permute-done.7.refs_1_), channel_id=1, source_target_pairs={{0,1},{1,0},{2,3},{3,2},{4,5},{5,4},{6,7},{7,6},{8,9},{9,8},{10,11... | collective-permute-start | bytes 6291464 | tf_op jit(solution)/shard_map/ppermute | solution.py:968
  504.5 7.0 copy-start
  504.5 7.2 copy-start.10
  511.5 1.3 copy-start.1
  511.7 1.7 copy-start.5
  515.2 202.7 %reduce-scatter.6.cloned.1.call-start = ((), (), s32[]{:S(2)}) async-start(), calls=%async_computation.4 | async-start | bytes 9437184 | tf_op jit(solution)/shard_map/reduce_scatter | solution.py:971
  603.8 295.5 %reduce-scatter.8.cloned.1.call-start = ((), (), s32[]{:S(2)}) async-start(), calls=%async_computation.5 | async-start | bytes 9437184 | tf_op jit(solution)/shard_map/reduce_scatter | solution.py:971
  603.8 47.8 %copy-start.12 = (f32[16,2048]{1,0:T(8,128)S(1)}, f32[16,2048]{1,0:T(8,128)}, u32[]{:S(2)}) copy-start(f32[16,2048]{1,0:T(8,128)} %get-tuple-element.226) | copy-start | bytes 393220
  720.7 1.1 copy-start.9
  894.7 4.6 copy-start.4
  894.7 4.6 copy-start.15
  899.3 1.9 copy-start.2
Sparse Core Ops, SparseCore 0:
  423.1 86.8 reduce-scatter.3
  515.3 80.4 all-gather.2
  603.9 87.8 reduce-scatter.5
  720.9 115.1 reduce-scatter.7

commit v4 on v3

--- a/solution.py
+++ b/solution.py
@@ -276,14 +276,45 @@
 UNIT = 2
 
 
-def expert_kernel(row_counts, cot_counts, batch, trades, ex_ref, wg, wu, wd, wr, *refs):
-    first, second = (len(row_counts), len(row_counts) + len(cot_counts))
+def expert_block(expert, rows_in, cots_in, wg, wu, wd, wr, x_ref, y_ref, m_ref, dg_ref, du_ref):
+    row_count, hidden = (rows_in[0].shape[0], wg.shape[-1])
+    for seq, (rows, cots) in enumerate(zip(rows_in, cots_in)):
+        spots = slot_spots(cots[row_count:, :row_count].astype(WIDE), expert)
+        span = pl.ds(seq * CAP, CAP)
+        x_ref[span] = dot_nn(spots, rows[...]).astype(LOW)
+        y_ref[span] = dot_nn(spots, cots[:row_count]).astype(LOW)
+    x_all, y_all = (x_ref[...], y_ref[...])
+    logits = dot_nn(x_all, wr[...])
+    expo = jnp.exp(logits - jnp.max(logits, axis=-1, keepdims=True))
+    chosen = lax.broadcasted_iota(jnp.int32, expo.shape, 1) == expert
+    gates = jnp.sum(jnp.where(chosen, expo, 0.0), axis=-1, keepdims=True) / jnp.sum(
+        expo, axis=-1, keepdims=True
+    )
+    step = min(256, hidden)
+    dgate = jnp.zeros((x_all.shape[0], 1), WIDE)
+    for start in range(0, hidden, step):
+        span = slice(start, start + step)
+        gate_act, up_act = (dot_nn(x_all, wg[:, span]), dot_nn(x_all, wu[:, span]))
+        plain_grad = dot_nt(y_all, wd[span, :])
+        sig = jax.nn.sigmoid(gate_act)
+        silu = gate_act * sig
+        joined = silu * up_act
+        dgate += jnp.sum(joined * plain_grad, axis=-1, keepdims=True)
+        grad = plain_grad * gates
+        m_ref[:, span] = (joined * gates).astype(LOW)
+        dg_ref[:, span] = (grad * up_act * (sig + silu * (1.0 - sig))).astype(LOW)
+        du_ref[:, span] = (grad * silu).astype(LOW)
+    return dgate
+
+
+def expert_kernel(row_spans, cot_spans, batch, trades, ex_ref, wg, wu, wd, wr, *refs):
+    first, second = (len(row_spans), len(row_spans) + len(cot_spans))
     rows_in, cots_in = (refs[:first], refs[first:second])
     third, number = (second + len(trades.trades), len(trades.trades))
     x_ref, y_ref, m_ref, dg_ref, du_ref, dgate_ref = refs[third : third + 6]
     rows_buf, cots_buf, sems = refs[third + 6 + number : third + 9 + number]
     trades.bind(refs[second:third], refs[third + 6 : third + 6 + number], refs[third + 9 + number :])
-    steps, units = (sum(row_counts) // batch, batch // UNIT)
+    steps, units = (sum(count for _, count in row_spans) // batch, batch // UNIT)
     turn = pl.program_id(0) * steps + pl.program_id(1)
     slot = lax.rem(turn, 2)
     row_count = rows_buf.shape[2]
@@ -299,14 +330,14 @@
     def fetch(step, place):
         for part in range(units):
             unit = step * units + part
-            for kind, sources, counts in ((0, rows_in, row_counts), (1, cots_in, cot_counts)):
+            for kind, sources, spans in ((0, rows_in, row_spans), (1, cots_in, cot_spans)):
                 begin = 0
-                for source, count in zip(sources, counts):
+                for source, (offset, count) in zip(sources, spans):
                     size = count // UNIT
 
                     @pl.when((unit >= begin) & (unit < begin + size))
-                    def _(source=source, begin=begin):
-                        copy(kind, source, (unit - begin) * UNIT, place, part).start()
+                    def _(source=source, begin=begin, offset=offset):
+                        copy(kind, source, offset + (unit - begin) * UNIT, place, part).start()
 
                     begin += size
 
@@ -323,35 +354,13 @@
     for part in range(units):
         copy(0, rows_in[0], 0, slot, part).wait()
         copy(1, cots_in[0], 0, slot, part).wait()
-    hidden = wg.shape[-1]
-    expert = ex_ref[pl.program_id(0)]
-    for seq in range(batch):
-        table = cots_buf[slot, seq, row_count:, :row_count].astype(WIDE)
-        spots = slot_spots(table, expert)
-        span = pl.ds(seq * CAP, CAP)
-        x_ref[0, span] = dot_nn(spots, rows_buf[slot, seq]).astype(LOW)
-        y_ref[0, span] = dot_nn(spots, cots_buf[slot, seq, :row_count]).astype(LOW)
-    x_all, y_all = (x_ref[0], y_ref[0])
-    logits = dot_nn(x_all, wr[...])
-    expo = jnp.exp(logits - jnp.max(logits, axis=-1, keepdims=True))
-    chosen = lax.broadcasted_iota(jnp.int32, expo.shape, 1) == expert
-    gates = jnp.sum(jnp.where(chosen, expo, 0.0), axis=-1, keepdims=True) / jnp.sum(
-        expo, axis=-1, keepdims=True
-    )
-    step = min(256, hidden)
-    dgate = jnp.zeros((x_all.shape[0], 1), WIDE)
-    for start in range(0, hidden, step):
-        span = slice(start, start + step)
-        gate_act, up_act = (dot_nn(x_all, wg[0, :, span]), dot_nn(x_all, wu[0, :, span]))
-        plain_grad = dot_nt(y_all, wd[0, span, :])
-        sig = jax.nn.sigmoid(gate_act)
-        silu = gate_act * sig
-        joined = silu * up_act
-        dgate += jnp.sum(joined * plain_grad, axis=-1, keepdims=True)
-        grad = plain_grad * gates
-        m_ref[0, :, span] = (joined * gates).astype(LOW)
-        dg_ref[0, :, span] = (grad * up_act * (sig + silu * (1.0 - sig))).astype(LOW)
-        du_ref[0, :, span] = (grad * silu).astype(LOW)
+    dgate = expert_block(
+        ex_ref[pl.program_id(0)],
+        [rows_buf.at[slot, seq] for seq in range(batch)],
+        [cots_buf.at[slot, seq] for seq in range(batch)],
+        wg.at[0], wu.at[0], wd.at[0], wr,
+        x_ref.at[0], y_ref.at[0], m_ref.at[0], dg_ref.at[0], du_ref.at[0],
+    )
     dgate_ref[0] = jnp.broadcast_to(dgate, dgate_ref.shape[1:])
     if number:
 
@@ -362,9 +371,10 @@
 
 def expert_acts(ids, rows, cots, wg, wu, wd, wr, batch=4, trades=(), collective=None):
     trades = Trades(trades)
-    row_count, width = rows[0].shape[1:]
-    row_counts, cot_counts = ([array.shape[0] for array in arrays] for arrays in (rows, cots))
-    count = sum(row_counts)
+    row_spans, cot_spans = ([span for _, span in items] for items in (rows, cots))
+    rows, cots = ([array for array, _ in items] for items in (rows, cots))
+    count = sum(size for _, size in row_spans)
+    width = rows[0].shape[2]
     own, _, hidden = wg.shape
     out_rows = batch * CAP
 
@@ -382,7 +392,7 @@
     any_spec = pl.BlockSpec(memory_space=pl.ANY)
     columns = (width, width, hidden, hidden, hidden, 128)
     return pl.pallas_call(
-        functools.partial(expert_kernel, row_counts, cot_counts, batch, trades),
+        functools.partial(expert_kernel, row_spans, cot_spans, batch, trades),
         grid=(own, count // batch),
         in_specs=[
             pl.BlockSpec(memory_space=pltpu.SMEM),
@@ -411,6 +421,26 @@
     )(ids, wg, wu, wd, wr, *rows, *cots, *trades.arrays)
 
 
+def pull_block(experts, rows, table, backs, dgates, wr):
+    logits = dot_nn(rows, wr[...])
+    expo = jnp.exp(logits - jnp.max(logits, axis=-1, keepdims=True))
+    probs = expo / jnp.sum(expo, axis=-1, keepdims=True)
+    columns = lax.broadcasted_iota(jnp.int32, probs.shape, 1)
+    grad_logits = jnp.zeros_like(probs)
+    total = jnp.zeros(rows.shape, WIDE)
+    for expert, back, dgate in zip(experts, backs, dgates):
+        spots = slot_spots(table, expert)
+        total += dot_tn(spots, back)
+        high = dgate.astype(LOW)
+        rest = (dgate - high.astype(WIDE)).astype(LOW)
+        at_rows = (dot_tn(spots, high) + dot_tn(spots, rest))[:, : probs.shape[1]]
+        chosen = (columns == expert).astype(WIDE)
+        prob = jnp.sum(probs * chosen, axis=-1, keepdims=True)
+        grad_logits += at_rows * prob * (chosen - probs)
+    low_logits = grad_logits.astype(LOW)
+    return (total + dot_nt(low_logits, wr[...])).astype(LOW), dot_tn(low_logits, rows)
+
+
 def pull_kernel(ex_ref, rows_ref, cot_ref, dg_ref, du_ref, dgate_ref, wg, wu, wr, part_ref, router):
     batch, row_count, _ = rows_ref.shape
     own = wg.shape[0]
@@ -423,27 +453,16 @@
         (dot_nt(dg_ref[e], wg[e]) + dot_nt(du_ref[e], wu[e])).astype(LOW) for e in range(own)
     ]
     for seq in range(batch):
-        table = cot_ref[seq, :, :row_count].astype(WIDE)
-        logits = dot_nn(rows_ref[seq], wr[...])
-        expo = jnp.exp(logits - jnp.max(logits, axis=-1, keepdims=True))
-        probs = expo / jnp.sum(expo, axis=-1, keepdims=True)
-        columns = lax.broadcasted_iota(jnp.int32, probs.shape, 1)
-        grad_logits = jnp.zeros_like(probs)
         span = slice(seq * CAP, (seq + 1) * CAP)
-        total = jnp.zeros(part_ref.shape[1:], WIDE)
-        for e in range(own):
-            spots = slot_spots(table, ex_ref[e])
-            total += dot_tn(spots, backs[e][span])
-            dgate = dgate_ref[e, span]
-            high = dgate.astype(LOW)
-            rest = (dgate - high.astype(WIDE)).astype(LOW)
-            at_rows = (dot_tn(spots, high) + dot_tn(spots, rest))[:, : probs.shape[1]]
-            chosen = (columns == ex_ref[e]).astype(WIDE)
-            prob = jnp.sum(probs * chosen, axis=-1, keepdims=True)
-            grad_logits += at_rows * prob * (chosen - probs)
-        low_logits = grad_logits.astype(LOW)
-        part_ref[seq] = (total + dot_nt(low_logits, wr[...])).astype(LOW)
-        router[...] += dot_tn(low_logits, rows_ref[seq])
+        part_ref[seq], router_part = pull_block(
+            [ex_ref[e] for e in range(own)],
+            rows_ref[seq],
+            cot_ref[seq, :, :row_count].astype(WIDE),
+            [back[span] for back in backs],
+            [dgate_ref[e, span] for e in range(own)],
+            wr,
+        )
+        router[...] += router_part
 
 
 def mix_kernel(ex_ref, cot_ref, m_ref, wd, part_ref):
@@ -520,222 +539,158 @@
 NEAR_LINES = 128
 
 
+def each(size, body):
+    def step(i, carry):
+        body(i)
+        return carry
+
+    lax.fori_loop(0, size, step, 0)
+
+
+def remote(source, target, send, recv, device):
+    return pltpu.make_async_remote_copy(
+        source, target, send, recv, device_id=device, device_id_type=pl.DeviceIdType.MESH
+    )
+
+
+class Links:
+    def __init__(self, replicas, groups):
+        rep, shard = (lax.axis_index("rep"), lax.axis_index("shard"))
+        self.rail = groups // 2
+        self.last = self.rail - 1
+        self.shard, self.place, self.core = (shard, shard // 2, shard % 2)
+        self.right, self.left = ((rep, shard + 2), (rep, shard - 2))
+        self.partner = (rep, shard + 1 - 2 * self.core)
+        self.over_x = (rep + 1 - 2 * (rep % 2), shard)
+        self.over_y = ((rep + 2) % replicas, shard)
+
+    def greet(self, others):
+        barrier = pltpu.get_barrier_semaphore()
+
+        def signal(device):
+            pl.semaphore_signal(
+                barrier, inc=1, device_id=device, device_id_type=pl.DeviceIdType.MESH
+            )
+
+        for device in others:
+            signal(device)
+        pl.when(self.place < self.last)(lambda: signal(self.right))
+        pl.when(self.place > 0)(lambda: signal(self.left))
+        inner = (self.place > 0) & (self.place < self.last)
+        pl.when(inner)(lambda: pl.semaphore_wait(barrier, len(others) + 2))
+        pl.when(jnp.logical_not(inner))(lambda: pl.semaphore_wait(barrier, len(others) + 1))
+
+
+class Flood:
+    def __init__(self, links, view, send, recv, pair, own):
+        self.links, self.view, self.own = (links, view, own)
+        self.send, self.recv, self.pair = (send, recv, pair)
+
+    def copy(self, way, q, own=False):
+        links = self.links
+        slot = 2 * q + links.core
+        source = self.own if own else self.view.at[slot]
+        recv = self.pair.at[q] if way == 2 else self.recv.at[q]
+        device = (links.right, links.left, links.partner)[way]
+        return remote(source, self.view.at[slot], self.send.at[way, q], recv, device)
+
+    def start(self):
+        place = self.links.place
+
+        @pl.when(place < self.links.last)
+        def _():
+            self.copy(0, place, True).start()
+
+        @pl.when(place > 0)
+        def _():
+            self.copy(1, place, True).start()
+
+        self.copy(2, place, True).start()
+
+    def onward(self, d, more=None):
+        place, last = (self.links.place, self.links.last)
+
+        @pl.when((d > 0) & (place - d >= 0))
+        def _():
+            q = place - d
+            self.copy(0, q).wait_recv()
+
+            @pl.when(place < last)
+            def _():
+                self.copy(0, q).start()
+
+            self.copy(2, q).start()
+            if more is not None:
+                more(q)
+
+        @pl.when((d > 0) & (place + d <= last))
+        def _():
+            q = place + d
+            self.copy(1, q).wait_recv()
+
+            @pl.when(place > 0)
+            def _():
+                self.copy(1, q).start()
+
+            self.copy(2, q).start()
+            if more is not None:
+                more(q)
+
+    def wait_pair(self, q):
+        slot = self.view.at[2 * q + 1 - self.links.core]
+        remote(slot, slot, self.send.at[2, q], self.pair.at[q], self.links.partner).wait_recv()
+
+    def finish(self, q):
+        place = self.links.place
+
+        @pl.when((place < self.links.last) & (q <= place))
+        def _():
+            self.copy(0, q).wait_send()
+
+        @pl.when((place > 0) & (q >= place))
+        def _():
+            self.copy(1, q).wait_send()
+
+        self.copy(2, q).wait_send()
+
+
 def front_kernel(
     replicas, groups,
-    packet, cot, tokens, wq, wk, wv, wo, gq, gk, cos_ref, sin_ref, gain_ref,
-    packets, qr_ref, kr_ref, v_ref, o_ref, hidden, rows_all, cots, fx, fy, fd, px, py, pd,
-    nb, mine, pair_out, pair_in, line_r, line_l, low,
-    n1_send, n1_recv, n1_pair, n2_send, n2_recv, n2_pair, cz_send, cz_recv, cz_pair,
-    xy_send, xy_recv, dg_send, dg_recv, fl_send, fl_recv,
-    po_send, po_recv, lr_send, lr_recv, ll_send, ll_recv, keep_sem, own_sem,
+    packet, tokens, wq, wk, wv, wo, gq, gk, cos_ref, sin_ref, gain_ref,
+    packets, qr_ref, kr_ref, v_ref, o_ref, hidden, low,
+    nb, mine, pair_out, pair_in, line_r, line_l,
+    n1_send, n1_recv, n1_pair, po_send, po_recv, lr_send, lr_recv, ll_send, ll_recv, keep_sem, own_sem,
 ):
-    rail = groups // 2
-    rep, shard = (lax.axis_index("rep"), lax.axis_index("shard"))
-    place, core = (shard // 2, shard % 2)
+    links = Links(replicas, groups)
+    rail, last, place, core = (links.rail, links.last, links.place, links.core)
     rows = tokens.shape[0]
     step_rows = rows // CHUNKS
-    last = rail - 1
-    right, left, partner = ((rep, shard + 2), (rep, shard - 2), (rep, shard + 1 - 2 * core))
-    over_x = (rep + 1 - 2 * (rep % 2), shard)
-    over_y = ((rep + 2) % replicas, shard)
-
-    def remote(source, target, send, recv, device):
-        return pltpu.make_async_remote_copy(
-            source, target, send, recv, device_id=device, device_id_type=pl.DeviceIdType.MESH
-        )
-
-    def each(size, body):
-        def step(i, carry):
-            body(i)
-            return carry
-
-        lax.fori_loop(0, size, step, 0)
-
-    class Flood:
-        def __init__(self, view, send, recv, pair, own):
-            self.view, self.send, self.recv, self.pair, self.own = (view, send, recv, pair, own)
-
-        def copy(self, way, q, own=False):
-            slot = 2 * q + core
-            source = self.own if own else self.view.at[slot]
-            recv = self.pair.at[q] if way == 2 else self.recv.at[q]
-            device = (right, left, partner)[way]
-            return remote(source, self.view.at[slot], self.send.at[way, q], recv, device)
-
-        def start_line(self):
-            @pl.when(place < last)
-            def _():
-                self.copy(0, place, True).start()
-
-            @pl.when(place > 0)
-            def _():
-                self.copy(1, place, True).start()
-
-        def start_pair(self):
-            self.copy(2, place, True).start()
-
-        def onward(self, d, more=None):
-            @pl.when((d > 0) & (place - d >= 0))
-            def _():
-                q = place - d
-                self.copy(0, q).wait_recv()
-
-                @pl.when(place < last)
-                def _():
-                    self.copy(0, q).start()
-
-                self.copy(2, q).start()
-                if more is not None:
-                    more(q)
-
-            @pl.when((d > 0) & (place + d <= last))
-            def _():
-                q = place + d
-                self.copy(1, q).wait_recv()
-
-                @pl.when(place > 0)
-                def _():
-                    self.copy(1, q).start()
-
-                self.copy(2, q).start()
-                if more is not None:
-                    more(q)
-
-        def wait_pair(self, q):
-            slot = 2 * q + 1 - core
-            remote(
-                self.view.at[slot], self.view.at[slot], self.send.at[2, q], self.pair.at[q], partner
-            ).wait_recv()
-
-        def finish(self, pairs):
-            def body(q):
-                @pl.when((place < last) & (q <= place))
-                def _():
-                    self.copy(0, q).wait_send()
-
-                @pl.when((place > 0) & (q >= place))
-                def _():
-                    self.copy(1, q).wait_send()
-
-                self.copy(2, q).wait_send()
-                if pairs:
-                    self.wait_pair(q)
-
-            each(rail, body)
-
-    flood_n1 = Flood(nb, n1_send, n1_recv, n1_pair, packet)
-    flood_n2 = Flood(rows_all, n2_send, n2_recv, n2_pair, low)
-    flood_cot = Flood(cots, cz_send, cz_recv, cz_pair, cot)
-
-    def cross(way, q, own=False):
-        source = cot if own else cots.at[2 * q + core]
-        target, device = ((fx, over_x), (fy, over_y))[way]
-        return remote(source, target.at[q], xy_send.at[way, q], xy_recv.at[way, q], device)
-
-    def cross_both(q):
-        cross(0, q).start()
-        cross(1, q).start()
-
-    def diagonal(way, q):
-        source, device = ((fx, over_y), (fy, over_x))[way]
-        span = (pl.ds(0, NEAR_LINES), pl.ds(NEAR_LINES, cot.shape[0] - NEAR_LINES))[way]
-        return remote(
-            source.at[q, span], fd.at[q, span], dg_send.at[way, q], dg_recv.at[way, q], device
-        )
-
-    def flip(which, q):
-        source, target = ((fx, px), (fy, py), (fd, pd))[which]
-        return remote(
-            source.at[q], target.at[q], fl_send.at[which, q], fl_recv.at[which, q], partner
-        )
-
-    def at_distance(d, body):
-        if d < 0 or d > last:
-            return
-        if d == 0:
-            body(place)
-            return
-
-        @pl.when(place - d >= 0)
-        def _():
-            body(place - d)
-
-        @pl.when(place + d <= last)
-        def _():
-            body(place + d)
-
-    def take_cross(q):
-        for way in (0, 1):
-            cross(way, q).wait_recv()
-            diagonal(way, q).start()
-            flip(way, q).start()
-
-    def take_diagonal(q):
-        for way in (0, 1):
-            diagonal(way, q).wait_recv()
-        flip(2, q).start()
-
-    def event(d):
-        if 1 <= d <= last:
-            flood_cot.onward(d, cross_both)
-        at_distance(d - 1, take_cross)
-        at_distance(d - 2, take_diagonal)
-
-    barrier = pltpu.get_barrier_semaphore()
-
-    def greet(device):
-        pl.semaphore_signal(
-            barrier, inc=1, device_id=device, device_id_type=pl.DeviceIdType.MESH
-        )
-
-    for device in (partner, over_x, over_y):
-        greet(device)
-
-    @pl.when(place < last)
-    def _():
-        greet(right)
-
-    @pl.when(place > 0)
-    def _():
-        greet(left)
-
-    inner = (place > 0) & (place < last)
-
-    @pl.when(inner)
-    def _():
-        pl.semaphore_wait(barrier, 5)
-
-    @pl.when(jnp.logical_not(inner))
-    def _():
-        pl.semaphore_wait(barrier, 4)
-
-    flood_n1.start_line()
-    flood_n1.start_pair()
-    own_block = pltpu.make_async_copy(packet, nb.at[shard], own_sem.at[0])
+    flood = Flood(links, nb, n1_send, n1_recv, n1_pair, packet)
+    links.greet([links.partner])
+    flood.start()
+    own_block = pltpu.make_async_copy(packet, nb.at[links.shard], own_sem.at[0])
     own_block.start()
-    own_cot = pltpu.make_async_copy(cot, cots.at[shard], own_sem.at[1])
-    own_cot.start()
-    cross(0, place, True).start()
-    cross(1, place, True).start()
-    flood_cot.start_pair()
     own_block.wait()
 
     def partial_out(q):
-        return remote(
-            pair_out.at[q], pair_in.at[q], po_send.at[q], po_recv.at[q], partner
-        )
+        return remote(pair_out.at[q], pair_in.at[q], po_send.at[q], po_recv.at[q], links.partner)
+
+    def chunk_span(chunk):
+        return pl.ds(pl.multiple_of(chunk * step_rows, step_rows), step_rows)
 
     def line(q, chunk, to_right):
-        span = pl.ds(pl.multiple_of(chunk * step_rows, step_rows), step_rows)
+        span = chunk_span(chunk)
         target, send, recv, device = (
-            (line_r, lr_send, lr_recv, right) if to_right else (line_l, ll_send, ll_recv, left)
+            (line_r, lr_send, lr_recv, links.right)
+            if to_right
+            else (line_l, ll_send, ll_recv, links.left)
         )
         return remote(
             mine.at[q, span], target.at[q, span], send.at[q, chunk], recv.at[q, chunk], device
         )
 
     def add_up(q, chunk, extras):
-        span = pl.ds(pl.multiple_of(chunk * step_rows, step_rows), step_rows)
+        span = chunk_span(chunk)
         total = mine[q, span].astype(WIDE) + pair_in[q, span].astype(WIDE)
         for extra in extras:
             total = total + extra[q, span].astype(WIDE)
@@ -749,8 +704,7 @@
             if not first:
                 line(q, chunk, to_right).wait_recv()
                 extras = [line_r if to_right else line_l]
-            span = pl.ds(pl.multiple_of(chunk * step_rows, step_rows), step_rows)
-            mine[q, span] = add_up(q, chunk, extras).astype(LOW)
+            mine[q, chunk_span(chunk)] = add_up(q, chunk, extras).astype(LOW)
             line(q, chunk, to_right).start()
 
         each(CHUNKS, body)
@@ -759,7 +713,7 @@
         return pltpu.make_async_copy(nb.at[slot], packets.at[slot], keep_sem.at[slot])
 
     def one_distance(d):
-        flood_n1.onward(d)
+        flood.onward(d)
 
         def one_block(k):
             side, other = (k % 2, k // 2)
@@ -769,7 +723,7 @@
             def _():
                 @pl.when(other == 1)
                 def _():
-                    flood_n1.wait_pair(q)
+                    flood.wait_pair(q)
 
                 slot = 2 * q + core + other * (1 - 2 * core)
                 keep_copy(slot).start()
@@ -804,7 +758,6 @@
             forward_line(last - d, False, True)
 
     each(rail, one_distance)
-    flood_cot.start_line()
 
     def rest_right():
         def body(j):
@@ -825,10 +778,8 @@
     near_end = place < rail // 2
     pl.when(near_end)(rest_right)
     pl.when(jnp.logical_not(near_end))(rest_left)
-    event(1)
     pl.when(near_end)(rest_left)
     pl.when(jnp.logical_not(near_end))(rest_right)
-
     partial_out(place).wait_recv()
 
     def finish_rows(chunk):
@@ -840,7 +791,7 @@
         def _():
             line(place, chunk, False).wait_recv()
 
-        span = pl.ds(pl.multiple_of(chunk * step_rows, step_rows), step_rows)
+        span = chunk_span(chunk)
         total = tokens[span].astype(WIDE) + add_up(place, chunk, [])
         from_left = jnp.where(place > 0, line_r[place, span].astype(WIDE), 0.0)
         from_right = jnp.where(place < last, line_l[place, span].astype(WIDE), 0.0)
@@ -850,32 +801,12 @@
         low[span] = (total * scale * gain_ref[...]).astype(LOW)
 
     each(CHUNKS, finish_rows)
-    flood_n2.start_line()
-    flood_n2.start_pair()
-    own_low = pltpu.make_async_copy(low, rows_all.at[shard], own_sem.at[2])
-    own_low.start()
-
-    event(2)
-    for d in range(1, rail):
-        flood_n2.onward(d)
-        event(d + 2)
-
-    flood_n1.finish(False)
-    flood_n2.finish(True)
-    flood_cot.finish(True)
-    own_cot.wait()
-    own_low.wait()
 
     def settle(q):
+        flood.finish(q)
         keep_copy(2 * q).wait()
         keep_copy(2 * q + 1).wait()
         partial_out(q).wait_send()
-        for way in (0, 1):
-            cross(way, q).wait_send()
-            diagonal(way, q).wait_send()
-        for which in (0, 1, 2):
-            flip(which, q).wait_send()
-            flip(which, q).wait_recv()
 
         def chunk_sends(chunk):
             @pl.when((place < last) & (q > place))
@@ -891,21 +822,23 @@
     each(rail, settle)
 
 
-def front(replicas, groups, packet, cot, tokens, wq, wk, wv, wo, gq, gk, cos_tab, sin_tab, gain):
+ANY_SPEC = pl.BlockSpec(memory_space=pl.ANY)
+FAST_SPEC = pl.BlockSpec(memory_space=pltpu.VMEM)
+
+
+def shape(*dims, kind=LOW):
+    return jax.ShapeDtypeStruct(dims, kind)
+
+
+def front(replicas, groups, packet, tokens, wq, wk, wv, wo, gq, gk, cos_tab, sin_tab, gain):
     lines, width = packet.shape
     rows, wide, rail = (tokens.shape[0], wq.shape[1], groups // 2)
-    any_spec, fast = (pl.BlockSpec(memory_space=pl.ANY), pl.BlockSpec(memory_space=pltpu.VMEM))
-
-    def shape(*dims, kind=LOW):
-        return jax.ShapeDtypeStruct(dims, kind)
-
-    far = [shape(rail, lines, width)] * 6
     block = pltpu.VMEM((rail, rows, width), LOW)
     dma = pltpu.SemaphoreType.DMA
     return pl.pallas_call(
         functools.partial(front_kernel, replicas, groups),
-        in_specs=[any_spec] * 2 + [fast] * 10,
-        out_specs=[any_spec] + [fast] * 5 + [any_spec] * 8,
+        in_specs=[ANY_SPEC] + [FAST_SPEC] * 10,
+        out_specs=[ANY_SPEC] + [FAST_SPEC] * 6,
         out_shape=[
             shape(groups, lines, width),
             shape(groups, rows, wide, kind=WIDE),
@@ -913,27 +846,214 @@
             shape(groups, rows, wide),
             shape(groups, rows, wide),
             shape(rows, width, kind=WIDE),
-            shape(groups, rows, width),
-            shape(groups, lines, width),
-        ]
-        + far,
-        scratch_shapes=[
-            pltpu.VMEM((groups, lines, width), LOW),
-            block, block, block, block, block,
-            pltpu.VMEM((rows, width), LOW),
-        ]
-        + [dma((3, rail)), dma((rail,)), dma((rail,))] * 3
-        + [dma((2, rail))] * 4
-        + [dma((3, rail))] * 2
+            shape(rows, width),
+        ],
+        scratch_shapes=[pltpu.VMEM((groups, lines, width), LOW), block, block, block, block, block]
+        + [dma((3, rail)), dma((rail,)), dma((rail,))]
         + [dma((rail,))] * 2
         + [dma((rail, CHUNKS))] * 4
-        + [dma((groups,)), dma((3,))],
+        + [dma((groups,)), dma((1,))],
         compiler_params=pltpu.CompilerParams(
             vmem_limit_bytes=VMEM_BYTES, collective_id=0, has_side_effects=True
         ),
         cost_estimate=COST,
         name="front",
-    )(packet, cot, tokens, wq, wk, wv, wo, gq, gk, cos_tab, sin_tab, gain)
+    )(packet, tokens, wq, wk, wv, wo, gq, gk, cos_tab, sin_tab, gain)
+
+
+def moe_kernel(
+    replicas, groups,
+    ex_ref, low, cot, wg_in, wu_in, wd_in, wr,
+    rows_all, cots, fx, fy, fd, px, py, pd, x_out, y_out, m_out, dg_out, du_out, part_out, router,
+    wg, wu, wd, rows_buf, cots_buf, x_s, y_s, m_s, dg_s, du_s, part_s,
+    n2_send, n2_recv, n2_pair, cz_send, cz_recv, cz_pair,
+    xy_send, xy_recv, dg_send, dg_recv, fl_send, fl_recv, own_sem, load_sem, out_sem, part_sem,
+):
+    links = Links(replicas, groups)
+    rail, last, place, core = (links.rail, links.last, links.place, links.core)
+    own, row_count = (wg.shape[0], low.shape[0])
+    flood_n2 = Flood(links, rows_all, n2_send, n2_recv, n2_pair, low)
+    flood_cot = Flood(links, cots, cz_send, cz_recv, cz_pair, cot)
+
+    def cross(way, q, own_block=False):
+        source = cot if own_block else cots.at[2 * q + core]
+        target, device = ((fx, links.over_x), (fy, links.over_y))[way]
+        return remote(source, target.at[q], xy_send.at[way, q], xy_recv.at[way, q], device)
+
+    def cross_both(q):
+        cross(0, q).start()
+        cross(1, q).start()
+
+    def diagonal(way, q):
+        source, device = ((fx, links.over_y), (fy, links.over_x))[way]
+        span = (pl.ds(0, NEAR_LINES), pl.ds(NEAR_LINES, cot.shape[0] - NEAR_LINES))[way]
+        return remote(
+            source.at[q, span], fd.at[q, span], dg_send.at[way, q], dg_recv.at[way, q], device
+        )
+
+    def flip(which, q):
+        source, target = ((fx, px), (fy, py), (fd, pd))[which]
+        return remote(
+            source.at[q], target.at[q], fl_send.at[which, q], fl_recv.at[which, q], links.partner
+        )
+
+    def at_distance(d, body):
+        @pl.when((d >= 0) & (place - d >= 0))
+        def _():
+            body(place - d)
+
+        @pl.when((d > 0) & (place + d <= last))
+        def _():
+            body(place + d)
+
+    def take_cross(q):
+        for way in (0, 1):
+            cross(way, q).wait_recv()
+            diagonal(way, q).start()
+            flip(way, q).start()
+
+    def take_diagonal(q):
+        for way in (0, 1):
+            diagonal(way, q).wait_recv()
+        flip(2, q).start()
+
+    links.greet([links.partner, links.over_x, links.over_y])
+    flood_cot.start()
+    flood_n2.start()
+    cross(0, place, True).start()
+    cross(1, place, True).start()
+    own_copies = (
+        pltpu.make_async_copy(low, rows_all.at[links.shard], own_sem.at[0]),
+        pltpu.make_async_copy(cot, cots.at[links.shard], own_sem.at[1]),
+        pltpu.make_async_copy(wg_in, wg, own_sem.at[2]),
+        pltpu.make_async_copy(wu_in, wu, own_sem.at[3]),
+        pltpu.make_async_copy(wd_in, wd, own_sem.at[4]),
+    )
+    for copy in own_copies:
+        copy.start()
+    router[...] = jnp.zeros_like(router)
+    for copy in own_copies:
+        copy.wait()
+
+    def out_copies(q):
+        span = pl.ds(2 * q * CAP, 2 * CAP)
+        pairs = ((x_s, x_out), (y_s, y_out), (m_s, m_out), (dg_s, dg_out), (du_s, du_out))
+        return [
+            pltpu.make_async_copy(source.at[e], target.at[e, span], out_sem.at[e, i])
+            for e in range(own)
+            for i, (source, target) in enumerate(pairs)
+        ]
+
+    def part_copy(q):
+        return pltpu.make_async_copy(part_s, part_out.at[pl.ds(2 * q, 2)], part_sem.at[0])
+
+    near = jnp.where(place <= last - place, place, last - place)
+    far_sign = jnp.where(place <= last - place, 1, -1)
+
+    def one_step(k):
+        flood_cot.onward(k, cross_both)
+        flood_n2.onward(k)
+        at_distance(k - 1, take_cross)
+        at_distance(k - 2, take_diagonal)
+        within = k <= 2 * near
+        sign = jnp.where(within & (k % 2 == 1), -far_sign, far_sign)
+        q = place + sign * jnp.where(within, (k + 1) // 2, k - near)
+        flood_cot.wait_pair(q)
+        flood_n2.wait_pair(q)
+        loads = (
+            pltpu.make_async_copy(rows_all.at[pl.ds(2 * q, 2)], rows_buf, load_sem.at[0]),
+            pltpu.make_async_copy(cots.at[pl.ds(2 * q, 2)], cots_buf, load_sem.at[1]),
+        )
+        for copy in loads:
+            copy.start()
+
+        @pl.when(k > 0)
+        def _():
+            for copy in out_copies(0):
+                copy.wait()
+            part_copy(0).wait()
+
+        for copy in loads:
+            copy.wait()
+        dgates, backs = ([], [])
+        for e in range(own):
+            dgate = expert_block(
+                ex_ref[e],
+                [rows_buf.at[seq] for seq in range(2)],
+                [cots_buf.at[seq] for seq in range(2)],
+                wg.at[e], wu.at[e], wd.at[e], wr,
+                x_s.at[e], y_s.at[e], m_s.at[e], dg_s.at[e], du_s.at[e],
+            )
+            dgates.append(jnp.broadcast_to(dgate, (dgate.shape[0], 128)))
+            backs.append((dot_nt(dg_s[e], wg[e]) + dot_nt(du_s[e], wu[e])).astype(LOW))
+        for copy in out_copies(q):
+            copy.start()
+        for seq in range(2):
+            span = slice(seq * CAP, (seq + 1) * CAP)
+            part_s[seq], router_part = pull_block(
+                [ex_ref[e] for e in range(own)],
+                rows_buf[seq],
+                cots_buf[seq, row_count:, :row_count].astype(WIDE),
+                [back[span] for back in backs],
+                [dgate[span] for dgate in dgates],
+                wr,
+            )
+            router[...] += router_part
+        part_copy(q).start()
+
+    each(rail, one_step)
+    at_distance(last, take_cross)
+    at_distance(last - 1, take_diagonal)
+    at_distance(last, take_diagonal)
+    for copy in out_copies(0):
+        copy.wait()
+    part_copy(0).wait()
+
+    def settle(q):
+        flood_n2.finish(q)
+        flood_cot.finish(q)
+        for way in (0, 1):
+            cross(way, q).wait_send()
+            diagonal(way, q).wait_send()
+        for which in (0, 1, 2):
+            flip(which, q).wait_send()
+            flip(which, q).wait_recv()
+
+    each(rail, settle)
+
+
+def moe(replicas, groups, ids, low, cot, wg, wu, wd, wr):
+    lines, width = cot.shape
+    rows, rail = (low.shape[0], groups // 2)
+    own, _, hidden = wg.shape
+    pair = 2 * CAP
+    dma, vmem = (pltpu.SemaphoreType.DMA, pltpu.VMEM)
+    acts = [shape(own, groups * CAP, cols) for cols in (width, width, hidden, hidden, hidden)]
+    return pl.pallas_call(
+        functools.partial(moe_kernel, replicas, groups),
+        in_specs=[pl.BlockSpec(memory_space=pltpu.SMEM)]
+        + [FAST_SPEC] * 2
+        + [ANY_SPEC] * 3
+        + [FAST_SPEC],
+        out_specs=[ANY_SPEC] * 14 + [FAST_SPEC],
+        out_shape=[shape(groups, rows, width), shape(groups, lines, width)]
+        + [shape(rail, lines, width)] * 6
+        + acts
+        + [shape(groups, rows, width), shape(wr.shape[1], width, kind=WIDE)],
+        scratch_shapes=[vmem(array.shape, LOW) for array in (wg, wu, wd)]
+        + [vmem((2, rows, width), LOW), vmem((2, lines, width), LOW)]
+        + [vmem((own, pair, cols), LOW) for cols in (width, width, hidden, hidden, hidden)]
+        + [vmem((2, rows, width), LOW)]
+        + [dma((3, rail)), dma((rail,)), dma((rail,))] * 2
+        + [dma((2, rail))] * 4
+        + [dma((3, rail))] * 2
+        + [dma((5,)), dma((2,)), dma((own, 5)), dma((1,))],
+        compiler_params=pltpu.CompilerParams(
+            vmem_limit_bytes=VMEM_BYTES, collective_id=3, has_side_effects=True
+        ),
+        cost_estimate=COST,
+        name="moe",
+    )(ids, low, cot, wg, wu, wd, wr)
 
 
 def rms_parts(values):
@@ -972,6 +1092,21 @@
             parts.reshape(-1, width), "shard", scatter_dimension=0, tiled=True
         ).astype(WIDE)
 
+    experts = (w_gate, w_up, w_down, w_router)
+
+    def whole(*arrays):
+        return [(array, (0, array.shape[0])) for array in arrays]
+
+    def add_grads(acts, grads=None):
+        return [
+            weight_grad(
+                [act[left] for act in acts],
+                [act[right] for act in acts],
+                None if grads is None else grads[number],
+            )
+            for number, (left, right) in enumerate(((0, 3), (0, 4), (2, 1)))
+        ]
+
     inputs = tokens.astype(WIDE)
     row_mask = (jnp.arange(row_count, dtype=jnp.int32) < lengths[0])[:, None]
     named = jnp.any(
@@ -989,16 +1124,21 @@
     heads = (w_query, w_key, w_value, w_out, gain_q, gain_k, cos_tab, sin_tab)
     share = replicas == 4 and groups == 8
     if share:
-        packets, *kept = front(
-            replicas, groups, packet, cot_packet, tokens, *heads, gain_moe.reshape(1, -1)
-        )
-        kept, (hidden, rows_all, cots), far_cots = (kept[:4], kept[4:7], kept[7:])
+        packets, *kept, hidden, low = front(
+            replicas, groups, packet, tokens, *heads, gain_moe.reshape(1, -1)
+        )
+        rows_all, cots, *found = moe(
+            replicas, groups, ids, low, cot_packet, w_gate, w_up, w_down, w_router
+        )
+        far_cots, acts, (pull_part, grad_router) = (found[:6], [found[6:11]], found[11:])
+        gated = acts[0][2]
         pairs = rows_all.reshape((groups // 2, 2) + rows_all.shape[1:])
         core = lax.axis_index("shard") % 2
         near = [
-            lax.dynamic_index_in_dim(part, core, 1, keepdims=False) for part in (pairs[:2], pairs[2:])
+            lax.dynamic_slice(pairs, (start, core, 0, 0), (2, 1) + pairs.shape[2:])[:, 0]
+            for start in (0, 2)
         ]
-        rows_all, near = after((rows_all, near))
+        early, late = ([flip_replica(part, bits) for bits in (1, 2)] for part in near)
     else:
         packets = lax.all_gather(packet, "shard", axis=0)
         cot_packet, packets = after((cot_packet, packets))
@@ -1008,34 +1148,28 @@
         plain_mid, scale_mid = rms_parts(hidden)
         rows_all = lax.all_gather((plain_mid * gain_moe).astype(LOW), "shard", axis=0)
 
-    acts = [expert_acts(ids, [rows_all], [cots], w_gate, w_up, w_down, w_router)]
-    if share:
-        early, late = ([flip_replica(part, bits) for bits in (1, 2)] for part in near)
-        acts, early = after((acts, early))
-    _, _, gated, grad_gate_act, grad_up_act, dgates = acts[0]
-    router_shape = (jax.ShapeDtypeStruct(w_router.shape[::-1], WIDE),)
-    pull_part, grad_router = spread_call(
-        pull_kernel, "expert_pull", ids, (rows_all,), cots,
-        (grad_gate_act, grad_up_act, dgates), (w_gate, w_up, w_router), router_shape,
-    )
-    if share:
-        early_flipped = [flip_shard(values, 1) for values in early]
-        pull_part, late, early_flipped = after((pull_part, late, early_flipped))
+        acts = [expert_acts(ids, whole(rows_all), whole(cots), *experts)]
+        _, _, gated, grad_gate_act, grad_up_act, dgates = acts[0]
+        pull_part, grad_router = spread_call(
+            pull_kernel, "expert_pull", ids, (rows_all,), cots,
+            (grad_gate_act, grad_up_act, dgates), (w_gate, w_up, w_router),
+            (jax.ShapeDtypeStruct(w_router.shape[::-1], WIDE),),
+        )
     grad_moe_in = scatter_sum(pull_part)
     gated, pull_part = after((gated, pull_part))
-    if share:
-        diagonal = [flip_replica(early[0], 2), flip_replica(late[1], 1)]
-        late_flipped = [flip_shard(values, 1) for values in late]
-        near, pull_part = after(([early[0], late[0], early[1], late[1]], pull_part))
-        acts.append(expert_acts(ids, near, far_cots[0:2], w_gate, w_up, w_down, w_router))
-        acts, diagonal, late_flipped = after((acts, diagonal, late_flipped))
-        gated, acts = after((gated, acts))
-        flipped = [early_flipped[0], late_flipped[0], early_flipped[1], late_flipped[1]]
-        diagonal_flipped = [flip_shard(values, 1) for values in diagonal]
     (mix_part,) = spread_call(mix_kernel, "expert_mix", ids, (), cots, (gated,), (w_down,), ())
     if share:
-        mix_part, diagonal_flipped = after((mix_part, diagonal_flipped))
-        grad_moe_in, mix_part = after((grad_moe_in, mix_part))
+        acts, mix_part = after((acts, mix_part))
+        grads = add_grads(acts)
+        grads, early = after((grads, early))
+        acts = [
+            expert_acts(
+                ids, whole(*early), [(array, (0, 2)) for array in far_cots[:2]], *experts
+            )
+        ]
+        early_flipped = [flip_shard(values, 1) for values in early]
+        acts, late, early_flipped, grads = after((acts, late, early_flipped, grads))
+        grad_moe_in, acts, grads = after((grad_moe_in, acts, grads))
 
     grad_out = cot_low.astype(WIDE)
     if share:
@@ -1046,18 +1180,19 @@
     branch_low = grad_hidden.astype(LOW)
     upper = lax.all_gather(branch_low, "shard", axis=0)
     if share:
-        acts, branch_low = after((acts, branch_low))
-        started = [
-            weight_grad([act[left] for act in acts], [act[right] for act in acts])
-            for left, right in ((0, 3), (0, 4), (2, 1))
-        ]
-        upper, started = after((upper, started))
+        late, acts, grads, branch_low = after((late, acts, grads, branch_low))
+        diagonal = [flip_replica(early[0], 2), flip_replica(late[1], 1)]
+        late_flipped = [flip_shard(values, 1) for values in late]
+        acts.append(
+            expert_acts(ids, whole(*late), [(array, (2, 2)) for array in far_cots[:2]], *experts)
+        )
+        grads = add_grads(acts, grads)
+        upper, grads, diagonal, late_flipped = after((upper, grads, diagonal, late_flipped))
+        diagonal_flipped = [flip_shard(values, 1) for values in diagonal]
+        flipped = [early_flipped[0], late_flipped[0], early_flipped[1], late_flipped[1]]
     mix_part, upper = after((mix_part, upper))
     mixture = scatter_sum(mix_part)
     part, gw_low, sum_q, sum_k, sum_n = attend_backward(upper, packets, kept, *heads)
-
-    def sets(place):
-        return [act[place] for act in acts]
 
     small = jnp.concatenate(
         [
@@ -1071,10 +1206,10 @@
         ]
     )
     if share:
-        experts = (w_gate, w_up, w_down, w_router)
+        part, gw_low, diagonal_flipped = after((part, gw_low, diagonal_flipped))
         pieces = gw_low.reshape((replicas, -1) + gw_low.shape[1:])
         *act, traded, smalls = expert_acts(
-            ids, flipped, far_cots[3:5], *experts,
+            ids, whole(*flipped), whole(*far_cots[3:5]), *experts,
             trades=((pieces, "rep", replicas, True), (small, "rep", replicas, False)), collective=1,
         )
         act, traded, smalls, part, mixture = after((act, traded, smalls, part, mixture))
@@ -1083,24 +1218,17 @@
         low = jnp.sum(traded.astype(WIDE), axis=0).astype(LOW)
         small = jnp.sum(smalls, axis=0)
         *act, found, smalls = expert_acts(
-            ids, diagonal + diagonal_flipped, [far_cots[2], far_cots[5]], *experts,
+            ids, whole(*diagonal, *diagonal_flipped), whole(far_cots[2], far_cots[5]), *experts,
             trades=((low, "rep", replicas, False), (small, "shard", groups, False)), collective=2,
         )
         acts.append(act)
         gw_sum = found.reshape(gw_low.shape)
         small = jnp.sum(smalls, axis=0)
-        grad_gate_w, grad_up_w, grad_down = (
-            weight_grad(sets(left), sets(right), begun)
-            for (left, right), begun in zip(((0, 3), (0, 4), (2, 1)), started)
-        )
+        grad_gate_w, grad_up_w, grad_down = add_grads(acts, grads)
     else:
         grad_normed = scatter_sum(part)
         over_reps = lax.psum(
-            (gw_low,)
-            + tuple(
-                weight_grad(sets(left), sets(right)).astype(LOW)
-                for left, right in ((0, 3), (0, 4), (2, 1))
-            ),
+            (gw_low,) + tuple(values.astype(LOW) for values in add_grads(acts)),
             "rep",
         )
         gw_sum = over_reps[0]

time: 928 us -> 924 us (level)
    pallas_call x4 -> x5, Pallas kernels: 239 us -> 396 us  [the longest x4 200 us: expert_acts(): pl.pallas_call(functools.partial(expert_kernel, row_spans, cot_spans, bat...]
    pallas_call x1, Pallas kernels: 293 us -> 143 us  [front(): pl.pallas_call(functools.partial(front_kernel, replicas, groups), in_spec...]
    pallas_call x6 -> x9, Pallas kernels: 186 us -> 229 us  [weight_grad(): pl.pallas_call(kernel, grid=(own, right_cols // right_tile, left_cols //...]
    pallas_call x2 -> x1, Pallas kernels: 61.3 us -> 20.1 us  [spread_call(): pl.pallas_call(kernel, grid=(count // batch,), in_specs=[pl.BlockSpec(mem...]
  transfers between devices with their start and end apart: 16 -> 16, of which waited for: 1 -> 0; matrix products, arithmetic and copies ran while one was open for 2% -> 3% of each run, Pallas kernels for 58% -> 55%
where the time goes in v4:
time: 924 us; the launch traced here: 908 us
  Pallas kernels  835 us (90%)
  other arithmetic  36.1 us (4%)
  between operations  15.3 us (2%)
  local copies, waits for them, and re-layouts  12.1 us (1%)
    pallas_call x9, Pallas kernels, weight_grad(): pl.pallas_call(kernel, grid=(own, right_cols // right_tile, left_cols //...  229 us
    pallas_call x4, Pallas kernels, expert_acts(): pl.pallas_call(functools.partial(expert_kernel, row_spans, cot_spans, bat...  200 us
    pallas_call x1, Pallas kernels, moe(): pl.pallas_call(functools.partial(moe_kernel, replicas, groups), in_specs=...  196 us
    pallas_call x1, Pallas kernels, front(): pl.pallas_call(functools.partial(front_kernel, replicas, groups), in_spec...  143 us
    pallas_call x1, Pallas kernels, attend_backward(): pl.pallas_call(attend_back_kernel, grid=(count,), in_specs=[first_spec(ar...  47.3 us
    pallas_call x1, Pallas kernels, spread_call(): pl.pallas_call(kernel, grid=(count // batch,), in_specs=[pl.BlockSpec(mem...  20.1 us
  transfers between devices with their start and end apart: 16, of which 0 were waited for; matrix products, arithmetic and copies ran while one was open for 3% of the time, Pallas kernels for 55%

profile of v4, /device:TPU:0, one launch (start us, length us, event | category | flops | bytes accessed | tf_op | source)
XLA Modules:
  0.0 907.7 jit_solution(2869011697361619695)
XLA Ops:
  7.3 0.5 fusion.16
  8.5 1.5 fusion.9
  10.0 0.7 fusion.15
  10.8 0.8 fusion.12
  11.5 0.5 iota_add_fusion.ex_ref
  12.0 1.8 copy.45.wr
  13.9 0.1 broadcast_select_fusion
  14.1 0.3 fusion.4
  14.4 0.8 pad_maximum_fusion
  15.2 1.6 fusion.11
  16.8 143.3 %front.1 = (bf16[8,272,2048]{2,1,0:T(8,128)(2,1)}, f32[8,256,256]{2,1,0:T(8,128)}, f32[8,256,256]{2,1,0:T(8,128)}, bf16[8,256,256]{2,1,0:T(8,128)(2,1)}, bf16[8,...) custom-call(bf16[272,2048]{1,0:T(8,128)(2,1)} %get-tuple-element.267.packet, ...), custom_call_target="tpu_custom_call" | custom-call | flops 1048576 | bytes 65536 | tf_op jit(solution)/shard_map/front/pallas_call | solution.py:838
  160.1 195.6 %moe.1 = (bf16[8,256,2048]{2,1,0:T(8,128)(2,1)}, bf16[8,272,2048]{2,1,0:T(8,128)(2,1)}, bf16[4,272,2048]{2,1,0:T(8,128)(2,1)}, bf16[4,272,2048]{2,1,0:T(8,128)(2...) custom-call(s32[2]{0:T(128)} %iota_add_fusion.ex_ref, ...), custom_call_target="tpu_custom_call" | custom-call | flops 1048576 | bytes 65536 | tf_op jit(solution)/shard_map/moe/pallas_call | solution.py:1032
  355.7 0.0 all-gather.3.cloned.1.call-start
  355.8 4.1 dynamic-slice_bitcast_fusion
  359.9 0.6 collective-permute-start
  360.5 1.5 collective-permute-start.1
  362.0 1.5 collective-permute-start.2
  363.5 0.5 collective-permute-start.3
  364.0 20.1 %expert_mix.1 = bf16[8,256,2048]{2,1,0:T(8,128)(2,1)} custom-call(s32[2]{0:T(128)} %iota_add_fusion.ex_ref, bf16[8,272,2048]{2,1,0:T(8,128)(2,1)} %get-tuple-element.141.cot_ref, bf16[2,1152,1024]{2,1,0:T(8,128)(2,1)} %get-tuple-element.146.m_ref.refs_0_, bf16[2,1024,2048]{2,1,0:T(8,128)(2,1)} %wd.9), custom_call_target="tpu_custom_call" | custom-call | flops 1048576 | bytes 65536 | tf_op jit(solution)/shard_map/expert_mix/pallas_call | solution.py:490
  384.1 18.6 %weight_grad.10.refs_4_ = f32[2,2048,1024]{2,1,0:T(8,128)} custom-call(bf16[2,1152,2048]{2,1,0:T(8,128)(2,1)} %get-tuple-element.143.refs_0_, bf16[2,1152,1024]{2,1,0:T(8,128)(2,1)} %get-tuple-element.145.refs_1_), custom_call_target="tpu_custom_call" | custom-call | flops 1048576 | bytes 65536 | tf_op jit(solution)/shard_map/weight_grad/pallas_call | solution.py:517
  402.7 18.8 %weight_grad.9.refs_4_ = f32[2,2048,1024]{2,1,0:T(8,128)} custom-call(bf16[2,1152,2048]{2,1,0:T(8,128)(2,1)} %get-tuple-element.143.refs_0_, bf16[2,1152,1024]{2,1,0:T(8,128)(2,1)} %get-tuple-element.144.refs_1_), custom_call_target="tpu_custom_call" | custom-call | flops 1048576 | bytes 65536 | tf_op jit(solution)/shard_map/weight_grad/pallas_call | solution.py:517
  421.5 21.5 %weight_grad.11.refs_4_ = f32[2,1024,2048]{2,1,0:T(8,128)} custom-call(bf16[2,1152,1024]{2,1,0:T(8,128)(2,1)} %get-tuple-element.146.m_ref.refs_0_, bf16[2,1152,2048]{2,1,0:T(8,128)(2,1)} %get-tuple-element.147.refs_1_), custom_call_target="tpu_custom_call" | custom-call | flops 1048576 | bytes 65536 | tf_op jit(solution)/shard_map/weight_grad/pallas_call | solution.py:517
  443.0 0.1 collective-permute-start.4
  443.1 0.5 collective-permute-start.5
  443.6 35.6 %expert_acts.4 = (bf16[2,576,2048]{2,1,0:T(8,128)(2,1)}, bf16[2,576,2048]{2,1,0:T(8,128)(2,1)}, bf16[2,576,1024]{2,1,0:T(8,128)(2,1)}, bf16[2,576,1024]{2,1,0:T(...) custom-call(s32[2]{0:T(128)} %iota_add_fusion.ex_ref, bf16[2,2048,1024]{2,1,0:T(8,128)(2,1)} %wg.7, ...), custom_call_target="tpu_custom_call" | custom-call | flops 1048576 | bytes 65536 | tf_op jit(solution)/shard_map/expert_acts/pallas_call | solution.py:394
  479.3 1.6 convert_element_type.52
  480.9 0.2 copy-done
  481.2 0.2 multiply_reduce_fusion.2
  481.4 0.7 multiply_reduce_fusion
  482.1 0.2 copy-done.1
  482.3 1.7 fusion.18
  484.0 0.0 reduce-scatter.6.cloned.1.call-start
  484.0 1.6 collective-permute-start.6
  485.6 0.4 collective-permute-start.7
  486.0 0.5 collective-permute-start.9
  486.5 37.5 %expert_acts.5 = (bf16[2,576,2048]{2,1,0:T(8,128)(2,1)}, bf16[2,576,2048]{2,1,0:T(8,128)(2,1)}, bf16[2,576,1024]{2,1,0:T(8,128)(2,1)}, bf16[2,576,1024]{2,1,0:T(...) custom-call(s32[2]{0:T(128)} %iota_add_fusion.ex_ref, bf16[2,2048,1024]{2,1,0:T(8,128)(2,1)} %wg.7, ...), custom_call_target="tpu_custom_call" | custom-call | flops 1048576 | bytes 65536 | tf_op jit(solution)/shard_map/expert_acts/pallas_call | solution.py:394
  524.0 23.3 %weight_grad.13.refs_4_ = f32[2,2048,1024]{2,1,0:T(8,128)} custom-call(bf16[2,576,2048]{2,1,0:T(8,128)(2,1)} %get-tuple-element.183.refs_0_, bf16[2,576,2048]{2,1,0:T(8,128)(2,1)} %get-tuple-element.186.refs_1_, bf16[2,576,1024]{2,1,0:T(8,128)(2,1)} %get-tuple-element.190.refs_2_, ...), custom_call_target="tpu_custom_call", output_to_operand_aliasing={{}: (4, {})} | custom-call | flops 1048576 | bytes 65536 | tf_op jit(solution)/shard_map/weight_grad/pallas_call | solution.py:517
  547.3 23.1 %weight_grad.12.refs_4_ = f32[2,2048,1024]{2,1,0:T(8,128)} custom-call(bf16[2,576,2048]{2,1,0:T(8,128)(2,1)} %get-tuple-element.183.refs_0_, bf16[2,576,2048]{2,1,0:T(8,128)(2,1)} %get-tuple-element.186.refs_1_, bf16[2,576,1024]{2,1,0:T(8,128)(2,1)} %get-tuple-element.187.refs_2_, ...), custom_call_target="tpu_custom_call", output_to_operand_aliasing={{}: (4, {})} | custom-call | flops 1048576 | bytes 65536 | tf_op jit(solution)/shard_map/weight_grad/pallas_call | solution.py:517
  570.4 25.8 %weight_grad.14.refs_4_ = f32[2,1024,2048]{2,1,0:T(8,128)} custom-call(bf16[2,576,1024]{2,1,0:T(8,128)(2,1)} %get-tuple-element.193.refs_0_, bf16[2,576,1024]{2,1,0:T(8,128)(2,1)} %get-tuple-element.194.refs_1_, bf16[2,576,2048]{2,1,0:T(8,128)(2,1)} %get-tuple-element.195.refs_2_, ...), custom_call_target="tpu_custom_call", output_to_operand_aliasing={{}: (4, {})} | custom-call | flops 1048576 | bytes 65536 | tf_op jit(solution)/shard_map/weight_grad/pallas_call | solution.py:517
  596.3 0.0 reduce-scatter.8.cloned.1.call-start
  596.3 0.1 collective-permute-start.10
  596.4 0.5 collective-permute-start.11
  596.9 47.3 %attend_backward.1 = (bf16[8,256,2048]{2,1,0:T(8,128)(2,1)}, bf16[2048,1024]{1,0:T(8,128)(2,1)}, f32[1,128]{1,0:T(1,128)}, f32[1,128]{1,0:T(1,128)}, f32[1,2048]{1,0:T(1,128)}) custom-call(bf16[8,256,2048]{2,1,0:T(8,128)(2,1)} %bitcast.37, bf16[8,272,2048]{2,1,0:T(8,128)(2,1)} %get-tuple-element.206.pk_ref, f32[8,256,256]{2,1,0:T(8,128)} %get-tuple-element.207.qr_ref, ...), custom_call_target="tpu_custom_call" | custom-call | flops 1048576 | bytes 65536 | tf_op jit(solution)/shard_map/attend_backward/pallas_call | solution.py:200
  644.2 0.7 div.18
  645.0 0.7 fusion.17
  645.7 1.3 concatenate.27.refs_7_
  647.0 67.0 %expert_acts.6 = (bf16[2,1152,2048]{2,1,0:T(8,128)(2,1)}, bf16[2,1152,2048]{2,1,0:T(8,128)(2,1)}, bf16[2,1152,1024]{2,1,0:T(8,128)(2,1)}, bf16[2,1152,1024]{2,1,...) custom-call(s32[2]{0:T(128)} %iota_add_fusion.ex_ref, ...), custom_call_target="tpu_custom_call" | custom-call | flops 1048576 | bytes 65536 | tf_op jit(solution)/shard_map/expert_acts/pallas_call | solution.py:394
  714.1 2.8 convert_element_type.55
  716.9 1.1 copy-done.6
  718.0 0.7 reduce_sum.81.refs_7_
  718.7 5.1 reduce_sum.80.refs_6_
  723.8 60.0 %expert_acts.7 = (bf16[2,1152,2048]{2,1,0:T(8,128)(2,1)}, bf16[2,1152,2048]{2,1,0:T(8,128)(2,1)}, bf16[2,1152,1024]{2,1,0:T(8,128)(2,1)}, bf16[2,1152,1024]{2,1,...) custom-call(s32[2]{0:T(128)} %iota_add_fusion.ex_ref, ...), custom_call_target="tpu_custom_call" | custom-call | flops 1048576 | bytes 65536 | tf_op jit(solution)/shard_map/expert_acts/pallas_call | solution.py:394
  783.9 5.1 fusion.19
  788.9 1.4 copy.55
  790.4 1.5 reduce_sum.82
  791.9 31.4 %weight_grad.16 = f32[2,2048,1024]{2,1,0:T(8,128)} custom-call(bf16[2,1152,2048]{2,1,0:T(8,128)(2,1)} %get-tuple-element.239.refs_0_, bf16[2,1152,2048]{2,1,0:T(8,128)(2,1)} %get-tuple-element.240.refs_1_, bf16[2,1152,1024]{2,1,0:T(8,128)(2,1)} %get-tuple-element.244.refs_2_, ...), custom_call_target="tpu_custom_call", output_to_operand_aliasing={{}: (4, {})} | custom-call | flops 1048576 | bytes 65536 | tf_op jit(solution)/shard_map/weight_grad/pallas_call | solution.py:517
  823.2 31.4 %weight_grad.15 = f32[2,2048,1024]{2,1,0:T(8,128)} custom-call(bf16[2,1152,2048]{2,1,0:T(8,128)(2,1)} %get-tuple-element.239.refs_0_, bf16[2,1152,2048]{2,1,0:T(8,128)(2,1)} %get-tuple-element.240.refs_1_, bf16[2,1152,1024]{2,1,0:T(8,128)(2,1)} %get-tuple-element.241.refs_2_, ...), custom_call_target="tpu_custom_call", output_to_operand_aliasing={{}: (4, {})} | custom-call | flops 1048576 | bytes 65536 | tf_op jit(solution)/shard_map/weight_grad/pallas_call | solution.py:517
  854.6 35.2 %weight_grad.17 = f32[2,1024,2048]{2,1,0:T(8,128)} custom-call(bf16[2,1152,1024]{2,1,0:T(8,128)(2,1)} %get-tuple-element.247.refs_0_, bf16[2,1152,1024]{2,1,0:T(8,128)(2,1)} %get-tuple-element.248.refs_1_, bf16[2,1152,2048]{2,1,0:T(8,128)(2,1)} %get-tuple-element.249.refs_2_, ...), custom_call_target="tpu_custom_call", output_to_operand_aliasing={{}: (4, {})} | custom-call | flops 1048576 | bytes 65536 | tf_op jit(solution)/shard_map/weight_grad/pallas_call | solution.py:517
  889.8 0.5 slice_bitcast_fusion.1
  890.3 0.6 fusion.20
  890.9 0.7 slice_bitcast_fusion
  891.6 2.8 convert_bitcast_fusion
  894.4 1.9 fusion.5
  896.3 4.4 fusion.8
  (52 shorter events, 0.3 us)
Async XLA Ops:
  7.2 6.7 copy-start.5
  7.2 472.1 %reduce-scatter.4.cloned.1.call-start = ((), (), s32[]{:S(2)}) async-start(), calls=%async_computation.3 | async-start | bytes 9437184 | tf_op jit(solution)/shard_map/reduce_scatter | solution.py:1091
  7.3 6.8 copy-start.3
  7.3 6.8 copy-start.8
  10.0 4.4 copy-start.10
  13.9 1.3 copy-start.12
  355.7 240.5 %all-gather.3.cloned.1.call-start = ((), (), s32[]{:S(2)}) async-start(), calls=%async_computation.6 | async-start | bytes 9437184 | tf_op jit(solution)/shard_map/all_gather | solution.py:1181
  359.9 83.1 %collective-permute-start = (bf16[2,256,2048]{2,1,0:T(8,128)(2,1)S(1)}, bf16[2,256,2048]{2,1,0:T(8,128)(2,1)}, u32[]{:S(2)}, u32[]{:S(2)}) collective-permute-start(bf16[2,256,2048]{2,1,0:T(8,128)(2,1)S(1)} %get-tuple-element.255), channel_id=1, source_target_pairs={{0,8},{8,0},{16,24},{24,16},{1,9},{9,1},{17,25},{25,17},{2,10},{10... | collective-permute-start | bytes 6291464 | tf_op jit(solution)/shard_map/ppermute | solution.py:1085
  360.5 82.5 %collective-permute-start.1 = (bf16[2,256,2048]{2,1,0:T(8,128)(2,1)S(1)}, bf16[2,256,2048]{2,1,0:T(8,128)(2,1)}, u32[]{:S(2)}, u32[]{:S(2)}) collective-permute-start(bf16[2,256,2048]{2,1,0:T(8,128)(2,1)S(1)} %get-tuple-element.255), channel_id=1, source_target_pairs={{0,16},{8,24},{16,0},{24,8},{1,17},{9,25},{17,1},{25,9},{2,18},{10... | collective-permute-start | bytes 6291464 | tf_op jit(solution)/shard_map/ppermute | solution.py:1085
  362.0 117.3 %collective-permute-start.2 = (bf16[2,256,2048]{2,1,0:T(8,128)(2,1)}, bf16[2,256,2048]{2,1,0:T(8,128)(2,1)}, u32[]{:S(2)}, u32[]{:S(2)}) collective-permute-start(bf16[2,256,2048]{2,1,0:T(8,128)(2,1)} %get-tuple-element.254), channel_id=1, source_target_pairs={{0,8},{8,0},{16,24},{24,16},{1,9},{9,1},{17,25},{25,17},{2,10},{10... | collective-permute-start | bytes 6291464 | tf_op jit(solution)/shard_map/ppermute | solution.py:1085
  363.5 115.8 %collective-permute-start.3 = (bf16[2,256,2048]{2,1,0:T(8,128)(2,1)}, bf16[2,256,2048]{2,1,0:T(8,128)(2,1)}, u32[]{:S(2)}, u32[]{:S(2)}) collective-permute-start(bf16[2,256,2048]{2,1,0:T(8,128)(2,1)} %get-tuple-element.254), channel_id=1, source_target_pairs={{0,16},{8,24},{16,0},{24,8},{1,17},{9,25},{17,1},{25,9},{2,18},{10... | collective-permute-start | bytes 6291464 | tf_op jit(solution)/shard_map/ppermute | solution.py:1085
  443.0 36.3 %collective-permute-start.4 = (bf16[2,256,2048]{2,1,0:T(8,128)(2,1)}, bf16[2,256,2048]{2,1,0:T(8,128)(2,1)}, u32[]{:S(2)}, u32[]{:S(2)}) collective-permute-start(bf16[2,256,2048]{2,1,0:T(8,128)(2,1)} %collective-permute-done.refs_0_), channel_id=1, source_target_pairs={{0,1},{1,0},{2,3},{3,2},{4,5},{5,4},{6,7},{7,6},{8,9},{9,8},{10,11... | collective-permute-start | bytes 6291464 | tf_op jit(solution)/shard_map/ppermute | solution.py:1088
  443.1 36.2 %collective-permute-start.5 = (bf16[2,256,2048]{2,1,0:T(8,128)(2,1)}, bf16[2,256,2048]{2,1,0:T(8,128)(2,1)}, u32[]{:S(2)}, u32[]{:S(2)}) collective-permute-start(bf16[2,256,2048]{2,1,0:T(8,128)(2,1)} %collective-permute-done.1.refs_1_), channel_id=1, source_target_pairs={{0,1},{1,0},{2,3},{3,2},{4,5},{5,4},{6,7},{7,6},{8,9},{9,8},{10,11... | collective-permute-start | bytes 6291464 | tf_op jit(solution)/shard_map/ppermute | solution.py:1088
  479.2 1.9 copy-start
  479.3 2.1 copy-start.7
  480.9 1.3 copy-start.1
  484.0 230.1 %reduce-scatter.6.cloned.1.call-start = ((), (), s32[]{:S(2)}) async-start(), calls=%async_computation.4 | async-start | bytes 9437184 | tf_op jit(solution)/shard_map/reduce_scatter | solution.py:1091
  484.0 112.2 %collective-permute-start.6 = (bf16[2,256,2048]{2,1,0:T(8,128)(2,1)}, bf16[2,256,2048]{2,1,0:T(8,128)(2,1)}, u32[]{:S(2)}, u32[]{:S(2)}) collective-permute-start(bf16[2,256,2048]{2,1,0:T(8,128)(2,1)} %collective-permute-done.refs_0_), channel_id=1, source_target_pairs={{0,16},{8,24},{16,0},{24,8},{1,17},{9,25},{17,1},{25,9},{2,18},{10... | collective-permute-start | bytes 6291464 | tf_op jit(solution)/shard_map/ppermute | solution.py:1085
  485.6 110.6 %collective-permute-start.7 = (bf16[2,256,2048]{2,1,0:T(8,128)(2,1)}, bf16[2,256,2048]{2,1,0:T(8,128)(2,1)}, u32[]{:S(2)}, u32[]{:S(2)}) collective-permute-start(bf16[2,256,2048]{2,1,0:T(8,128)(2,1)} %collective-permute-done.3.refs_1_), channel_id=1, source_target_pairs={{0,8},{8,0},{16,24},{24,16},{1,9},{9,1},{17,25},{25,17},{2,10},{10... | collective-permute-start | bytes 6291464 | tf_op jit(solution)/shard_map/ppermute | solution.py:1085
  486.0 110.2 %collective-permute-start.8 = (bf16[2,256,2048]{2,1,0:T(8,128)(2,1)}, bf16[2,256,2048]{2,1,0:T(8,128)(2,1)}, u32[]{:S(2)}, u32[]{:S(2)}) collective-permute-start(bf16[2,256,2048]{2,1,0:T(8,128)(2,1)} %collective-permute-done.2.refs_0_), channel_id=1, source_target_pairs={{0,1},{1,0},{2,3},{3,2},{4,5},{5,4},{6,7},{7,6},{8,9},{9,8},{10,11... | collective-permute-start | bytes 6291464 | tf_op jit(solution)/shard_map/ppermute | solution.py:1088
  486.0 110.2 %collective-permute-start.9 = (bf16[2,256,2048]{2,1,0:T(8,128)(2,1)}, bf16[2,256,2048]{2,1,0:T(8,128)(2,1)}, u32[]{:S(2)}, u32[]{:S(2)}) collective-permute-start(bf16[2,256,2048]{2,1,0:T(8,128)(2,1)} %collective-permute-done.3.refs_1_), channel_id=1, source_target_pairs={{0,1},{1,0},{2,3},{3,2},{4,5},{5,4},{6,7},{7,6},{8,9},{9,8},{10,11... | collective-permute-start | bytes 6291464 | tf_op jit(solution)/shard_map/ppermute | solution.py:1088
  596.3 298.1 %reduce-scatter.8.cloned.1.call-start = ((), (), s32[]{:S(2)}) async-start(), calls=%async_computation.5 | async-start | bytes 9437184 | tf_op jit(solution)/shard_map/reduce_scatter | solution.py:1091
  596.3 50.7 %collective-permute-start.10 = (bf16[2,256,2048]{2,1,0:T(8,128)(2,1)}, bf16[2,256,2048]{2,1,0:T(8,128)(2,1)}, u32[]{:S(2)}, u32[]{:S(2)}) collective-permute-start(bf16[2,256,2048]{2,1,0:T(8,128)(2,1)} %collective-permute-done.6.refs_0_), channel_id=1, source_target_pairs={{0,1},{1,0},{2,3},{3,2},{4,5},{5,4},{6,7},{7,6},{8,9},{9,8},{10,11... | collective-permute-start | bytes 6291464 | tf_op jit(solution)/shard_map/ppermute | solution.py:1088
  596.4 50.6 %collective-permute-start.11 = (bf16[2,256,2048]{2,1,0:T(8,128)(2,1)}, bf16[2,256,2048]{2,1,0:T(8,128)(2,1)}, u32[]{:S(2)}, u32[]{:S(2)}) collective-permute-start(bf16[2,256,2048]{2,1,0:T(8,128)(2,1)} %collective-permute-done.7.refs_1_), channel_id=1, source_target_pairs={{0,1},{1,0},{2,3},{3,2},{4,5},{5,4},{6,7},{7,6},{8,9},{9,8},{10,11... | collective-permute-start | bytes 6291464 | tf_op jit(solution)/shard_map/ppermute | solution.py:1088
  596.9 48.7 %copy-start.9 = (f32[16,2048]{1,0:T(8,128)S(1)}, f32[16,2048]{1,0:T(8,128)}, u32[]{:S(2)}) copy-start(f32[16,2048]{1,0:T(8,128)} %get-tuple-element.216) | copy-start | bytes 393220
  716.9 1.1 copy-start.6
  889.8 4.6 copy-start.4
  889.8 4.6 copy-start.11
  894.4 1.9 copy-start.2
Sparse Core Ops, SparseCore 0:
  355.8 86.8 reduce-scatter.3
  484.1 79.3 all-gather.2
  596.4 86.9 reduce-scatter.5
  717.0 111.9 reduce-scatter.7

commit v5 on v4

--- a/solution.py
+++ b/solution.py
@@ -503,36 +503,62 @@
     )(ids, *by_seq, cots, *by_slot, *fixed)
 
 
-def weight_grad(lefts, rights, start=None):
+def weight_grad(lefts, rights, starts=None, trades=(), collective=None, in_place=True):
     own, _, left_cols = lefts[0].shape
-    right_cols = rights[0].shape[-1]
-    sets = len(lefts)
-    left_tile, right_tile = (min(512, left_cols), min(1024, right_cols))
+    right_cols = rights[0][0].shape[-1]
+    sets, outs = (len(lefts), len(rights))
+    tile = min(512, left_cols)
+    trades = Trades(trades)
+    number, begun = (len(trades.trades), 0 if starts is None else outs)
+    first = sets * (1 + outs)
 
     def kernel(*refs):
-        total = sum(dot_tn(refs[i][0], refs[sets + i][0]) for i in range(sets))
-        refs[-1][0] = total if start is None else total + refs[2 * sets][0]
-
-    out_spec = pl.BlockSpec((1, left_tile, right_tile), lambda e, r, l: (e, l, r))
+        refs, tail = (refs[: first + begun], refs[first + begun :])
+        results = tail[number : number + outs]
+        trades.bind(
+            tail[:number], tail[number + outs : 2 * number + outs], tail[2 * number + outs :]
+        )
+        if number:
+
+            @pl.when((pl.program_id(0) == 0) & (pl.program_id(1) == 0))
+            def _():
+                trades.start()
+
+        for place in range(outs):
+            total = sum(
+                dot_tn(refs[i][0], refs[sets * (1 + place) + i][0]) for i in range(sets)
+            )
+            results[place][0] = total + refs[first + place][0] if begun else total
+        if number:
+
+            @pl.when((pl.program_id(0) == own - 1) & (pl.program_id(1) == left_cols // tile - 1))
+            def _():
+                trades.finish()
+
+    out_spec = pl.BlockSpec((1, tile, right_cols), lambda e, l: (e, l, 0))
+    flat = [array for group in rights for array in group]
     return pl.pallas_call(
         kernel,
-        grid=(own, right_cols // right_tile, left_cols // left_tile),
+        grid=(own, left_cols // tile),
         in_specs=[
-            pl.BlockSpec((1, array.shape[1], left_tile), lambda e, r, l: (e, 0, l))
-            for array in lefts
+            pl.BlockSpec((1, array.shape[1], tile), lambda e, l: (e, 0, l)) for array in lefts
         ]
-        + [
-            pl.BlockSpec((1, array.shape[1], right_tile), lambda e, r, l: (e, 0, r))
-            for array in rights
-        ]
-        + [out_spec] * (start is not None),
-        out_specs=out_spec,
-        out_shape=jax.ShapeDtypeStruct((own, left_cols, right_cols), WIDE),
-        input_output_aliases={} if start is None else {2 * sets: 0},
-        compiler_params=pltpu.CompilerParams(vmem_limit_bytes=VMEM_BYTES),
+        + [pl.BlockSpec((1,) + array.shape[1:], lambda e, l: (e, 0, 0)) for array in flat]
+        + [out_spec] * begun
+        + trades.in_specs,
+        out_specs=[out_spec] * outs + trades.out_specs,
+        out_shape=[jax.ShapeDtypeStruct((own, left_cols, right_cols), WIDE)] * outs
+        + trades.out_shapes,
+        scratch_shapes=trades.scratch,
+        input_output_aliases={first + place: place for place in range(begun * in_place)},
+        compiler_params=pltpu.CompilerParams(
+            vmem_limit_bytes=VMEM_BYTES,
+            collective_id=collective,
+            has_side_effects=collective is not None,
+        ),
         cost_estimate=COST,
         name="weight_grad",
-    )(*lefts, *rights, *([] if start is None else [start]))
+    )(*lefts, *flat, *(starts or []), *trades.arrays)
 
 
 CHUNKS = 4
@@ -1097,15 +1123,13 @@
     def whole(*arrays):
         return [(array, (0, array.shape[0])) for array in arrays]
 
-    def add_grads(acts, grads=None):
-        return [
-            weight_grad(
-                [act[left] for act in acts],
-                [act[right] for act in acts],
-                None if grads is None else grads[number],
-            )
-            for number, (left, right) in enumerate(((0, 3), (0, 4), (2, 1)))
-        ]
+    def in_grads(acts, grads=None, **more):
+        return weight_grad(
+            [act[0] for act in acts], [[act[place] for act in acts] for place in (3, 4)], grads, **more
+        )
+
+    def down_grads(acts, grads=None):
+        return weight_grad([act[2] for act in acts], [[act[1] for act in acts]], grads)
 
     inputs = tokens.astype(WIDE)
     row_mask = (jnp.arange(row_count, dtype=jnp.int32) < lengths[0])[:, None]
@@ -1160,16 +1184,12 @@
     (mix_part,) = spread_call(mix_kernel, "expert_mix", ids, (), cots, (gated,), (w_down,), ())
     if share:
         acts, mix_part = after((acts, mix_part))
-        grads = add_grads(acts)
-        grads, early = after((grads, early))
-        acts = [
-            expert_acts(
-                ids, whole(*early), [(array, (0, 2)) for array in far_cots[:2]], *experts
-            )
-        ]
+        in_sums = in_grads(acts)
+        in_sums, early = after((in_sums, early))
         early_flipped = [flip_shard(values, 1) for values in early]
-        acts, late, early_flipped, grads = after((acts, late, early_flipped, grads))
-        grad_moe_in, acts, grads = after((grad_moe_in, acts, grads))
+        down_sums = down_grads(acts)
+        down_sums, late, early_flipped = after((down_sums, late, early_flipped))
+        grad_moe_in, in_sums, down_sums = after((grad_moe_in, in_sums, down_sums))
 
     grad_out = cot_low.astype(WIDE)
     if share:
@@ -1180,16 +1200,16 @@
     branch_low = grad_hidden.astype(LOW)
     upper = lax.all_gather(branch_low, "shard", axis=0)
     if share:
-        late, acts, grads, branch_low = after((late, acts, grads, branch_low))
+        late, in_sums, down_sums, branch_low = after((late, in_sums, down_sums, branch_low))
         diagonal = [flip_replica(early[0], 2), flip_replica(late[1], 1)]
         late_flipped = [flip_shard(values, 1) for values in late]
-        acts.append(
-            expert_acts(ids, whole(*late), [(array, (2, 2)) for array in far_cots[:2]], *experts)
-        )
-        grads = add_grads(acts, grads)
-        upper, grads, diagonal, late_flipped = after((upper, grads, diagonal, late_flipped))
+        branch_low, late_flipped = after((branch_low, late_flipped))
+        rows = whole(early[0], late[0], early[1], late[1])
+        for pair in zip(early_flipped, late_flipped):
+            rows = rows + whole(*pair)
+        acts = [expert_acts(ids, rows, whole(*far_cots[:2], *far_cots[3:5]), *experts)]
+        upper, acts, diagonal = after((upper, acts, diagonal))
         diagonal_flipped = [flip_shard(values, 1) for values in diagonal]
-        flipped = [early_flipped[0], late_flipped[0], early_flipped[1], late_flipped[1]]
     mix_part, upper = after((mix_part, upper))
     mixture = scatter_sum(mix_part)
     part, gw_low, sum_q, sum_k, sum_n = attend_backward(upper, packets, kept, *heads)
@@ -1209,26 +1229,27 @@
         part, gw_low, diagonal_flipped = after((part, gw_low, diagonal_flipped))
         pieces = gw_low.reshape((replicas, -1) + gw_low.shape[1:])
         *act, traded, smalls = expert_acts(
-            ids, whole(*flipped), whole(*far_cots[3:5]), *experts,
+            ids, whole(*diagonal, *diagonal_flipped), whole(far_cots[2], far_cots[5]), *experts,
             trades=((pieces, "rep", replicas, True), (small, "rep", replicas, False)), collective=1,
         )
         act, traded, smalls, part, mixture = after((act, traded, smalls, part, mixture))
-        acts = [act]
         grad_normed = scatter_sum(part)
         low = jnp.sum(traded.astype(WIDE), axis=0).astype(LOW)
         small = jnp.sum(smalls, axis=0)
-        *act, found, smalls = expert_acts(
-            ids, whole(*diagonal, *diagonal_flipped), whole(far_cots[2], far_cots[5]), *experts,
+        *in_sums, found, smalls = in_grads(
+            acts, in_sums,
             trades=((low, "rep", replicas, False), (small, "shard", groups, False)), collective=2,
         )
-        acts.append(act)
+        in_sums, found, smalls, act = after((in_sums, found, smalls, act))
         gw_sum = found.reshape(gw_low.shape)
         small = jnp.sum(smalls, axis=0)
-        grad_gate_w, grad_up_w, grad_down = add_grads(acts, grads)
+        grad_gate_w, grad_up_w = in_grads([act], in_sums, in_place=False)
+        (grad_down,) = down_grads(acts + [act], down_sums)
     else:
         grad_normed = scatter_sum(part)
         over_reps = lax.psum(
-            (gw_low,) + tuple(values.astype(LOW) for values in add_grads(acts)),
+            (gw_low,)
+            + tuple(values.astype(LOW) for values in in_grads(acts) + down_grads(acts)),
             "rep",
         )
         gw_sum = over_reps[0]

time: 924 us -> 856 us (0.926)
  Pallas kernels: 835 us -> 744 us
  waiting for transfers between devices: 0.16 us -> 23.9 us
    pallas_call x9 -> x5, Pallas kernels: 229 us -> 186 us  [weight_grad(): pl.pallas_call(kernel, grid=(own, left_cols // tile), in_specs=[pl.BlockS...]
    pallas_call x4 -> x2, Pallas kernels: 200 us -> 164 us  [expert_acts(): pl.pallas_call(functools.partial(expert_kernel, row_spans, cot_spans, bat...]
    ppermute x6, waiting for transfers between devices: 0.02 us -> 19.8 us  [flip_replica(): return lax.ppermute(values, 'rep', [(i, i ^ bits) for i in range(replicas)])]
    pallas_call x1, Pallas kernels: 196 us -> 184 us  [moe(): pl.pallas_call(functools.partial(moe_kernel, replicas, groups), in_specs=...]
  transfers between devices with their start and end apart: 16 -> 16, of which waited for: 0 -> 4; matrix products, arithmetic and copies ran while one was open for 3% -> 3% of each run, Pallas kernels for 55% -> 50%
where the time goes in v5:
time: 856 us; the launch traced here: 840 us
  Pallas kernels  744 us (87%)
  other arithmetic  35.3 us (4%)
  waiting for transfers between devices  23.9 us (3%)
  between operations  15.2 us (2%)
  local copies, waits for them, and re-layouts  12.1 us (1%)
  starting transfers between devices  9 us (1%)
    pallas_call x5, Pallas kernels, weight_grad(): pl.pallas_call(kernel, grid=(own, left_cols // tile), in_specs=[pl.BlockS...  186 us
    pallas_call x1, Pallas kernels, moe(): pl.pallas_call(functools.partial(moe_kernel, replicas, groups), in_specs=...  184 us
    pallas_call x2, Pallas kernels, expert_acts(): pl.pallas_call(functools.partial(expert_kernel, row_spans, cot_spans, bat...  164 us
    pallas_call x1, Pallas kernels, front(): pl.pallas_call(functools.partial(front_kernel, replicas, groups), in_spec...  143 us
    pallas_call x1, Pallas kernels, attend_backward(): pl.pallas_call(attend_back_kernel, grid=(count,), in_specs=[first_spec(ar...  46.4 us
    pallas_call x1, Pallas kernels, spread_call(): pl.pallas_call(kernel, grid=(count // batch,), in_specs=[pl.BlockSpec(mem...  20.1 us
    ppermute x6, waiting for transfers between devices, flip_replica(): return lax.ppermute(values, 'rep', [(i, i ^ bits) for i in range(replicas)])  19.8 us
  transfers between devices with their start and end apart: 16, of which 4 were waited for; matrix products, arithmetic and copies ran while one was open for 3% of the time, Pallas kernels for 50%

profile of v5, /device:TPU:0, one launch (start us, length us, event | category | flops | bytes accessed | tf_op | source)
XLA Modules:
  0.0 839.8 jit_solution(6638990042417445727)
XLA Ops:
  7.2 0.0 reduce-scatter.4.cloned.1.call-start
  7.3 0.5 iota_add_fusion.ex_ref
  7.8 1.9 copy.40.wr
  9.7 0.7 fusion.15
  10.5 0.1 fusion.12
  11.3 1.5 fusion.9
  12.8 0.5 fusion.16
  13.3 0.1 broadcast_select_fusion
  13.5 0.3 fusion.4
  13.8 0.8 pad_maximum_fusion
  14.6 1.6 fusion.11
  16.3 143.4 %front.1 = (bf16[8,272,2048]{2,1,0:T(8,128)(2,1)}, f32[8,256,256]{2,1,0:T(8,128)}, f32[8,256,256]{2,1,0:T(8,128)}, bf16[8,256,256]{2,1,0:T(8,128)(2,1)}, bf16[8,...) custom-call(bf16[272,2048]{1,0:T(8,128)(2,1)} %get-tuple-element.245.packet, ...), custom_call_target="tpu_custom_call" | custom-call | flops 1048576 | bytes 65536 | tf_op jit(solution)/shard_map/front/pallas_call | solution.py:864
  159.7 184.4 %moe.1 = (bf16[8,256,2048]{2,1,0:T(8,128)(2,1)}, bf16[8,272,2048]{2,1,0:T(8,128)(2,1)}, bf16[4,272,2048]{2,1,0:T(8,128)(2,1)}, bf16[4,272,2048]{2,1,0:T(8,128)(2...) custom-call(s32[2]{0:T(128)} %iota_add_fusion.ex_ref, ...), custom_call_target="tpu_custom_call" | custom-call | flops 1048576 | bytes 65536 | tf_op jit(solution)/shard_map/moe/pallas_call | solution.py:1058
  344.1 0.0 all-gather.3.cloned.1.call-start
  344.1 4.1 dynamic-slice_bitcast_fusion
  348.3 0.5 collective-permute-start
  348.8 1.5 collective-permute-start.1
  350.3 1.5 collective-permute-start.2
  351.8 0.5 collective-permute-start.3
  352.3 20.1 %expert_mix.1 = bf16[8,256,2048]{2,1,0:T(8,128)(2,1)} custom-call(s32[2]{0:T(128)} %iota_add_fusion.ex_ref, bf16[8,272,2048]{2,1,0:T(8,128)(2,1)} %get-tuple-element.130.cot_ref, bf16[2,1152,1024]{2,1,0:T(8,128)(2,1)} %get-tuple-element.140.m_ref.refs_0_, bf16[2,1024,2048]{2,1,0:T(8,128)(2,1)} %wd.5), custom_call_target="tpu_custom_call" | custom-call | flops 1048576 | bytes 65536 | tf_op jit(solution)/shard_map/expert_mix/pallas_call | solution.py:490
  372.4 29.7 %weight_grad.5 = (f32[2,2048,1024]{2,1,0:T(8,128)}, f32[2,2048,1024]{2,1,0:T(8,128)}) custom-call(bf16[2,1152,2048]{2,1,0:T(8,128)(2,1)} %get-tuple-element.132.refs_0_, bf16[2,1152,1024]{2,1,0:T(8,128)(2,1)} %get-tuple-element.133.refs_1_, bf16[2,1152,1024]{2,1,0:T(8,128)(2,1)} %get-tuple-element.134.refs_2_), custom_call_target="tpu_custom_call" | custom-call | flops 1048576 | bytes 65536 | tf_op jit(solution)/shard_map/weight_grad/pallas_call | solution.py:540
  402.1 0.1 collective-permute-start.4
  402.2 0.5 collective-permute-start.5
  402.7 18.7 %weight_grad.6.refs_4_ = f32[2,1024,2048]{2,1,0:T(8,128)} custom-call(bf16[2,1152,1024]{2,1,0:T(8,128)(2,1)} %get-tuple-element.140.m_ref.refs_0_, bf16[2,1152,2048]{2,1,0:T(8,128)(2,1)} %get-tuple-element.141.refs_1_), custom_call_target="tpu_custom_call" | custom-call | flops 1048576 | bytes 65536 | tf_op jit(solution)/shard_map/weight_grad/pallas_call | solution.py:540
  421.4 19.6 %collective-permute-done.2.refs_1_ = bf16[2,256,2048]{2,1,0:T(8,128)(2,1)} collective-permute-done((bf16[2,256,2048]{2,1,0:T(8,128)(2,1)}, bf16[2,256,2048]{2,1,0:T(8,128)(2,1)}, u32[]{:S(2)}, u32[]{:S(2)}) %collective-permute-start.2) | collective-permute-done | bytes 2097184 | tf_op jit(solution)/shard_map/ppermute | solution.py:1111
  441.0 0.2 collective-permute-done.3.refs_3_
  441.3 1.5 convert_element_type.52
  442.7 0.2 multiply_reduce_fusion.2
  443.0 0.7 multiply_reduce_fusion
  443.7 0.4 copy-done.1
  444.1 1.7 fusion.18
  445.8 0.0 reduce-scatter.6.cloned.1.call-start
  445.8 0.1 collective-permute-start.6
  445.9 0.5 collective-permute-start.7
  446.4 1.5 collective-permute-start.8
  447.9 1.6 collective-permute-start.9
  449.5 0.9 collective-permute-done.6.refs_5_
  450.4 3.0 collective-permute-done.7.refs_7_
  453.4 96.7 %expert_acts.2 = (bf16[2,2304,2048]{2,1,0:T(8,128)(2,1)}, bf16[2,2304,2048]{2,1,0:T(8,128)(2,1)}, bf16[2,2304,1024]{2,1,0:T(8,128)(2,1)}, bf16[2,2304,1024]{2,1,...) custom-call(s32[2]{0:T(128)} %iota_add_fusion.ex_ref, bf16[2,2048,1024]{2,1,0:T(8,128)(2,1)} %wg.3, ...), custom_call_target="tpu_custom_call" | custom-call | flops 1048576 | bytes 65536 | tf_op jit(solution)/shard_map/expert_acts/pallas_call | solution.py:394
  550.2 0.0 reduce-scatter.8.cloned.1.call-start
  550.2 0.2 collective-permute-start.10
  550.4 0.4 collective-permute-start.11
  550.8 46.4 %attend_backward.1 = (bf16[8,256,2048]{2,1,0:T(8,128)(2,1)}, bf16[2048,1024]{1,0:T(8,128)(2,1)}, f32[1,128]{1,0:T(1,128)}, f32[1,128]{1,0:T(1,128)}, f32[1,2048]{1,0:T(1,128)}) custom-call(bf16[8,256,2048]{2,1,0:T(8,128)(2,1)} %bitcast.37, bf16[8,272,2048]{2,1,0:T(8,128)(2,1)} %get-tuple-element.173.pk_ref, f32[8,256,256]{2,1,0:T(8,128)} %get-tuple-element.174.qr_ref, ...), custom_call_target="tpu_custom_call" | custom-call | flops 1048576 | bytes 65536 | tf_op jit(solution)/shard_map/attend_backward/pallas_call | solution.py:200
  597.2 0.7 div.18
  597.9 0.7 fusion.17
  598.6 1.3 concatenate.27.refs_7_
  600.0 67.4 %expert_acts.3 = (bf16[2,1152,2048]{2,1,0:T(8,128)(2,1)}, bf16[2,1152,2048]{2,1,0:T(8,128)(2,1)}, bf16[2,1152,1024]{2,1,0:T(8,128)(2,1)}, bf16[2,1152,1024]{2,1,...) custom-call(s32[2]{0:T(128)} %iota_add_fusion.ex_ref, ...), custom_call_target="tpu_custom_call" | custom-call | flops 1048576 | bytes 65536 | tf_op jit(solution)/shard_map/expert_acts/pallas_call | solution.py:394
  667.4 0.0 reduce-scatter.6.cloned.1.call-done
  667.4 2.8 convert_element_type.55
  670.2 1.1 copy-done.6
  671.3 0.7 reduce_sum.81.refs_6_
  672.0 4.4 reduce_sum.80.refs_5_
  676.4 60.0 %weight_grad.7 = (f32[2,2048,1024]{2,1,0:T(8,128)}, f32[2,2048,1024]{2,1,0:T(8,128)}, bf16[4,512,1024]{2,1,0:T(8,128)(2,1)}, f32[8,24,2048]{2,1,0:T(8,128)}) custom-call(bf16[2,2304,2048]{2,1,0:T(8,128)(2,1)} %get-tuple-element.200.refs_0_, bf16[2,2304,1024]{2,1,0:T(8,128)(2,1)} %get-tuple-element.201.refs_1_, ...), custom_call_target="tpu_custom_call", output_to_operand_aliasing={{0}: (3, {}), {1}: (4, {})} | custom-call | flops 1048576 | bytes 65536 | tf_op jit(solution)/shard_map/weight_grad/pallas_call | solution.py:540
  736.4 1.5 reduce_sum.82
  738.0 5.1 fusion.19
  743.1 1.4 copy.48
  744.5 35.8 %weight_grad.8 = (f32[2,2048,1024]{2,1,0:T(8,128)}, f32[2,2048,1024]{2,1,0:T(8,128)}) custom-call(bf16[2,1152,2048]{2,1,0:T(8,128)(2,1)} %get-tuple-element.218.refs_0_, bf16[2,1152,1024]{2,1,0:T(8,128)(2,1)} %get-tuple-element.219.refs_1_, bf16[2,1152,1024]{2,1,0:T(8,128)(2,1)} %get-tuple-element.220.refs_2_, f32[2,2048,1024]{2,1,0:T(8,128)} %get-tuple-element.221.refs_3_, ...), custom_call_target="tpu_custom_call" | custom-call | flops 1048576 | bytes 65536 | tf_op jit(solution)/shard_map/weight_grad/pallas_call | solution.py:540
  780.3 41.6 %weight_grad.9 = f32[2,1024,2048]{2,1,0:T(8,128)} custom-call(bf16[2,2304,1024]{2,1,0:T(8,128)(2,1)} %get-tuple-element.225.refs_0_, bf16[2,1152,1024]{2,1,0:T(8,128)(2,1)} %get-tuple-element.226.refs_1_, bf16[2,2304,2048]{2,1,0:T(8,128)(2,1)} %get-tuple-element.227.refs_2_, ...), custom_call_target="tpu_custom_call", output_to_operand_aliasing={{}: (4, {})} | custom-call | flops 1048576 | bytes 65536 | tf_op jit(solution)/shard_map/weight_grad/pallas_call | solution.py:540
  821.9 0.5 slice_bitcast_fusion.1
  822.4 0.6 fusion.20
  823.0 0.7 slice_bitcast_fusion
  823.7 2.8 convert_bitcast_fusion
  826.5 1.9 fusion.5
  828.4 4.4 fusion.8
  (40 shorter events, 0.2 us)
Async XLA Ops:
  7.2 6.1 copy-start.5
  7.2 434.1 %reduce-scatter.4.cloned.1.call-start = ((), (), s32[]{:S(2)}) async-start(), calls=%async_computation.3 | async-start | bytes 9437184 | tf_op jit(solution)/shard_map/reduce_scatter | solution.py:1117
  7.8 5.7 copy-start.3
  7.8 5.7 copy-start.8
  344.1 206.1 %all-gather.3.cloned.1.call-start = ((), (), s32[]{:S(2)}) async-start(), calls=%async_computation.6 | async-start | bytes 9437184 | tf_op jit(solution)/shard_map/all_gather | solution.py:1201
  348.3 53.8 %collective-permute-start = (bf16[2,256,2048]{2,1,0:T(8,128)(2,1)S(1)}, bf16[2,256,2048]{2,1,0:T(8,128)(2,1)}, u32[]{:S(2)}, u32[]{:S(2)}) collective-permute-start(bf16[2,256,2048]{2,1,0:T(8,128)(2,1)S(1)} %get-tuple-element.233), channel_id=1, source_target_pairs={{0,8},{8,0},{16,24},{24,16},{1,9},{9,1},{17,25},{25,17},{2,10},{10... | collective-permute-start | bytes 6291464 | tf_op jit(solution)/shard_map/ppermute | solution.py:1111
  348.8 53.3 %collective-permute-start.1 = (bf16[2,256,2048]{2,1,0:T(8,128)(2,1)S(1)}, bf16[2,256,2048]{2,1,0:T(8,128)(2,1)}, u32[]{:S(2)}, u32[]{:S(2)}) collective-permute-start(bf16[2,256,2048]{2,1,0:T(8,128)(2,1)S(1)} %get-tuple-element.233), channel_id=1, source_target_pairs={{0,16},{8,24},{16,0},{24,8},{1,17},{9,25},{17,1},{25,9},{2,18},{10... | collective-permute-start | bytes 6291464 | tf_op jit(solution)/shard_map/ppermute | solution.py:1111
  350.3 90.7 %collective-permute-start.2 = (bf16[2,256,2048]{2,1,0:T(8,128)(2,1)}, bf16[2,256,2048]{2,1,0:T(8,128)(2,1)}, u32[]{:S(2)}, u32[]{:S(2)}) collective-permute-start(bf16[2,256,2048]{2,1,0:T(8,128)(2,1)} %get-tuple-element.232), channel_id=1, source_target_pairs={{0,8},{8,0},{16,24},{24,16},{1,9},{9,1},{17,25},{25,17},{2,10},{10... | collective-permute-start | bytes 6291464 | tf_op jit(solution)/shard_map/ppermute | solution.py:1111
  351.8 89.4 %collective-permute-start.3 = (bf16[2,256,2048]{2,1,0:T(8,128)(2,1)}, bf16[2,256,2048]{2,1,0:T(8,128)(2,1)}, u32[]{:S(2)}, u32[]{:S(2)}) collective-permute-start(bf16[2,256,2048]{2,1,0:T(8,128)(2,1)} %get-tuple-element.232), channel_id=1, source_target_pairs={{0,16},{8,24},{16,0},{24,8},{1,17},{9,25},{17,1},{25,9},{2,18},{10... | collective-permute-start | bytes 6291464 | tf_op jit(solution)/shard_map/ppermute | solution.py:1111
  402.1 39.1 %collective-permute-start.4 = (bf16[2,256,2048]{2,1,0:T(8,128)(2,1)}, bf16[2,256,2048]{2,1,0:T(8,128)(2,1)}, u32[]{:S(2)}, u32[]{:S(2)}) collective-permute-start(bf16[2,256,2048]{2,1,0:T(8,128)(2,1)} %collective-permute-done.refs_0_), channel_id=1, source_target_pairs={{0,1},{1,0},{2,3},{3,2},{4,5},{5,4},{6,7},{7,6},{8,9},{9,8},{10,11... | collective-permute-start | bytes 6291464 | tf_op jit(solution)/shard_map/ppermute | solution.py:1114
  402.2 39.1 %collective-permute-start.5 = (bf16[2,256,2048]{2,1,0:T(8,128)(2,1)}, bf16[2,256,2048]{2,1,0:T(8,128)(2,1)}, u32[]{:S(2)}, u32[]{:S(2)}) collective-permute-start(bf16[2,256,2048]{2,1,0:T(8,128)(2,1)} %collective-permute-done.1.refs_2_), channel_id=1, source_target_pairs={{0,1},{1,0},{2,3},{3,2},{4,5},{5,4},{6,7},{7,6},{8,9},{9,8},{10,11... | collective-permute-start | bytes 6291464 | tf_op jit(solution)/shard_map/ppermute | solution.py:1114
  421.4 21.3 %copy-start = (f32[256,2048]{1,0:T(8,128)S(1)}, f32[256,2048]{1,0:T(8,128)}, u32[]{:S(2)}) copy-start(f32[256,2048]{1,0:T(8,128)} %get-tuple-element.146) | copy-start | bytes 6291460
  421.4 21.6 %copy-start.7 = (f32[2048]{0:T(1024)S(1)}, f32[2048]{0:T(1024)}, u32[]{:S(2)}) copy-start(f32[2048]{0:T(1024)} %param.26) | copy-start | bytes 24580
  442.7 1.3 copy-start.1
  445.8 221.6 %reduce-scatter.6.cloned.1.call-start = ((), (), s32[]{:S(2)}) async-start(), calls=%async_computation.4 | async-start | bytes 9437184 | tf_op jit(solution)/shard_map/reduce_scatter | solution.py:1117
  445.8 4.6 collective-permute-start.6
  445.9 7.5 collective-permute-start.7
  446.4 103.7 %collective-permute-start.8 = (bf16[2,256,2048]{2,1,0:T(8,128)(2,1)}, bf16[2,256,2048]{2,1,0:T(8,128)(2,1)}, u32[]{:S(2)}, u32[]{:S(2)}) collective-permute-start(bf16[2,256,2048]{2,1,0:T(8,128)(2,1)} %collective-permute-done.refs_0_), channel_id=1, source_target_pairs={{0,16},{8,24},{16,0},{24,8},{1,17},{9,25},{17,1},{25,9},{2,18},{10... | collective-permute-start | bytes 6291464 | tf_op jit(solution)/shard_map/ppermute | solution.py:1111
  447.9 102.2 %collective-permute-start.9 = (bf16[2,256,2048]{2,1,0:T(8,128)(2,1)}, bf16[2,256,2048]{2,1,0:T(8,128)(2,1)}, u32[]{:S(2)}, u32[]{:S(2)}) collective-permute-start(bf16[2,256,2048]{2,1,0:T(8,128)(2,1)} %collective-permute-done.3.refs_3_), channel_id=1, source_target_pairs={{0,8},{8,0},{16,24},{24,16},{1,9},{9,1},{17,25},{25,17},{2,10},{10... | collective-permute-start | bytes 6291464 | tf_op jit(solution)/shard_map/ppermute | solution.py:1111
  550.2 276.3 %reduce-scatter.8.cloned.1.call-start = ((), (), s32[]{:S(2)}) async-start(), calls=%async_computation.5 | async-start | bytes 9437184 | tf_op jit(solution)/shard_map/reduce_scatter | solution.py:1117
  550.2 49.7 %collective-permute-start.10 = (bf16[2,256,2048]{2,1,0:T(8,128)(2,1)}, bf16[2,256,2048]{2,1,0:T(8,128)(2,1)}, u32[]{:S(2)}, u32[]{:S(2)}) collective-permute-start(bf16[2,256,2048]{2,1,0:T(8,128)(2,1)} %collective-permute-done.8.refs_0_), channel_id=1, source_target_pairs={{0,1},{1,0},{2,3},{3,2},{4,5},{5,4},{6,7},{7,6},{8,9},{9,8},{10,11... | collective-permute-start | bytes 6291464 | tf_op jit(solution)/shard_map/ppermute | solution.py:1114
  550.4 49.5 %collective-permute-start.11 = (bf16[2,256,2048]{2,1,0:T(8,128)(2,1)}, bf16[2,256,2048]{2,1,0:T(8,128)(2,1)}, u32[]{:S(2)}, u32[]{:S(2)}) collective-permute-start(bf16[2,256,2048]{2,1,0:T(8,128)(2,1)} %collective-permute-done.9.refs_1_), channel_id=1, source_target_pairs={{0,1},{1,0},{2,3},{3,2},{4,5},{5,4},{6,7},{7,6},{8,9},{9,8},{10,11... | collective-permute-start | bytes 6291464 | tf_op jit(solution)/shard_map/ppermute | solution.py:1114
  550.8 47.8 %copy-start.9 = (f32[16,2048]{1,0:T(8,128)S(1)}, f32[16,2048]{1,0:T(8,128)}, u32[]{:S(2)}) copy-start(f32[16,2048]{1,0:T(8,128)} %get-tuple-element.185) | copy-start | bytes 393220
  670.2 1.1 copy-start.6
  821.9 4.6 copy-start.4
  826.5 1.9 copy-start.2
Sparse Core Ops, SparseCore 0:
  344.2 86.9 reduce-scatter.3
  445.9 80.3 all-gather.2
  550.3 88.4 reduce-scatter.5
  670.3 113.2 reduce-scatter.7

commit v6 on v5

--- a/solution.py
+++ b/solution.py
@@ -276,7 +276,10 @@
 UNIT = 2
 
 
-def expert_block(expert, rows_in, cots_in, wg, wu, wd, wr, x_ref, y_ref, m_ref, dg_ref, du_ref):
+def expert_block(
+    expert, rows_in, cots_in, wg, wu, wd, wr, x_ref, y_ref, m_ref, dg_ref, du_ref,
+    most=256, before=None, behind=None,
+):
     row_count, hidden = (rows_in[0].shape[0], wg.shape[-1])
     for seq, (rows, cots) in enumerate(zip(rows_in, cots_in)):
         spots = slot_spots(cots[row_count:, :row_count].astype(WIDE), expert)
@@ -290,8 +293,10 @@
     gates = jnp.sum(jnp.where(chosen, expo, 0.0), axis=-1, keepdims=True) / jnp.sum(
         expo, axis=-1, keepdims=True
     )
-    step = min(256, hidden)
+    step = min(most, hidden)
     dgate = jnp.zeros((x_all.shape[0], 1), WIDE)
+    if before is not None:
+        before()
     for start in range(0, hidden, step):
         span = slice(start, start + step)
         gate_act, up_act = (dot_nn(x_all, wg[:, span]), dot_nn(x_all, wu[:, span]))
@@ -304,16 +309,19 @@
         m_ref[:, span] = (joined * gates).astype(LOW)
         dg_ref[:, span] = (grad * up_act * (sig + silu * (1.0 - sig))).astype(LOW)
         du_ref[:, span] = (grad * silu).astype(LOW)
+    if behind is not None:
+        behind()
     return dgate
 
 
-def expert_kernel(row_spans, cot_spans, batch, trades, ex_ref, wg, wu, wd, wr, *refs):
+def expert_kernel(row_spans, cot_spans, batch, trades, ex_ref, wg_in, wu_in, wd_in, wr, *refs):
     first, second = (len(row_spans), len(row_spans) + len(cot_spans))
     rows_in, cots_in = (refs[:first], refs[first:second])
     third, number = (second + len(trades.trades), len(trades.trades))
     x_ref, y_ref, m_ref, dg_ref, du_ref, dgate_ref = refs[third : third + 6]
-    rows_buf, cots_buf, sems = refs[third + 6 + number : third + 9 + number]
-    trades.bind(refs[second:third], refs[third + 6 : third + 6 + number], refs[third + 9 + number :])
+    scratch = refs[third + 6 + number :]
+    rows_buf, cots_buf, sems, wg, wu, wd, weight_sems = scratch[:7]
+    trades.bind(refs[second:third], refs[third + 6 : third + 6 + number], scratch[7:])
     steps, units = (sum(count for _, count in row_spans) // batch, batch // UNIT)
     turn = pl.program_id(0) * steps + pl.program_id(1)
     slot = lax.rem(turn, 2)
@@ -341,9 +349,33 @@
 
                     begin += size
 
+    own = wg_in.shape[0]
+    lane, at_step = (pl.program_id(0), pl.program_id(1))
+
+    def weight_copies(expert):
+        pairs = ((wg_in, wg), (wu_in, wu), (wd_in, wd))
+        return [
+            pltpu.make_async_copy(source.at[expert], target, weight_sems.at[i])
+            for i, (source, target) in enumerate(pairs)
+        ]
+
+    def before():
+        @pl.when(at_step == 0)
+        def _():
+            for item in weight_copies(0):
+                item.wait()
+
+    def behind():
+        @pl.when((at_step == steps - 1) & (lane < own - 1))
+        def _():
+            for item in weight_copies(lane + 1):
+                item.start()
+
     @pl.when(turn == 0)
     def _():
         fetch(turn, slot)
+        for item in weight_copies(0):
+            item.start()
         if number:
             trades.start()
 
@@ -358,8 +390,9 @@
         ex_ref[pl.program_id(0)],
         [rows_buf.at[slot, seq] for seq in range(batch)],
         [cots_buf.at[slot, seq] for seq in range(batch)],
-        wg.at[0], wu.at[0], wd.at[0], wr,
+        wg, wu, wd, wr,
         x_ref.at[0], y_ref.at[0], m_ref.at[0], dg_ref.at[0], du_ref.at[0],
+        256, before, behind,
     )
     dgate_ref[0] = jnp.broadcast_to(dgate, dgate_ref.shape[1:])
     if number:
@@ -384,11 +417,6 @@
     def act_spec(cols):
         return pl.BlockSpec((1, out_rows, cols), lambda e, i: (e, i, 0))
 
-    def weight_spec(array):
-        return pl.BlockSpec(
-            (1,) + array.shape[1:], lambda e, i: (e, 0, 0), pipeline_mode=pl.Buffered(1)
-        )
-
     any_spec = pl.BlockSpec(memory_space=pl.ANY)
     columns = (width, width, hidden, hidden, hidden, 128)
     return pl.pallas_call(
@@ -396,9 +424,9 @@
         grid=(own, count // batch),
         in_specs=[
             pl.BlockSpec(memory_space=pltpu.SMEM),
-            weight_spec(wg),
-            weight_spec(wu),
-            weight_spec(wd),
+            any_spec,
+            any_spec,
+            any_spec,
             pl.BlockSpec(wr.shape, lambda e, i: (0, 0)),
         ]
         + [any_spec] * (len(rows) + len(cots))
@@ -409,6 +437,10 @@
             pltpu.VMEM((2, batch) + rows[0].shape[1:], LOW),
             pltpu.VMEM((2, batch) + cots[0].shape[1:], LOW),
             pltpu.SemaphoreType.DMA((2, 2, batch // UNIT)),
+            pltpu.VMEM(wg.shape[1:], LOW),
+            pltpu.VMEM(wu.shape[1:], LOW),
+            pltpu.VMEM(wd.shape[1:], LOW),
+            pltpu.SemaphoreType.DMA((3,)),
         ]
         + trades.scratch,
         compiler_params=pltpu.CompilerParams(
@@ -507,7 +539,8 @@
     own, _, left_cols = lefts[0].shape
     right_cols = rights[0][0].shape[-1]
     sets, outs = (len(lefts), len(rights))
-    tile = min(512, left_cols)
+    deep = sum(array.shape[1] for array in lefts)
+    tile = min(256 if starts is not None and deep * outs > 4096 else 512, left_cols)
     trades = Trades(trades)
     number, begun = (len(trades.trades), 0 if starts is None else outs)
     first = sets * (1 + outs)
@@ -1188,7 +1221,7 @@
         in_sums, early = after((in_sums, early))
         early_flipped = [flip_shard(values, 1) for values in early]
         down_sums = down_grads(acts)
-        down_sums, late, early_flipped = after((down_sums, late, early_flipped))
+        down_sums, early_flipped = after((down_sums, early_flipped))
         grad_moe_in, in_sums, down_sums = after((grad_moe_in, in_sums, down_sums))
 
     grad_out = cot_low.astype(WIDE)
@@ -1203,11 +1236,10 @@
         late, in_sums, down_sums, branch_low = after((late, in_sums, down_sums, branch_low))
         diagonal = [flip_replica(early[0], 2), flip_replica(late[1], 1)]
         late_flipped = [flip_shard(values, 1) for values in late]
-        branch_low, late_flipped = after((branch_low, late_flipped))
-        rows = whole(early[0], late[0], early[1], late[1])
-        for pair in zip(early_flipped, late_flipped):
-            rows = rows + whole(*pair)
-        acts = [expert_acts(ids, rows, whole(*far_cots[:2], *far_cots[3:5]), *experts)]
+        rows = whole(early[0], late[0], early[1], late[1], *early_flipped)
+        from_pairs = [(array, (0, 2)) for array in far_cots[3:5]]
+        acts = [expert_acts(ids, rows, whole(*far_cots[:2]) + from_pairs, *experts)]
+        acts, late_flipped = after((acts, late_flipped))
         upper, acts, diagonal = after((upper, acts, diagonal))
         diagonal_flipped = [flip_shard(values, 1) for values in diagonal]
     mix_part, upper = after((mix_part, upper))
@@ -1229,22 +1261,32 @@
         part, gw_low, diagonal_flipped = after((part, gw_low, diagonal_flipped))
         pieces = gw_low.reshape((replicas, -1) + gw_low.shape[1:])
         *act, traded, smalls = expert_acts(
-            ids, whole(*diagonal, *diagonal_flipped), whole(far_cots[2], far_cots[5]), *experts,
-            trades=((pieces, "rep", replicas, True), (small, "rep", replicas, False)), collective=1,
+            ids, whole(*late_flipped, *diagonal, *diagonal_flipped),
+            [(array, (2, 2)) for array in far_cots[3:5]] + whole(far_cots[2], far_cots[5]), *experts,
+            trades=((pieces, "rep", replicas, True), (small, "shard", groups, False)), collective=1,
         )
         act, traded, smalls, part, mixture = after((act, traded, smalls, part, mixture))
+        acts.append(act)
         grad_normed = scatter_sum(part)
         low = jnp.sum(traded.astype(WIDE), axis=0).astype(LOW)
         small = jnp.sum(smalls, axis=0)
-        *in_sums, found, smalls = in_grads(
-            acts, in_sums,
-            trades=((low, "rep", replicas, False), (small, "shard", groups, False)), collective=2,
-        )
-        in_sums, found, smalls, act = after((in_sums, found, smalls, act))
-        gw_sum = found.reshape(gw_low.shape)
-        small = jnp.sum(smalls, axis=0)
-        grad_gate_w, grad_up_w = in_grads([act], in_sums, in_place=False)
-        (grad_down,) = down_grads(acts + [act], down_sums)
+        found = [low] + [flip_replica(low, bits) for bits in range(1, replicas)]
+        other = flip_replica(small, 1)
+        grad_gate_w, grad_up_w = in_grads(acts, in_sums)
+        grad_gate_w, grad_up_w, found, other, acts = after(
+            (grad_gate_w, grad_up_w, found, other, acts)
+        )
+        small = small + other
+        other = flip_replica(small, 2)
+        gw_sum = jnp.zeros((replicas,) + low.shape, LOW)
+        for bits, piece in enumerate(found):
+            gw_sum = lax.dynamic_update_index_in_dim(
+                gw_sum, piece, lax.axis_index("rep") ^ bits, axis=0
+            )
+        gw_sum = gw_sum.reshape(gw_low.shape)
+        (grad_down,) = down_grads(acts, down_sums)
+        grad_down, other = after((grad_down, other))
+        small = small + other
     else:
         grad_normed = scatter_sum(part)
         over_reps = lax.psum(

time: 856 us -> 916 us (1.070)
  local copies, waits for them, and re-layouts: 12.1 us -> 81.3 us
  Pallas kernels: 744 us -> 710 us
  waiting for transfers between devices: 23.9 us -> 55.9 us
    dynamic_update_slice x0 -> x5, local copies, waits for them, and re-layouts: none -> 51 us  [local(): lax.dynamic_update_index_in_dim(gw_sum, piece, lax.axis_index('rep') ^ bi...]
    ppermute x6 -> x11, waiting for transfers between devices: 19.8 us -> 43.8 us  [flip_replica(): return lax.ppermute(values, 'rep', [(i, i ^ bits) for i in range(replicas)])]
    pallas_call x5 -> x4, Pallas kernels: 186 us -> 165 us  [weight_grad(): pl.pallas_call(kernel, grid=(own, left_cols // tile), in_specs=[pl.BlockS...]
    pallas_call x2, Pallas kernels: 164 us -> 151 us  [expert_acts(): pl.pallas_call(functools.partial(expert_kernel, row_spans, cot_spans, bat...]
    reduce_scatter x3, waiting for transfers between devices: 0.04 us -> 12 us  [scatter_sum(): lax.psum_scatter(parts.reshape(-1, width), 'shard', scatter_dimension=0,...]
    unnamed x22 -> x39, local copies, waits for them, and re-layouts: 4.86 us -> 14.5 us
  transfers between devices with their start and end apart: 16 -> 21, of which waited for: 4 -> 3; matrix products, arithmetic and copies ran while one was open for 3% -> 10% of each run, Pallas kernels for 50% -> 42%
where the time goes in v6:
time: 916 us; the launch traced here: 908 us
  Pallas kernels  710 us (78%)
  local copies, waits for them, and re-layouts  81.3 us (9%)
  waiting for transfers between devices  55.9 us (6%)
  other arithmetic  29.7 us (3%)
  between operations  15.1 us (2%)
  starting transfers between devices  14.9 us (2%)
    pallas_call x1, Pallas kernels, moe(): pl.pallas_call(functools.partial(moe_kernel, replicas, groups), in_specs=...  184 us
    pallas_call x4, Pallas kernels, weight_grad(): pl.pallas_call(kernel, grid=(own, left_cols // tile), in_specs=[pl.BlockS...  165 us
    pallas_call x2, Pallas kernels, expert_acts(): pl.pallas_call(functools.partial(expert_kernel, row_spans, cot_spans, bat...  151 us
    pallas_call x1, Pallas kernels, front(): pl.pallas_call(functools.partial(front_kernel, replicas, groups), in_spec...  143 us
    dynamic_update_slice x5, local copies, waits for them, and re-layouts, local(): lax.dynamic_update_index_in_dim(gw_sum, piece, lax.axis_index('rep') ^ bi...  51 us
    pallas_call x1, Pallas kernels, attend_backward(): pl.pallas_call(attend_back_kernel, grid=(count,), in_specs=[first_spec(ar...  46.3 us
    ppermute x11, waiting for transfers between devices, flip_replica(): return lax.ppermute(values, 'rep', [(i, i ^ bits) for i in range(replicas)])  43.8 us
    pallas_call x1, Pallas kernels, spread_call(): pl.pallas_call(kernel, grid=(count // batch,), in_specs=[pl.BlockSpec(mem...  20.1 us
  transfers between devices with their start and end apart: 21, of which 3 were waited for; matrix products, arithmetic and copies ran while one was open for 10% of the time, Pallas kernels for 42%

profile of v6, /device:TPU:0, one launch (start us, length us, event | category | flops | bytes accessed | tf_op | source)
XLA Modules:
  0.0 907.7 jit_solution(17179287976923621550)
XLA Ops:
  8.0 0.5 iota_add_fusion.ex_ref
  8.5 1.6 fusion.9
  10.1 0.7 fusion.15
  10.9 0.8 fusion.12
  11.6 0.5 fusion.16
  12.2 1.8 copy.56.wr
  14.0 0.3 fusion.4
  14.5 0.8 pad_maximum_fusion
  15.3 1.6 fusion.11
  16.9 143.3 %front.1 = (bf16[8,272,2048]{2,1,0:T(8,128)(2,1)}, f32[8,256,256]{2,1,0:T(8,128)}, f32[8,256,256]{2,1,0:T(8,128)}, bf16[8,256,256]{2,1,0:T(8,128)(2,1)}, bf16[8,...) custom-call(bf16[272,2048]{1,0:T(8,128)(2,1)} %get-tuple-element.293.packet, ...), custom_call_target="tpu_custom_call" | custom-call | flops 1048576 | bytes 65536 | tf_op jit(solution)/shard_map/front/pallas_call | solution.py:897
  160.2 184.1 %moe.1 = (bf16[8,256,2048]{2,1,0:T(8,128)(2,1)}, bf16[8,272,2048]{2,1,0:T(8,128)(2,1)}, bf16[4,272,2048]{2,1,0:T(8,128)(2,1)}, bf16[4,272,2048]{2,1,0:T(8,128)(2...) custom-call(s32[2]{0:T(128)} %iota_add_fusion.ex_ref, ...), custom_call_target="tpu_custom_call" | custom-call | flops 1048576 | bytes 65536 | tf_op jit(solution)/shard_map/moe/pallas_call | solution.py:1091
  344.4 4.1 dynamic-slice_bitcast_fusion
  348.5 1.5 collective-permute-start.1
  350.1 0.5 collective-permute-start
  350.6 20.1 %expert_mix.1 = bf16[8,256,2048]{2,1,0:T(8,128)(2,1)} custom-call(s32[2]{0:T(128)} %iota_add_fusion.ex_ref, bf16[8,272,2048]{2,1,0:T(8,128)(2,1)} %get-tuple-element.133.cot_ref, bf16[2,1152,1024]{2,1,0:T(8,128)(2,1)} %get-tuple-element.143.m_ref.refs_0_, bf16[2,1024,2048]{2,1,0:T(8,128)(2,1)} %wd_in.5), custom_call_target="tpu_custom_call" | custom-call | flops 1048576 | bytes 65536 | tf_op jit(solution)/shard_map/expert_mix/pallas_call | solution.py:522
  370.6 29.6 %weight_grad.4 = (f32[2,2048,1024]{2,1,0:T(8,128)}, f32[2,2048,1024]{2,1,0:T(8,128)}) custom-call(bf16[2,1152,2048]{2,1,0:T(8,128)(2,1)} %get-tuple-element.135.refs_0_, bf16[2,1152,1024]{2,1,0:T(8,128)(2,1)} %get-tuple-element.136.refs_1_, bf16[2,1152,1024]{2,1,0:T(8,128)(2,1)} %get-tuple-element.137.refs_2_), custom_call_target="tpu_custom_call" | custom-call | flops 1048576 | bytes 65536 | tf_op jit(solution)/shard_map/weight_grad/pallas_call | solution.py:573
  400.3 0.5 collective-permute-start.2
  400.8 18.6 %weight_grad.5.refs_4_ = f32[2,1024,2048]{2,1,0:T(8,128)} custom-call(bf16[2,1152,1024]{2,1,0:T(8,128)(2,1)} %get-tuple-element.143.m_ref.refs_0_, bf16[2,1152,2048]{2,1,0:T(8,128)(2,1)} %get-tuple-element.144.refs_1_), custom_call_target="tpu_custom_call" | custom-call | flops 1048576 | bytes 65536 | tf_op jit(solution)/shard_map/weight_grad/pallas_call | solution.py:573
  419.4 11.9 %reduce-scatter.4.cloned.1.call-done = bf16[256,2048]{1,0:T(8,128)(2,1)} async-done(((bf16[2048,2048]{1,0:T(8,128)(2,1)}), bf16[256,2048]{1,0:T(8,128)(2,1)}) %reduce-scatter.4.cloned.1.call-update) | async-done | bytes 1048592 | tf_op jit(solution)/shard_map/reduce_scatter | solution.py:1150
  431.4 1.5 convert_element_type.52
  433.1 0.7 multiply_reduce_fusion
  433.8 0.4 copy-done.1
  434.2 1.7 fusion.18
  436.0 1.6 collective-permute-start.5
  437.5 1.4 collective-permute-start.4
  439.0 42.6 %collective-permute-done.5.refs_3_ = bf16[2,256,2048]{2,1,0:T(8,128)(2,1)} collective-permute-done((bf16[2,256,2048]{2,1,0:T(8,128)(2,1)}, bf16[2,256,2048]{2,1,0:T(8,128)(2,1)}, u32[]{:S(2)}, u32[]{:S(2)}) %collective-permute-start.5) | collective-permute-done | bytes 2097184 | tf_op jit(solution)/shard_map/ppermute | solution.py:1144
  481.6 1.2 collective-permute-done.4.refs_1_
  482.8 0.5 collective-permute-start.7
  483.3 0.6 collective-permute-start.8
  483.8 1.5 collective-permute-start.9
  485.3 73.9 %expert_acts.2 = (bf16[2,1728,2048]{2,1,0:T(8,128)(2,1)}, bf16[2,1728,2048]{2,1,0:T(8,128)(2,1)}, bf16[2,1728,1024]{2,1,0:T(8,128)(2,1)}, bf16[2,1728,1024]{2,1,...) custom-call(s32[2]{0:T(128)} %iota_add_fusion.ex_ref, bf16[2,2048,1024]{2,1,0:T(8,128)(2,1)} %wg_in.5, ...), custom_call_target="tpu_custom_call" | custom-call | flops 1048576 | bytes 65536 | tf_op jit(solution)/shard_map/expert_acts/pallas_call | solution.py:422
  559.5 0.5 collective-permute-start.11
  560.0 46.3 %attend_backward.1 = (bf16[8,256,2048]{2,1,0:T(8,128)(2,1)}, bf16[2048,1024]{1,0:T(8,128)(2,1)}, f32[1,128]{1,0:T(1,128)}, f32[1,128]{1,0:T(1,128)}, f32[1,2048]{1,0:T(1,128)}) custom-call(bf16[8,256,2048]{2,1,0:T(8,128)(2,1)} %bitcast.49, bf16[8,272,2048]{2,1,0:T(8,128)(2,1)} %get-tuple-element.179.pk_ref, f32[8,256,256]{2,1,0:T(8,128)} %get-tuple-element.180.qr_ref, ...), custom_call_target="tpu_custom_call" | custom-call | flops 1048576 | bytes 65536 | tf_op jit(solution)/shard_map/attend_backward/pallas_call | solution.py:200
  606.3 0.7 div.18
  607.0 0.7 fusion.17
  607.7 1.3 concatenate.27.refs_11_
  609.1 76.9 %expert_acts.3 = (bf16[2,1728,2048]{2,1,0:T(8,128)(2,1)}, bf16[2,1728,2048]{2,1,0:T(8,128)(2,1)}, bf16[2,1728,1024]{2,1,0:T(8,128)(2,1)}, bf16[2,1728,1024]{2,1,...) custom-call(s32[2]{0:T(128)} %iota_add_fusion.ex_ref, ...), custom_call_target="tpu_custom_call" | custom-call | flops 1048576 | bytes 65536 | tf_op jit(solution)/shard_map/expert_acts/pallas_call | solution.py:422
  686.0 2.9 convert_element_type.55
  688.9 3.3 reduce_sum.72
  692.2 1.6 collective-permute-start.14
  693.9 0.6 collective-permute-start.13
  694.4 1.3 collective-permute-start.12
  695.8 1.5 reduce_sum.71
  697.3 0.9 collective-permute-start.15
  698.2 75.4 %weight_grad.6 = (f32[2,2048,1024]{2,1,0:T(8,128)}, f32[2,2048,1024]{2,1,0:T(8,128)}) custom-call(bf16[2,1728,2048]{2,1,0:T(8,128)(2,1)} %get-tuple-element.207.refs_0_, bf16[2,1728,2048]{2,1,0:T(8,128)(2,1)} %get-tuple-element.208.refs_1_, bf16[2,1728,1024]{2,1,0:T(8,128)(2,1)} %get-tuple-element.209.refs_2_, ...), custom_call_target="tpu_custom_call", output_to_operand_aliasing={{0}: (6, {}), {1}: (7, {})} | custom-call | flops 1048576 | bytes 65536 | tf_op jit(solution)/shard_map/weight_grad/pallas_call | solution.py:573
  773.7 2.6 broadcast_in_dim.62
  776.3 1.1 bitcast_dynamic-update-slice_fusion.2
  777.3 2.3 bitcast_dynamic-update-slice_fusion.1
  779.7 2.3 bitcast_dynamic-update-slice_fusion
  781.9 7.9 copy.61
  789.9 1.5 collective-permute-start.16
  791.4 6.0 copy.62
  797.4 37.4 %dynamic_update_slice.16 = bf16[4,512,1024]{1,0,2:T(4,128)(2,1)} dynamic-update-slice(bf16[4,512,1024]{1,0,2:T(4,128)(2,1)} %copy.61, bf16[1,512,1024]{1,0,2:T(2,128)(2,1)} %copy.62, s32[]{:T(128)S(6)} %select_n.39, s32[]{:T(128)} %constant.53.clone.1, s32[]{:T(128)} %constant.53.clone.1) | dynamic-update-slice | bytes 2097156 | tf_op jit(solution)/shard_map/jit(dynamic_update_index_in_dim)/dynamic_update_slice | solution.py:1283
  834.8 3.6 copy.68
  838.4 3.8 convert_bitcast_fusion
  842.2 2.9 copy.65
  845.1 2.9 copy.64
  848.0 2.9 copy.63
  850.9 41.7 %weight_grad.7 = f32[2,1024,2048]{2,1,0:T(8,128)} custom-call(bf16[2,1728,1024]{2,1,0:T(8,128)(2,1)} %get-tuple-element.223.refs_0_, bf16[2,1728,1024]{2,1,0:T(8,128)(2,1)} %get-tuple-element.224.refs_1_, bf16[2,1728,2048]{2,1,0:T(8,128)(2,1)} %get-tuple-element.225.refs_2_, ...), custom_call_target="tpu_custom_call", output_to_operand_aliasing={{}: (4, {})} | custom-call | flops 1048576 | bytes 65536 | tf_op jit(solution)/shard_map/weight_grad/pallas_call | solution.py:573
  892.6 0.5 slice_bitcast_fusion.1
  893.1 0.6 fusion.19
  893.7 0.7 slice_bitcast_fusion
  894.4 1.9 fusion.5
  896.4 4.5 fusion.8
  (73 shorter events, 1.0 us)
Async XLA Ops:
  7.2 6.8 copy-start.3
  7.2 6.8 copy-start.9
  7.2 424.2 %reduce-scatter.4.cloned.1.call-start = ((), (), s32[]{:S(2)}) async-start(), calls=%async_computation.3 | async-start | bytes 9437184 | tf_op jit(solution)/shard_map/reduce_scatter | solution.py:1150
  8.5 5.8 copy-start.15
  8.5 5.8 copy-start.5
  10.1 4.4 copy-start.11
  14.0 1.3 copy-start.14
  344.3 215.0 %all-gather.3.cloned.1.call-start = ((), (), s32[]{:S(2)}) async-start(), calls=%async_computation.6 | async-start | bytes 9437184 | tf_op jit(solution)/shard_map/all_gather | solution.py:1234
  348.5 51.7 %collective-permute-start.1 = (bf16[2,256,2048]{2,1,0:T(8,128)(2,1)S(1)}, bf16[2,256,2048]{2,1,0:T(8,128)(2,1)}, u32[]{:S(2)}, u32[]{:S(2)}) collective-permute-start(bf16[2,256,2048]{2,1,0:T(8,128)(2,1)S(1)} %get-tuple-element.281), channel_id=1, source_target_pairs={{0,16},{8,24},{16,0},{24,8},{1,17},{9,25},{17,1},{25,9},{2,18},{10... | collective-permute-start | bytes 6291464 | tf_op jit(solution)/shard_map/ppermute | solution.py:1144
  350.1 50.1 %collective-permute-start = (bf16[2,256,2048]{2,1,0:T(8,128)(2,1)S(1)}, bf16[2,256,2048]{2,1,0:T(8,128)(2,1)}, u32[]{:S(2)}, u32[]{:S(2)}) collective-permute-start(bf16[2,256,2048]{2,1,0:T(8,128)(2,1)S(1)} %get-tuple-element.281), channel_id=1, source_target_pairs={{0,8},{8,0},{16,24},{24,16},{1,9},{9,1},{17,25},{25,17},{2,10},{10... | collective-permute-start | bytes 6291464 | tf_op jit(solution)/shard_map/ppermute | solution.py:1144
  400.2 19.2 %collective-permute-start.3 = (bf16[2,256,2048]{2,1,0:T(8,128)(2,1)}, bf16[2,256,2048]{2,1,0:T(8,128)(2,1)}, u32[]{:S(2)}, u32[]{:S(2)}) collective-permute-start(bf16[2,256,2048]{2,1,0:T(8,128)(2,1)} %collective-permute-done.1.refs_2_), channel_id=1, source_target_pairs={{0,1},{1,0},{2,3},{3,2},{4,5},{5,4},{6,7},{7,6},{8,9},{9,8},{10,11... | collective-permute-start | bytes 6291464 | tf_op jit(solution)/shard_map/ppermute | solution.py:1147
  400.3 19.1 %collective-permute-start.2 = (bf16[2,256,2048]{2,1,0:T(8,128)(2,1)}, bf16[2,256,2048]{2,1,0:T(8,128)(2,1)}, u32[]{:S(2)}, u32[]{:S(2)}) collective-permute-start(bf16[2,256,2048]{2,1,0:T(8,128)(2,1)} %collective-permute-done.refs_0_), channel_id=1, source_target_pairs={{0,1},{1,0},{2,3},{3,2},{4,5},{5,4},{6,7},{7,6},{8,9},{9,8},{10,11... | collective-permute-start | bytes 6291464 | tf_op jit(solution)/shard_map/ppermute | solution.py:1147
  419.4 13.4 %copy-start = (f32[256,2048]{1,0:T(8,128)S(1)}, f32[256,2048]{1,0:T(8,128)}, u32[]{:S(2)}) copy-start(f32[256,2048]{1,0:T(8,128)} %get-tuple-element.149) | copy-start | bytes 6291460
  419.4 13.7 %copy-start.8 = (f32[2048]{0:T(1024)S(1)}, f32[2048]{0:T(1024)}, u32[]{:S(2)}) copy-start(f32[2048]{0:T(1024)} %param.26) | copy-start | bytes 24580
  432.8 1.3 copy-start.1
  433.1 1.1 copy-start.12
  433.1 1.1 copy-start.16
  434.2 1.7 copy-start.13
  435.9 250.1 %reduce-scatter.6.cloned.1.call-start = ((), (), s32[]{:S(2)}) async-start(), calls=%async_computation.4 | async-start | bytes 9437184 | tf_op jit(solution)/shard_map/reduce_scatter | solution.py:1150
  436.0 45.6 %collective-permute-start.5 = (bf16[2,256,2048]{2,1,0:T(8,128)(2,1)}, bf16[2,256,2048]{2,1,0:T(8,128)(2,1)}, u32[]{:S(2)}, u32[]{:S(2)}) collective-permute-start(bf16[2,256,2048]{2,1,0:T(8,128)(2,1)} %get-tuple-element.280), channel_id=1, source_target_pairs={{0,16},{8,24},{16,0},{24,8},{1,17},{9,25},{17,1},{25,9},{2,18},{10... | collective-permute-start | bytes 6291464 | tf_op jit(solution)/shard_map/ppermute | solution.py:1144
  437.5 45.2 %collective-permute-start.4 = (bf16[2,256,2048]{2,1,0:T(8,128)(2,1)}, bf16[2,256,2048]{2,1,0:T(8,128)(2,1)}, u32[]{:S(2)}, u32[]{:S(2)}) collective-permute-start(bf16[2,256,2048]{2,1,0:T(8,128)(2,1)} %get-tuple-element.280), channel_id=1, source_target_pairs={{0,8},{8,0},{16,24},{24,16},{1,9},{9,1},{17,25},{25,17},{2,10},{10... | collective-permute-start | bytes 6291464 | tf_op jit(solution)/shard_map/ppermute | solution.py:1144
  482.8 76.5 %collective-permute-start.6 = (bf16[2,256,2048]{2,1,0:T(8,128)(2,1)}, bf16[2,256,2048]{2,1,0:T(8,128)(2,1)}, u32[]{:S(2)}, u32[]{:S(2)}) collective-permute-start(bf16[2,256,2048]{2,1,0:T(8,128)(2,1)} %collective-permute-done.4.refs_1_), channel_id=1, source_target_pairs={{0,1},{1,0},{2,3},{3,2},{4,5},{5,4},{6,7},{7,6},{8,9},{9,8},{10,11... | collective-permute-start | bytes 6291464 | tf_op jit(solution)/shard_map/ppermute | solution.py:1147
  482.8 76.5 %collective-permute-start.7 = (bf16[2,256,2048]{2,1,0:T(8,128)(2,1)}, bf16[2,256,2048]{2,1,0:T(8,128)(2,1)}, u32[]{:S(2)}, u32[]{:S(2)}) collective-permute-start(bf16[2,256,2048]{2,1,0:T(8,128)(2,1)} %collective-permute-done.5.refs_3_), channel_id=1, source_target_pairs={{0,1},{1,0},{2,3},{3,2},{4,5},{5,4},{6,7},{7,6},{8,9},{9,8},{10,11... | collective-permute-start | bytes 6291464 | tf_op jit(solution)/shard_map/ppermute | solution.py:1147
  483.3 76.0 %collective-permute-start.8 = (bf16[2,256,2048]{2,1,0:T(8,128)(2,1)}, bf16[2,256,2048]{2,1,0:T(8,128)(2,1)}, u32[]{:S(2)}, u32[]{:S(2)}) collective-permute-start(bf16[2,256,2048]{2,1,0:T(8,128)(2,1)} %collective-permute-done.refs_0_), channel_id=1, source_target_pairs={{0,16},{8,24},{16,0},{24,8},{1,17},{9,25},{17,1},{25,9},{2,18},{10... | collective-permute-start | bytes 6291464 | tf_op jit(solution)/shard_map/ppermute | solution.py:1144
  483.8 75.4 %collective-permute-start.9 = (bf16[2,256,2048]{2,1,0:T(8,128)(2,1)}, bf16[2,256,2048]{2,1,0:T(8,128)(2,1)}, u32[]{:S(2)}, u32[]{:S(2)}) collective-permute-start(bf16[2,256,2048]{2,1,0:T(8,128)(2,1)} %collective-permute-done.5.refs_3_), channel_id=1, source_target_pairs={{0,8},{8,0},{16,24},{24,16},{1,9},{9,1},{17,25},{25,17},{2,10},{10... | collective-permute-start | bytes 6291464 | tf_op jit(solution)/shard_map/ppermute | solution.py:1144
  559.3 335.1 %reduce-scatter.8.cloned.1.call-start = ((), (), s32[]{:S(2)}) async-start(), calls=%async_computation.5 | async-start | bytes 9437184 | tf_op jit(solution)/shard_map/reduce_scatter | solution.py:1150
  559.4 49.7 %collective-permute-start.10 = (bf16[2,256,2048]{2,1,0:T(8,128)(2,1)}, bf16[2,256,2048]{2,1,0:T(8,128)(2,1)}, u32[]{:S(2)}, u32[]{:S(2)}) collective-permute-start(bf16[2,256,2048]{2,1,0:T(8,128)(2,1)} %collective-permute-done.8.refs_2_), channel_id=1, source_target_pairs={{0,1},{1,0},{2,3},{3,2},{4,5},{5,4},{6,7},{7,6},{8,9},{9,8},{10,11... | collective-permute-start | bytes 6291464 | tf_op jit(solution)/shard_map/ppermute | solution.py:1147
  559.5 49.6 %collective-permute-start.11 = (bf16[2,256,2048]{2,1,0:T(8,128)(2,1)}, bf16[2,256,2048]{2,1,0:T(8,128)(2,1)}, u32[]{:S(2)}, u32[]{:S(2)}) collective-permute-start(bf16[2,256,2048]{2,1,0:T(8,128)(2,1)} %collective-permute-done.9.refs_3_), channel_id=1, source_target_pairs={{0,1},{1,0},{2,3},{3,2},{4,5},{5,4},{6,7},{7,6},{8,9},{9,8},{10,11... | collective-permute-start | bytes 6291464 | tf_op jit(solution)/shard_map/ppermute | solution.py:1147
  560.0 47.7 %copy-start.10 = (f32[16,2048]{1,0:T(8,128)S(1)}, f32[16,2048]{1,0:T(8,128)}, u32[]{:S(2)}) copy-start(f32[16,2048]{1,0:T(8,128)} %get-tuple-element.191) | copy-start | bytes 393220
  692.2 81.5 %collective-permute-start.14 = (bf16[512,1024]{1,0:T(8,128)(2,1)S(1)}, bf16[512,1024]{1,0:T(8,128)(2,1)}, u32[]{:S(2)}, u32[]{:S(2)}) collective-permute-start(bf16[512,1024]{1,0:T(8,128)(2,1)S(1)} %reduce_sum.72), channel_id=1, source_target_pairs={{0,24},{8,16},{16,8},{24,0},{1,25},{9,17},{17,9},{25,1},{2,26},{10... | collective-permute-start | bytes 3145736 | tf_op jit(solution)/shard_map/ppermute | solution.py:1144
  693.9 79.8 %collective-permute-start.13 = (bf16[512,1024]{1,0:T(8,128)(2,1)S(1)}, bf16[512,1024]{1,0:T(8,128)(2,1)}, u32[]{:S(2)}, u32[]{:S(2)}) collective-permute-start(bf16[512,1024]{1,0:T(8,128)(2,1)S(1)} %reduce_sum.72), channel_id=1, source_target_pairs={{0,16},{8,24},{16,0},{24,8},{1,17},{9,25},{17,1},{25,9},{2,18},{10... | collective-permute-start | bytes 3145736 | tf_op jit(solution)/shard_map/ppermute | solution.py:1144
  694.4 79.3 %collective-permute-start.12 = (bf16[512,1024]{1,0:T(8,128)(2,1)S(1)}, bf16[512,1024]{1,0:T(8,128)(2,1)}, u32[]{:S(2)}, u32[]{:S(2)}) collective-permute-start(bf16[512,1024]{1,0:T(8,128)(2,1)S(1)} %reduce_sum.72), channel_id=1, source_target_pairs={{0,8},{8,0},{16,24},{24,16},{1,9},{9,1},{17,25},{25,17},{2,10},{10... | collective-permute-start | bytes 3145736 | tf_op jit(solution)/shard_map/ppermute | solution.py:1144
  697.3 76.4 %collective-permute-start.15 = (f32[24,2048]{1,0:T(8,128)S(1)}, f32[24,2048]{1,0:T(8,128)S(1)}, u32[]{:S(2)}, u32[]{:S(2)}) collective-permute-start(f32[24,2048]{1,0:T(8,128)S(1)} %reduce_sum.71), channel_id=1, source_target_pairs={{0,8},{8,0},{16,24},{24,16},{1,9},{9,1},{17,25},{25,17},{2,10},{10... | collective-permute-start | bytes 589832 | tf_op jit(solution)/shard_map/ppermute | solution.py:1144
  773.7 2.6 copy-start.6
  781.9 7.9 copy-start.7
  789.9 102.7 %collective-permute-start.16 = (f32[24,2048]{1,0:T(8,128)S(1)}, f32[24,2048]{1,0:T(8,128)S(1)}, u32[]{:S(2)}, u32[]{:S(2)}) collective-permute-start(f32[24,2048]{1,0:T(8,128)S(1)} %add.77), channel_id=1, source_target_pairs={{0,16},{8,24},{16,0},{24,8},{1,17},{9,25},{17,1},{25,9},{2,18},{10... | collective-permute-start | bytes 589832 | tf_op jit(solution)/shard_map/ppermute | solution.py:1144
  850.9 43.5 %copy-start.4 = (bf16[256,2048]{1,0:T(8,128)(2,1)S(1)}, bf16[256,2048]{1,0:T(8,128)(2,1)}, u32[]{:S(2)}) copy-start(bf16[256,2048]{1,0:T(8,128)(2,1)} %tokens.1) | copy-start | bytes 3145732
  894.4 1.9 copy-start.2
Sparse Core Ops, SparseCore 0:
  344.5 86.8 reduce-scatter.3
  436.0 80.3 all-gather.2
  559.5 114.5 reduce-scatter.5
  689.0 89.2 reduce-scatter.7
